TPU v7x, 32 devices: a whole 2x2x4 slice. The times are simulated.
32 devices in a mesh: tilt: 2 (over y), row: 8 (over z, x), col: 2 (over core).
Axes of the slice: x: 2, y: 2, z: 4, core: 2. Of those that a mesh axis runs over, the one named last changes fastest.
Arguments:
- object_field: float32 [2, 2048, 256], P(None, ('tilt', 'row'), 'col'), parts along dimension 1, may hold values from -4.2 to 4.2
- probe: float32 [8, 2, 128, 128], P('tilt'), parts along dimension 0, may hold values from -2.1 to 2.1
- patterns: float32 [16, 2, 2, 128, 128], P(('tilt', 'row'), 'col'), parts along dimension 0, may hold values from 0.1 to 3
- offsets: int32 [16, 2, 2, 2], P(('tilt', 'row'), 'col'), parts along dimension 0, may hold values from 0 to 256
- counts: int32 [16, 2], P(('tilt', 'row'), 'col'), parts along dimension 0, may hold values from 1 to 2, as said below
Outputs:
- object_out: float32 [2, 2048, 256], P(None, ('tilt', 'row'), 'col'), parts along dimension 1
- probe_out: float32 [8, 2, 128, 128], P('tilt'), parts along dimension 0
There are 2 independent parts, one for each index of `tilt`. A program takes and returns all parts, laid end to end along the dimension named above; each array names one. Nothing has to cross between parts.
Inputs may be any that keep to these rules, and one draw needn't show every extreme that they name: Only the first counts[r, c] slots of a tile are live; some tile has all 2 live. `offsets`: A window lies inside its tile's frame of 384 pixels a side.
All inputs are finite; a program needn't handle non-finite values.
Results may differ from a plain program's by a relative error of at most 0.0003.
Values sent between devices are 32-bit elements; how exact they have to be, the bound alone decides.
No kernel may reach another device: no remote copies, remote signals or barrier semaphores. Data moves between devices by JAX's collectives and lax.ppermute only.
A program may use at most 64 MiB of HBM per device.

v0:
```python
import jax
import jax.numpy as jnp
from jax import lax
from jax.sharding import PartitionSpec as P

H = 128


object_rate = 1.0
probe_rate = 1.0
epsilon = 1e-06


def with_halo(block, sides, width):
    for axis, dim in sides:
        count = lax.axis_size(axis)
        forward = [(i, i + 1) for i in range(count - 1)]
        backward = [(target, source) for source, target in forward]
        low = lax.ppermute(
            lax.slice_in_dim(block, block.shape[dim] - width, None, axis=dim), axis, forward
        )
        high = lax.ppermute(lax.slice_in_dim(block, 0, width, axis=dim), axis, backward)
        block = jnp.concatenate([low, block, high], axis=dim)
    return block


def as_index(value):
    return jnp.asarray(value).astype(jnp.int32)


def dft_tables(length):
    counter = jnp.arange(length, dtype=jnp.int32)
    product = counter[:, None] * counter[None, :] % length
    angle = -2.0 * jnp.pi / length * product.astype(jnp.float32)
    norm = 1.0 / jnp.sqrt(jnp.float32(length))
    return (jnp.cos(angle) * norm, jnp.sin(angle) * norm)


def left_product(cos_table, sin_table, real_part, imag_part):
    hp = lax.Precision.HIGHEST
    real_out = jnp.einsum("ab,kbc->kac", cos_table, real_part, precision=hp) - jnp.einsum(
        "ab,kbc->kac", sin_table, imag_part, precision=hp
    )
    imag_out = jnp.einsum("ab,kbc->kac", cos_table, imag_part, precision=hp) + jnp.einsum(
        "ab,kbc->kac", sin_table, real_part, precision=hp
    )
    return (real_out, imag_out)


def right_product(real_part, imag_part, cos_table, sin_table):
    hp = lax.Precision.HIGHEST
    real_out = jnp.einsum("kab,bc->kac", real_part, cos_table, precision=hp) - jnp.einsum(
        "kab,bc->kac", imag_part, sin_table, precision=hp
    )
    imag_out = jnp.einsum("kab,bc->kac", real_part, sin_table, precision=hp) + jnp.einsum(
        "kab,bc->kac", imag_part, cos_table, precision=hp
    )
    return (real_out, imag_out)


def transform(real_part, imag_part, cos_table, sin_table):
    middle_re, middle_im = left_product(cos_table, sin_table, real_part, imag_part)
    return right_product(middle_re, middle_im, cos_table, sin_table)


def slot_terms(window, probe, pattern, cos_table, sin_table):
    window_re, window_im = (window[0], window[1])
    probe_re, probe_im = (probe[:, 0], probe[:, 1])
    exit_re = probe_re * window_re - probe_im * window_im
    exit_im = probe_re * window_im + probe_im * window_re
    far_re, far_im = transform(exit_re, exit_im, cos_table, sin_table)
    intensity = jnp.sum(far_re * far_re + far_im * far_im, axis=0)
    misfit = intensity - pattern
    back_re, back_im = transform(misfit * far_re, misfit * far_im, cos_table, -sin_table)
    grad_re = jnp.sum(probe_re * back_re + probe_im * back_im, axis=0)
    grad_im = jnp.sum(probe_re * back_im - probe_im * back_re, axis=0)
    term_re = window_re * back_re + window_im * back_im
    term_im = window_re * back_im - window_im * back_re
    return (jnp.stack([grad_re, grad_im]), jnp.stack([term_re, term_im], axis=1))


def body(object_field, probe, patterns, offsets, counts):
    width = probe.shape[-1]
    block = object_field.shape[1]
    slot_total = patterns.shape[2]
    cos_table, sin_table = dft_tables(width)
    tile_total = lax.axis_size("row") * lax.axis_size("col")
    live_count = counts[0, 0]
    frame = with_halo(object_field, (("row", 1), ("col", 2)), H)

    def slot_step(slot_index, inner):
        local_grad, probe_acc = inner
        slot_index = as_index(slot_index)
        corner_y = as_index(offsets[0, 0, slot_index, 0])
        corner_x = as_index(offsets[0, 0, slot_index, 1])
        window = lax.dynamic_slice(frame, (as_index(0), corner_y, corner_x), (2, width, width))
        window_grad, probe_term = slot_terms(
            window, probe, patterns[0, 0, slot_index], cos_table, sin_table
        )
        live = (slot_index < live_count).astype(jnp.float32)
        region = (
            lax.dynamic_slice(local_grad, (as_index(0), corner_y, corner_x), (2, width, width))
            + live * window_grad
        )
        local_grad = lax.dynamic_update_slice(local_grad, region, (as_index(0), corner_y, corner_x))
        return (local_grad, probe_acc + live * probe_term)

    start_carry = (jnp.zeros_like(frame), jnp.zeros_like(probe))
    gradient, probe_grad = lax.fori_loop(0, slot_total, slot_step, start_carry)
    upper_strip = gradient[:, :H, :]
    lower_strip = gradient[:, H + block :, :]
    middle = gradient[:, H : H + block, :]
    row_edges = jnp.concatenate([upper_strip, lower_strip], axis=1)
    row_grown = with_halo(row_edges, (("row", 1),), H)
    from_above = row_grown[:, :H, :]
    from_below = row_grown[:, 3 * H :, :]
    middle = middle.at[:, :H, :].add(from_above).at[:, block - H :, :].add(from_below)
    left_strip = middle[:, :, :H]
    right_strip = middle[:, :, H + block :]
    object_grad = middle[:, :, H : H + block]
    col_edges = jnp.concatenate([left_strip, right_strip], axis=2)
    col_grown = with_halo(col_edges, (("col", 2),), H)
    from_left = col_grown[:, :, :H]
    from_right = col_grown[:, :, 3 * H :]
    object_grad = object_grad.at[:, :, :H].add(from_left).at[:, :, block - H :].add(from_right)
    weight = (
        jnp.max(jnp.sum(probe[:, 0] * probe[:, 0] + probe[:, 1] * probe[:, 1], axis=0)) + epsilon
    )
    object_field = object_field - object_rate * object_grad / weight
    summed = lax.psum(probe_grad, ("row", "col"))
    probe = probe - probe_rate * summed / tile_total
    return (object_field, probe)


def solution(mesh):
    placed = (
        P(None, ("tilt", "row"), "col"),
        P("tilt", None, None, None),
        P(("tilt", "row"), "col", None, None, None),
        P(("tilt", "row"), "col", None, None),
        P(("tilt", "row"), "col"),
    )
    return jax.shard_map(
        body,
        mesh=mesh,
        in_specs=placed,
        out_specs=(P(None, ("tilt", "row"), "col"), P("tilt", None, None, None)),
        check_vma=False,
    )
```

profile of v0, /device:TPU:0, one launch (start us, length us, event | category | flops | bytes accessed | tf_op | source)
XLA Modules:
  0.0 179.7 jit_solution(4061278362378386647)
XLA Ops:
  7.2 4.9 %collective-permute-start = (f32[2,128,128]{2,1,0:T(8,128)}, f32[2,128,128]{2,1,0:T(8,128)S(1)}, u32[]{:S(2)}, u32[]{:S(2)}) collective-permute-start(f32[2,128,128]{2,1,0:T(8,128)} %param.23), channel_id=1, source_target_pairs={{0,2},{2,4},{4,6},{6,8},{8,10},{10,12},{12,14},{1,3},{3,5},{5,7},{... | collective-permute-start | bytes 393224 | tf_op jit(solution)/shard_map/ppermute | solution.py:19
  12.1 1.3 collective-permute-start.1
  13.4 1.7 collective-permute-done
  15.2 0.9 constant_dynamic-update-slice_fusion.1
  16.1 3.1 %collective-permute-done.1 = f32[2,128,128]{2,1,0:T(8,128)S(1)} collective-permute-done((f32[2,128,128]{2,1,0:T(8,128)}, f32[2,128,128]{2,1,0:T(8,128)S(1)}, u32[]{:S(2)}, u32[]{:S(2)}) %collective-permute-start.1) | collective-permute-done | bytes 131104 | tf_op jit(solution)/shard_map/ppermute | solution.py:22
  19.2 1.3 collective-permute-start.2
  20.5 1.3 collective-permute-start.3
  21.8 1.1 copy.41
  22.9 1.2 collective-permute-done.3
  24.1 1.1 pad_maximum_fusion
  25.3 0.8 copy-done.1
  26.1 42.2 %while.26 = (s32[]{:T(128)}, f32[2,384,384]{2,1,0:T(8,128)S(1)}, f32[4,2,128,128]{3,2,0,1:T(8,128)S(1)}, s32[1,1,2,2]{3,2,1,0:T(2,128)S(1)}, s32[]{:T(128)}, /*i...) while((s32[]{:T(128)}, f32[2,384,384]{2,1,0:T(8,128)S(1)}, ...), condition=%wide.region_4.5_spmd.clone.clone, body=%wide.region_0.4_spmd.clone.clone.sunk | while | flops 1617952768 | bytes 16646421 | solution.py:109
  30.7 1.1 dynamic-slice_bitcast_fusion.3
  44.8 2.5 %dynamic_update_slice.11 = f32[2,384,384]{2,1,0:T(8,128)S(1)} dynamic-update-slice(f32[2,384,384]{2,1,0:T(8,128)S(1)} %get-tuple-element.543, f32[2,128,128]{2,1,0:T(8,128)S(1)} %fusion.247, s32[]{:T(128)} %constant.191.clone.1..sunk, s32[]{:T(128)S(6)} %select_n.177, s32[]{:T(128)S(6)} %select_n.178) | dynamic-update-slice | bytes 262148 | tf_op jit(solution)/shard_map/while/body/eval_jaxpr/dynamic_update_slice | solution.py:105
  51.9 1.1 dynamic-slice_bitcast_fusion.3
  66.0 2.3 %dynamic_update_slice.11 = f32[2,384,384]{2,1,0:T(8,128)S(1)} dynamic-update-slice(f32[2,384,384]{2,1,0:T(8,128)S(1)} %get-tuple-element.543, f32[2,128,128]{2,1,0:T(8,128)S(1)} %fusion.247, s32[]{:T(128)} %constant.191.clone.1..sunk, s32[]{:T(128)S(6)} %select_n.177, s32[]{:T(128)S(6)} %select_n.178) | dynamic-update-slice | bytes 262148 | tf_op jit(solution)/shard_map/while/body/eval_jaxpr/dynamic_update_slice | solution.py:105
  69.1 4.4 %collective-permute-start.4 = (f32[2,128,384]{2,1,0:T(8,128)}, f32[2,128,384]{2,1,0:T(8,128)S(1)}, u32[]{:S(2)}, u32[]{:S(2)}) collective-permute-start(f32[2,128,384]{2,1,0:T(8,128)} %get-tuple-element.457), channel_id=1, source_target_pairs={{0,2},{2,4},{4,6},{6,8},{8,10},{10,12},{12,14},{1,3},{3,5},{5,7},{... | collective-permute-start | bytes 1179656 | tf_op jit(solution)/shard_map/ppermute | solution.py:19
  73.6 1.3 collective-permute-start.5
  76.2 0.8 copy.42
  77.1 14.9 %collective-permute-done.4 = f32[2,128,384]{2,1,0:T(8,128)S(1)} collective-permute-done((f32[2,128,384]{2,1,0:T(8,128)}, f32[2,128,384]{2,1,0:T(8,128)S(1)}, u32[]{:S(2)}, u32[]{:S(2)}) %collective-permute-start.4) | collective-permute-done | bytes 393248 | tf_op jit(solution)/shard_map/ppermute | solution.py:19
  92.1 1.4 collective-permute-start.6
  93.5 1.3 collective-permute-start.7
  94.8 75.4 %all-reduce.2.cloned.1.call-done = f32[4,2,128,128]{3,2,1,0:T(8,128)} async-done(((f32[4,2,128,128]{3,2,1,0:T(8,128)}), f32[4,2,128,128]{3,2,1,0:T(8,128)}) %all-reduce.2.cloned.1.call-update) | async-done | bytes 524304 | tf_op jit(solution)/shard_map/psum | solution.py:130
  170.2 1.9 %multiply_subtract_fusion = f32[4,2,128,128]{3,2,1,0:T(8,128)} fusion(f32[4,2,128,128]{3,2,1,0:T(8,128)S(1)} %copy-done, f32[4,2,128,128]{3,2,1,0:T(8,128)} %all-reduce.2.cloned.1.call-done), kind=kLoop, calls=%fused_computation.169 | loop fusion | flops 262144 | bytes 1572864 | tf_op jit(solution)/shard_map/sub | solution.py:131
  (63 shorter events, 27.9 us)
Async XLA Ops:
  7.2 163.1 %all-reduce.2.cloned.1.call-start = ((), (), s32[]{:S(2)}) async-start(), calls=%async_computation | async-start | bytes 1048576 | tf_op jit(solution)/shard_map/psum | solution.py:130
  7.2 7.9 %collective-permute-start = (f32[2,128,128]{2,1,0:T(8,128)}, f32[2,128,128]{2,1,0:T(8,128)S(1)}, u32[]{:S(2)}, u32[]{:S(2)}) collective-permute-start(f32[2,128,128]{2,1,0:T(8,128)} %param.23), channel_id=1, source_target_pairs={{0,2},{2,4},{4,6},{6,8},{8,10},{10,12},{12,14},{1,3},{3,5},{5,7},{... | collective-permute-start | bytes 393224 | tf_op jit(solution)/shard_map/ppermute | solution.py:19
  12.1 7.1 %collective-permute-start.1 = (f32[2,128,128]{2,1,0:T(8,128)}, f32[2,128,128]{2,1,0:T(8,128)S(1)}, u32[]{:S(2)}, u32[]{:S(2)}) collective-permute-start(f32[2,128,128]{2,1,0:T(8,128)} %param.23), channel_id=1, source_target_pairs={{2,0},{4,2},{6,4},{8,6},{10,8},{12,10},{14,12},{3,1},{5,3},{7,5},{... | collective-permute-start | bytes 393224 | tf_op jit(solution)/shard_map/ppermute | solution.py:22
  19.2 3.7 %collective-permute-start.2 = (f32[2,384,128]{2,1,0:T(8,128)S(1)}, f32[2,384,128]{2,1,0:T(8,128)S(1)}, u32[]{:S(2)}, u32[]{:S(2)}) collective-permute-start(f32[2,384,128]{2,1,0:T(8,128)S(1)} %constant_dynamic-update-slice_fusion), channel_id=1, source_target_pairs={{0,1},{2,3},{4,5},{6,7},{8,9},{10,11},{12,13},{14,15},{16,17},{18,... | collective-permute-start | bytes 1179656 | tf_op jit(solution)/shard_map/ppermute | solution.py:19
  20.5 3.6 %collective-permute-start.3 = (f32[2,384,128]{2,1,0:T(8,128)S(1)}, f32[2,384,128]{2,1,0:T(8,128)S(1)}, u32[]{:S(2)}, u32[]{:S(2)}) collective-permute-start(f32[2,384,128]{2,1,0:T(8,128)S(1)} %constant_dynamic-update-slice_fusion), channel_id=1, source_target_pairs={{1,0},{3,2},{5,4},{7,6},{9,8},{11,10},{13,12},{15,14},{17,16},{19,... | collective-permute-start | bytes 1179656 | tf_op jit(solution)/shard_map/ppermute | solution.py:22
  25.2 0.9 copy-start.1
  25.2 0.9 copy-start.3
  68.3 6.6 %copy-start = (f32[4,2,128,128]{3,2,1,0:T(8,128)S(1)}, f32[4,2,128,128]{3,2,1,0:T(8,128)}, u32[]{:S(2)}) copy-start(f32[4,2,128,128]{3,2,1,0:T(8,128)} %param.24) | copy-start | bytes 1572868
  69.1 22.8 %collective-permute-start.4 = (f32[2,128,384]{2,1,0:T(8,128)}, f32[2,128,384]{2,1,0:T(8,128)S(1)}, u32[]{:S(2)}, u32[]{:S(2)}) collective-permute-start(f32[2,128,384]{2,1,0:T(8,128)} %get-tuple-element.457), channel_id=1, source_target_pairs={{0,2},{2,4},{4,6},{6,8},{8,10},{10,12},{12,14},{1,3},{3,5},{5,7},{... | collective-permute-start | bytes 1179656 | tf_op jit(solution)/shard_map/ppermute | solution.py:19
  73.6 18.4 %collective-permute-start.5 = (f32[2,128,384]{2,1,0:T(8,128)S(1)}, f32[2,128,384]{2,1,0:T(8,128)S(1)}, u32[]{:S(2)}, u32[]{:S(2)}) collective-permute-start(f32[2,128,384]{2,1,0:T(8,128)S(1)} %get-tuple-element.458), channel_id=1, source_target_pairs={{2,0},{4,2},{6,4},{8,6},{10,8},{12,10},{14,12},{3,1},{5,3},{7,5},{... | collective-permute-start | bytes 1179656 | tf_op jit(solution)/shard_map/ppermute | solution.py:22
  92.0 80.1 %copy-start.2 = (f32[2,128,128]{2,1,0:T(8,128)S(1)}, f32[2,128,128]{2,1,0:T(8,128)}, u32[]{:S(2)}) copy-start(f32[2,128,128]{2,1,0:T(8,128)} %param.23) | copy-start | bytes 393220
  92.1 80.1 %collective-permute-start.6 = (f32[2,128,128]{2,1,0:T(8,128)S(1)}, f32[2,128,128]{2,1,0:T(8,128)S(1)}, u32[]{:S(2)}, u32[]{:S(2)}) collective-permute-start(f32[2,128,128]{2,1,0:T(8,128)S(1)} %get-tuple-element.459), channel_id=1, source_target_pairs={{0,1},{2,3},{4,5},{6,7},{8,9},{10,11},{12,13},{14,15},{16,17},{18,... | collective-permute-start | bytes 393224 | tf_op jit(solution)/shard_map/ppermute | solution.py:19
  93.5 78.6 %collective-permute-start.7 = (f32[2,128,128]{2,1,0:T(8,128)S(1)}, f32[2,128,128]{2,1,0:T(8,128)S(1)}, u32[]{:S(2)}, u32[]{:S(2)}) collective-permute-start(f32[2,128,128]{2,1,0:T(8,128)S(1)} %get-tuple-element.460), channel_id=1, source_target_pairs={{1,0},{3,2},{5,4},{7,6},{9,8},{11,10},{13,12},{15,14},{17,16},{19,... | collective-permute-start | bytes 393224 | tf_op jit(solution)/shard_map/ppermute | solution.py:22
Sparse Core Ops, SparseCore 0:
  77.2 93.0 all-reduce.1
where the time goes:
time: 180 us
  waiting for transfers between devices  96.4 us (54%)
  matrix products  23.8 us (13%)
  starting transfers between devices  17.3 us (10%)
  between operations  14.8 us (8%)
  local copies, waits for them, and re-layouts  12.8 us (7%)
  loops' own time  9.63 us (5%)
  other arithmetic  4.97 us (3%)
    psum x1, waiting for transfers between devices, body(): summed = lax.psum(probe_grad, ('row', 'col'))  75.4 us
    ppermute x4, waiting for transfers between devices, with_halo(): lax.ppermute(lax.slice_in_dim(block, block.shape[dim] - width, None, axis...  16.7 us
    ppermute x4, starting transfers between devices, with_halo(): lax.ppermute(lax.slice_in_dim(block, block.shape[dim] - width, None, axis...  12.1 us
    another operation x1, loops' own time, body(): gradient, probe_grad = lax.fori_loop(0, slot_total, slot_step, start_carry)  9.63 us
    ppermute x4, starting transfers between devices, with_halo(): lax.ppermute(lax.slice_in_dim(block, 0, width, axis=dim), axis, backward)  5.17 us
    dynamic_update_slice x2, local copies, waits for them, and re-layouts, slot_step(): lax.dynamic_update_slice(local_grad, region, (as_index(0), corner_y, corn...  4.83 us
    ppermute x4, waiting for transfers between devices, with_halo(): lax.ppermute(lax.slice_in_dim(block, 0, width, axis=dim), axis, backward)  4.31 us
  transfers between devices with their start and end apart: 9, of which 5 were waited for; matrix products, arithmetic and copies ran while one was open for 3% of the time, Pallas kernels for 0%

commit v1 on v0

v1 whole, which is shorter than its diff:
```python
import jax
import jax.numpy as jnp
import numpy as np
from jax import lax
from jax.experimental import pallas as pl
from jax.experimental.pallas import tpu as pltpu
from jax.sharding import PartitionSpec as P

H = 128


object_rate = 1.0
probe_rate = 1.0
epsilon = 1e-06


def split(value):
    high = value.astype(jnp.bfloat16)
    low = (value - high.astype(jnp.float32)).astype(jnp.bfloat16)
    return high, low


def host_tables(length):
    counter = np.arange(length)
    angle = -2.0 * np.pi / length * (counter[:, None] * counter[None, :] % length)
    cosine = (np.cos(angle) / np.sqrt(length)).astype(np.float32)
    sine = (np.sin(angle) / np.sqrt(length)).astype(np.float32)
    plain = np.block([[cosine, sine], [-sine, cosine]])
    conj = np.block([[cosine, -sine], [sine, cosine]])
    both = np.stack([plain, conj])
    high = both.astype(jnp.bfloat16)
    low = (both - high.astype(np.float32)).astype(jnp.bfloat16)
    return np.concatenate([high, low])


def slots_kernel(
    place_ref,
    offsets_ref,
    counts_ref,
    own_ref,
    own_pair_ref,
    near_ref,
    near_pair_ref,
    far_ref,
    far_pair_ref,
    probe_ref,
    patterns_ref,
    tables_ref,
    keep_probe_ref,
    send_probe_ref,
    keep_grad_ref,
    send_grad_ref,
    weight_ref,
    frame,
    grad,
    term,
):
    modes = probe_ref.shape[0]
    width = probe_ref.shape[-1]
    slots = patterns_ref.shape[2]
    half = modes // 2
    core = place_ref[0]
    odd = place_ref[1]
    near_at = pl.multiple_of((1 - odd) * (2 * width), width)
    far_at = pl.multiple_of(odd * (2 * width), width)
    pair_at = 2 - 2 * core
    void_at = 2 * core

    empty = jnp.zeros((2, 3 * width, width), jnp.float32)
    frame[3] = empty
    frame[void_at] = empty
    frame[1, :, pl.ds(width, width), :] = own_ref[...]
    frame[1, :, pl.ds(near_at, width), :] = near_ref[...]
    frame[1, :, pl.ds(far_at, width), :] = far_ref[...]
    frame[pair_at, :, pl.ds(width, width), :] = own_pair_ref[...]
    frame[pair_at, :, pl.ds(near_at, width), :] = near_pair_ref[...]
    frame[pair_at, :, pl.ds(far_at, width), :] = far_pair_ref[...]
    grad[...] = jnp.zeros_like(grad)

    power = jnp.zeros((width, width), jnp.float32)
    for k in range(modes):
        power = power + probe_ref[k, 0] * probe_ref[k, 0] + probe_ref[k, 1] * probe_ref[k, 1]
    weight_ref[...] = jnp.full(weight_ref.shape, jnp.max(power) + epsilon, jnp.float32)

    lane = lax.broadcasted_iota(jnp.int32, (width, width), 1)

    def right(parts, which):
        value = jnp.concatenate([jnp.concatenate(part, axis=1) for part in parts], axis=0)
        high, low = split(value)
        table = jnp.concatenate(
            [tables_ref[which], tables_ref[which], tables_ref[2 + which]], axis=0
        )
        out = jnp.dot(
            jnp.concatenate([high, low, high], axis=1), table, preferred_element_type=jnp.float32
        )
        return [
            (out[k * width : (k + 1) * width, :width], out[k * width : (k + 1) * width, width:])
            for k in range(modes)
        ]

    def left(parts, which):
        value = jnp.concatenate([jnp.concatenate(part, axis=0) for part in parts], axis=1)
        high, low = split(value)
        table = jnp.concatenate(
            [tables_ref[1 - which], tables_ref[3 - which], tables_ref[1 - which]], axis=1
        )
        out = jnp.dot(
            table, jnp.concatenate([high, high, low], axis=0), preferred_element_type=jnp.float32
        )
        return [
            (out[:width, k * width : (k + 1) * width], out[width:, k * width : (k + 1) * width])
            for k in range(modes)
        ]

    for slot in range(slots):
        corner_y = offsets_ref[0, 0, slot, 0]
        corner_x = offsets_ref[0, 0, slot, 1]
        column = corner_x // width
        shift = corner_x - column * width
        back_shift = lax.rem(width - shift, width)
        rows = pl.ds(corner_y, width)
        live = (slot < counts_ref[0, 0]).astype(jnp.float32)

        window = []
        for part in range(2):
            both = jnp.where(
                lane >= shift, frame[column, part, rows, :], frame[column + 1, part, rows, :]
            )
            window.append(pltpu.roll(both, back_shift, 1))
        win_re, win_im = window

        exits = []
        for k in range(modes):
            probe_re, probe_im = probe_ref[k, 0], probe_ref[k, 1]
            exits.append(
                (
                    probe_re * win_re - probe_im * win_im,
                    probe_re * win_im + probe_im * win_re,
                )
            )
        far = left(right(exits, 0), 0)
        intensity = sum(re * re + im * im for re, im in far)
        misfit = (intensity - patterns_ref[0, 0, slot]) * live
        back = right(left([(misfit * re, misfit * im) for re, im in far], 1), 1)

        grad_re = jnp.zeros((width, width), jnp.float32)
        grad_im = jnp.zeros((width, width), jnp.float32)
        for k in range(modes):
            probe_re, probe_im = probe_ref[k, 0], probe_ref[k, 1]
            back_re, back_im = back[k]
            grad_re = grad_re + probe_re * back_re + probe_im * back_im
            grad_im = grad_im + probe_re * back_im - probe_im * back_re
            term_re = win_re * back_re + win_im * back_im
            term_im = win_re * back_im - win_im * back_re
            if slot == 0:
                term[k, 0] = term_re
                term[k, 1] = term_im
            else:
                term[k, 0] += term_re
                term[k, 1] += term_im
        for part, value in enumerate((grad_re, grad_im)):
            turned = pltpu.roll(value, shift, 1)
            grad[column, part, rows, :] += jnp.where(lane >= shift, turned, 0.0)
            grad[column + 1, part, rows, :] += jnp.where(lane >= shift, 0.0, turned)

    mine = core * half
    theirs = half - mine
    keep_probe_ref[...] = term[pl.ds(mine, half)]
    send_probe_ref[...] = term[pl.ds(theirs, half)]
    for index, place in enumerate((near_at, far_at, width)):
        keep_grad_ref[index] = grad[1, :, pl.ds(place, width), :]
        send_grad_ref[index] = grad[pair_at, :, pl.ds(place, width), :]


def run_slots(place, offsets, counts, blocks, probe, patterns):
    modes, _, width, _ = probe.shape
    half = modes // 2
    tables = jnp.asarray(host_tables(width))
    smem = pl.BlockSpec(memory_space=pltpu.SMEM)
    vmem = pl.BlockSpec(memory_space=pltpu.VMEM)
    probe_half = jax.ShapeDtypeStruct((half, 2, width, width), jnp.float32)
    grad_rows = jax.ShapeDtypeStruct((3, 2, width, width), jnp.float32)
    slots = patterns.shape[2]
    return pl.pallas_call(
        slots_kernel,
        out_shape=(
            probe_half,
            probe_half,
            grad_rows,
            grad_rows,
            jax.ShapeDtypeStruct((8, width), jnp.float32),
        ),
        in_specs=[smem] * 3 + [vmem] * 9,
        out_specs=(vmem,) * 5,
        scratch_shapes=[
            pltpu.VMEM((4, 2, 3 * width, width), jnp.float32),
            pltpu.VMEM((4, 2, 3 * width, width), jnp.float32),
            pltpu.VMEM((modes, 2, width, width), jnp.float32),
        ],
        cost_estimate=pl.CostEstimate(
            flops=slots * modes * 4 * 3 * 8 * width**3,
            bytes_accessed=40 * width * width * 4,
            transcendentals=0,
        ),
        name="slots",
    )(place, offsets, counts, *blocks, probe, patterns, tables)


def body(object_field, probe, patterns, offsets, counts):
    row_total = lax.axis_size("row")
    tile_total = row_total * lax.axis_size("col")
    modes, _, width, _ = probe.shape
    half = modes // 2
    row = lax.axis_index("row")
    core = lax.axis_index("col")
    place = jnp.stack([core, row % 2]).astype(jnp.int32)

    pair = [(0, 1), (1, 0)]
    near = [(i, i ^ 1) for i in range(row_total)]
    far = [(i, i + 1) for i in range(1, row_total - 1, 2)]
    far = far + [(target, source) for source, target in far]

    near_block = lax.ppermute(object_field, "row", near)
    far_block = lax.ppermute(object_field, "row", far)
    own_pair = lax.ppermute(object_field, "col", pair)
    near_pair = lax.ppermute(near_block, "col", pair)
    far_pair = lax.ppermute(far_block, "col", pair)
    blocks = (object_field, own_pair, near_block, near_pair, far_block, far_pair)
    keep_probe, send_probe, keep_grad, send_grad, weight = run_slots(
        place, offsets, counts, blocks, probe, patterns
    )

    got_probe = lax.ppermute(send_probe, "col", pair)
    got_grad = lax.ppermute(send_grad, "col", pair)
    mine = (keep_probe + got_probe).reshape(row_total, -1, width)
    mine = lax.all_to_all(mine, "row", 0, 0, tiled=True)
    mine = jnp.broadcast_to(jnp.sum(mine, axis=0, keepdims=True), mine.shape)
    strips = keep_grad + got_grad
    near_strip = lax.ppermute(strips[0], "row", near)
    far_strip = lax.ppermute(strips[1], "row", far)
    mine = lax.all_to_all(mine, "row", 0, 0, tiled=True).reshape(half, 2, width, width)
    other = lax.ppermute(mine, "col", pair)
    summed = jnp.where(
        core == 0,
        jnp.concatenate([mine, other], axis=0),
        jnp.concatenate([other, mine], axis=0),
    )
    object_grad = strips[2] + near_strip + far_strip
    object_field = object_field - object_rate * object_grad / weight[0, 0]
    probe = probe - probe_rate * summed / tile_total
    return (object_field, probe)


def solution(mesh):
    placed = (
        P(None, ("tilt", "row"), "col"),
        P("tilt", None, None, None),
        P(("tilt", "row"), "col", None, None, None),
        P(("tilt", "row"), "col", None, None),
        P(("tilt", "row"), "col"),
    )
    return jax.shard_map(
        body,
        mesh=mesh,
        in_specs=placed,
        out_specs=(P(None, ("tilt", "row"), "col"), P("tilt", None, None, None)),
        check_vma=False,
    )
```

time: 180 us -> 57.8 us (0.32)
  waiting for transfers between devices: 96.4 us -> 22.3 us
  matrix products: 23.8 us -> 0 us
  between operations: 14.8 us -> 1.46 us
  loops' own time: 9.63 us -> 0 us
  local copies, waits for them, and re-layouts: 12.8 us -> 3.26 us
  Pallas kernels: 0 us -> 5.83 us
  starting transfers between devices: 17.3 us -> 19.8 us
    psum x1 -> x0, waiting for transfers between devices: 75.4 us -> none  [body(): summed = lax.psum(probe_grad, ('row', 'col'))]
    dot_general x32 -> x0, matrix products: 23.8 us -> none  [the longest x4 3.06 us: right_product(): jnp.einsum('kab,bc->kac', imag_part, sin_table, precision=hp)]
    all_to_all x0 -> x2, waiting for transfers between devices: none -> 16.3 us  [the longest x1 9.29 us: body(): mine = lax.all_to_all(mine, 'row', 0, 0, tiled=True)]
    ppermute x8 -> x10, waiting for transfers between devices: 21 us -> 6.02 us  [the longest x1 4.63 us: body(): near_block = lax.ppermute(object_field, 'row', near)]
    another operation x1 -> x0, loops' own time: 9.63 us -> none  [body(): gradient, probe_grad = lax.fori_loop(0, slot_total, slot_step, start_carry)]
    all_to_all x0 -> x2, starting transfers between devices: none -> 9.48 us  [the longest x1 5.9 us: body(): mine = lax.all_to_all(mine, 'row', 0, 0, tiled=True)]
    ppermute x8 -> x10, starting transfers between devices: 17.2 us -> 10.4 us  [the longest x1 5.82 us: body(): near_block = lax.ppermute(object_field, 'row', near)]
    pallas_call x0 -> x1, Pallas kernels: none -> 5.83 us  [run_slots(): pl.pallas_call(slots_kernel, out_shape=(probe_half, probe_half, grad_rows...]
  transfers between devices with their start and end apart: 9 -> 12, of which waited for: 5 -> 4; matrix products, arithmetic and copies ran while one was open for 3% -> 7% of each run, Pallas kernels for 0% -> 0%
where the time goes in v1:
time: 57.8 us; the launch traced here: 57.3 us
  waiting for transfers between devices  22.3 us (39%)
  starting transfers between devices  19.8 us (34%)
  Pallas kernels  5.83 us (10%)
  other arithmetic  4.62 us (8%)
  local copies, waits for them, and re-layouts  3.26 us (6%)
  between operations  1.46 us (3%)
    all_to_all x1, waiting for transfers between devices, body(): mine = lax.all_to_all(mine, 'row', 0, 0, tiled=True)  9.29 us
    all_to_all x1, waiting for transfers between devices, body(): lax.all_to_all(mine, 'row', 0, 0, tiled=True).reshape(half, 2, width, width)  7 us
    all_to_all x1, starting transfers between devices, body(): mine = lax.all_to_all(mine, 'row', 0, 0, tiled=True)  5.9 us
    pallas_call x1, Pallas kernels, run_slots(): pl.pallas_call(slots_kernel, out_shape=(probe_half, probe_half, grad_rows...  5.83 us
    ppermute x1, starting transfers between devices, body(): near_block = lax.ppermute(object_field, 'row', near)  5.82 us
    ppermute x1, waiting for transfers between devices, body(): near_block = lax.ppermute(object_field, 'row', near)  4.63 us
    all_to_all x1, starting transfers between devices, body(): lax.all_to_all(mine, 'row', 0, 0, tiled=True).reshape(half, 2, width, width)  3.59 us
    ppermute x1, starting transfers between devices, body(): near_strip = lax.ppermute(strips[0], 'row', near)  2.08 us
  transfers between devices with their start and end apart: 12, of which 4 were waited for; matrix products, arithmetic and copies ran while one was open for 7% of the time, Pallas kernels for 0%

profile of v1, /device:TPU:0, one launch (start us, length us, event | category | flops | bytes accessed | tf_op | source)
XLA Modules:
  0.0 57.3 jit_solution(2686054038586609530)
XLA Ops:
  0.6 0.7 %collective-permute-start.3 = (f32[2,128,128]{2,1,0:T(8,128)}, f32[2,128,128]{2,1,0:T(8,128)S(1)}, u32[]{:S(2)}, u32[]{:S(2)}) collective-permute-start(f32[2,128,128]{2,1,0:T(8,128)} %own_ref.1), channel_id=1, source_target_pairs={{2,4},{6,8},{10,12},{4,2},{8,6},{12,10},{3,5},{7,9},{11,13},{5,3},... | collective-permute-start | bytes 393224 | tf_op jit(solution)/shard_map/ppermute | solution.py:224
  1.3 5.8 %collective-permute-start.1 = (f32[2,128,128]{2,1,0:T(8,128)}, f32[2,128,128]{2,1,0:T(8,128)S(1)}, u32[]{:S(2)}, u32[]{:S(2)}) collective-permute-start(f32[2,128,128]{2,1,0:T(8,128)} %own_ref.1), channel_id=1, source_target_pairs={{0,2},{2,0},{4,6},{6,4},{8,10},{10,8},{12,14},{14,12},{1,3},{3,1},... | collective-permute-start | bytes 393224 | tf_op jit(solution)/shard_map/ppermute | solution.py:223
  7.1 0.5 collective-permute-start.4
  7.6 4.6 %collective-permute-done.1.near_ref = f32[2,128,128]{2,1,0:T(8,128)S(1)} collective-permute-done((f32[2,128,128]{2,1,0:T(8,128)}, f32[2,128,128]{2,1,0:T(8,128)S(1)}, u32[]{:S(2)}, u32[]{:S(2)}) %collective-permute-start.1) | collective-permute-done | bytes 131104 | tf_op jit(solution)/shard_map/ppermute | solution.py:223
  12.3 0.0 collective-permute-start.2
  13.0 0.7 %pad_add_fusion.place_ref = s32[2]{0:T(128)} fusion(s32[1]{0:T(128)} %bitcast.1, s32[1]{0:T(128)} %bitcast), kind=kLoop, calls=%fused_computation.10 | loop fusion | flops 2 | bytes 16 | tf_op jit(solution)/shard_map/stack | solution.py:216
  13.7 0.6 %copy-done.6 = f32[2,128,128]{2,1,0:T(8,128)} copy-done((f32[2,128,128]{2,1,0:T(8,128)}, f32[2,128,128]{2,1,0:T(8,128)S(1)}, u32[]{:S(2)}) %copy-start.6) | copy-done | bytes 131096
  14.3 0.0 copy-done.7
  14.4 0.6 %copy-done.8 = f32[2,128,128]{2,1,0:T(8,128)} copy-done((f32[2,128,128]{2,1,0:T(8,128)}, f32[2,128,128]{2,1,0:T(8,128)S(1)}, u32[]{:S(2)}) %copy-start.8) | copy-done | bytes 131096
  15.0 5.8 %slots.1 = (f32[2,2,128,128]{3,2,1,0:T(8,128)}, f32[2,2,128,128]{3,2,1,0:T(8,128)}, f32[3,2,128,128]{3,2,1,0:T(8,128)}, f32[3,2,128,128]{3,2,1,0:T(8,128)}, f32[8,128]{1,0:T(8,128)}) custom-call(s32[2]{0:T(128)} %pad_add_fusion.place_ref, s32[1,1,2,2]{3,2,1,0:T(2,128)} %offsets_ref.1, s32[1,1]{1,0:T(1,128)S(6)} %copy.8.counts_ref, f32[2,128,128]{2,1,0:T(8,128)} %own_ref.1, ...), custom_call_target="tpu_custom_call" | custom-call | flops 1610612736 | bytes 2621440 | tf_op jit(solution)/shard_map/slots/pallas_call | solution.py:184
  20.8 0.4 collective-permute-start.8
  21.3 1.4 %collective-permute-done.8 = f32[2,2,128,128]{3,2,1,0:T(8,128)S(1)} collective-permute-done((f32[2,2,128,128]{3,2,1,0:T(8,128)}, f32[2,2,128,128]{3,2,1,0:T(8,128)S(1)}, u32[]{:S(2)}, u32[]{:S(2)}) %collective-permute-start.8) | collective-permute-done | bytes 262176 | tf_op jit(solution)/shard_map/ppermute | solution.py:233
  22.7 1.7 %add.20 = f32[2,2,128,128]{3,2,1,0:T(8,128)} add(f32[2,2,128,128]{3,2,1,0:T(8,128)} %get-tuple-element.10, f32[2,2,128,128]{3,2,1,0:T(8,128)S(1)} %collective-permute-done.8) | non-fusion elementwise | flops 65536 | bytes 786432 | tf_op jit(solution)/shard_map/add | solution.py:235
  24.4 5.9 %all-to-all-start = ((f32[8,64,128]{2,1,0:T(8,128)}), f32[8,64,128]{2,1,0:T(8,128)S(1)}, u32[]{:S(2)}, u32[]{:S(2)}) async-start(f32[8,64,128]{2,1,0:T(8,128)} %bitcast.6), calls=%async_computation | async-start | bytes 524288 | tf_op jit(solution)/shard_map/all_to_all | solution.py:236
  30.3 0.2 collective-permute-start.5
  30.4 9.3 %all-to-all-done = f32[8,64,128]{2,1,0:T(8,128)S(1)} async-done(((f32[8,64,128]{2,1,0:T(8,128)}), f32[8,64,128]{2,1,0:T(8,128)S(1)}, u32[]{:S(2)}, u32[]{:S(2)}) %all-to-all-start) | async-done | bytes 262176 | tf_op jit(solution)/shard_map/all_to_all | solution.py:236
  39.8 0.7 %broadcast_in_dim.2 = f32[8,64,128]{2,1,0:T(8,128)} broadcast(f32[64,128]{1,0:T(8,128)S(1)} %reduce_sum.9), dimensions={1,2} | broadcast | bytes 294912 | tf_op jit(solution)/shard_map/broadcast_in_dim | solution.py:237
  40.5 3.6 %all-to-all-start.1 = ((f32[8,64,128]{2,1,0:T(8,128)}), f32[8,64,128]{2,1,0:T(8,128)S(1)}, u32[]{:S(2)}, u32[]{:S(2)}) async-start(f32[8,64,128]{2,1,0:T(8,128)} %broadcast_in_dim.2), calls=%async_computation.1 | async-start | bytes 524288 | tf_op jit(solution)/shard_map/all_to_all | solution.py:241
  44.2 2.1 %collective-permute-start.6 = (f32[2,128,128]{2,1,0:T(8,128)S(1)}, f32[2,128,128]{2,1,0:T(8,128)S(1)}, u32[]{:S(2)}, u32[]{:S(2)}) collective-permute-start(f32[2,128,128]{2,1,0:T(8,128)S(1)} %get-tuple-element.12), channel_id=1, source_target_pairs={{0,2},{2,0},{4,6},{6,4},{8,10},{10,8},{12,14},{14,12},{1,3},{3,1},... | collective-permute-start | bytes 393224 | tf_op jit(solution)/shard_map/ppermute | solution.py:239
  46.3 0.7 %collective-permute-start.7 = (f32[2,128,128]{2,1,0:T(8,128)S(1)}, f32[2,128,128]{2,1,0:T(8,128)S(1)}, u32[]{:S(2)}, u32[]{:S(2)}) collective-permute-start(f32[2,128,128]{2,1,0:T(8,128)S(1)} %get-tuple-element.13), channel_id=1, source_target_pairs={{2,4},{6,8},{10,12},{4,2},{8,6},{12,10},{3,5},{7,9},{11,13},{5,3},... | collective-permute-start | bytes 393224 | tf_op jit(solution)/shard_map/ppermute | solution.py:240
  46.9 7.0 %all-to-all-done.1 = f32[8,64,128]{2,1,0:T(8,128)S(1)} async-done(((f32[8,64,128]{2,1,0:T(8,128)}), f32[8,64,128]{2,1,0:T(8,128)S(1)}, u32[]{:S(2)}, u32[]{:S(2)}) %all-to-all-start.1) | async-done | bytes 262176 | tf_op jit(solution)/shard_map/all_to_all | solution.py:241
  53.9 1.2 %slice.15 = f32[1,1]{1,0:T(1,128)} slice(f32[8,128]{1,0:T(8,128)} %get-tuple-element.9), slice={[0:1], [0:1]} | slice | bytes 8 | tf_op jit(solution)/shard_map/slice | solution.py:249
  55.1 1.3 %fusion.5 = f32[2,128,128]{2,1,0:T(8,128)} fusion(f32[2,128,128]{2,1,0:T(8,128)S(1)} %copy-done.2, f32[2,128,128]{2,1,0:T(8,128)S(1)} %collective-permute-done.7, f32[2,128,128]{2,1,0:T(8,128)S(1)} %collective-permute-done.6, f32[3,2,128,128]{3,2,1,0:T(8,128)S(1)} %add.17, f32[]{:T(128)} %bitcast.5), kind=kLoop, calls=%fused_computation.9 | loop fusion | flops 131072 | bytes 655364 | tf_op jit(solution)/shard_map/sub | solution.py:249
  56.5 0.9 %fusion.1 = f32[4,2,128,128]{3,2,1,0:T(8,128)} fusion(f32[4,2,128,128]{3,2,1,0:T(8,128)S(1)} %copy-done, f32[2,2,128,128]{3,2,1,0:T(8,128)S(1)} %collective-permute-done.9, f32[2,2,128,128]{3,2,1,0:T(8,128)S(1)} %bitcast.20, pred[]{:T(512)S(6)} %eq.5), kind=kLoop, calls=%fused_computation.2 | loop fusion | flops 655360 | bytes 1572865 | tf_op jit(solution)/shard_map/sub | solution.py:250
  (28 shorter events, 0.1 us)
Async XLA Ops:
  0.6 6.5 %collective-permute-start.3 = (f32[2,128,128]{2,1,0:T(8,128)}, f32[2,128,128]{2,1,0:T(8,128)S(1)}, u32[]{:S(2)}, u32[]{:S(2)}) collective-permute-start(f32[2,128,128]{2,1,0:T(8,128)} %own_ref.1), channel_id=1, source_target_pairs={{2,4},{6,8},{10,12},{4,2},{8,6},{12,10},{3,5},{7,9},{11,13},{5,3},... | collective-permute-start | bytes 393224 | tf_op jit(solution)/shard_map/ppermute | solution.py:224
  1.3 11.0 %collective-permute-start.1 = (f32[2,128,128]{2,1,0:T(8,128)}, f32[2,128,128]{2,1,0:T(8,128)S(1)}, u32[]{:S(2)}, u32[]{:S(2)}) collective-permute-start(f32[2,128,128]{2,1,0:T(8,128)} %own_ref.1), channel_id=1, source_target_pairs={{0,2},{2,0},{4,6},{6,4},{8,10},{10,8},{12,14},{14,12},{1,3},{3,1},... | collective-permute-start | bytes 393224 | tf_op jit(solution)/shard_map/ppermute | solution.py:223
  7.1 6.5 %collective-permute-start = (f32[2,128,128]{2,1,0:T(8,128)}, f32[2,128,128]{2,1,0:T(8,128)S(1)}, u32[]{:S(2)}, u32[]{:S(2)}) collective-permute-start(f32[2,128,128]{2,1,0:T(8,128)} %own_ref.1), channel_id=1, source_target_pairs={{0,1},{1,0},{2,3},{3,2},{4,5},{5,4},{6,7},{7,6},{8,9},{9,8},{10,11... | collective-permute-start | bytes 393224 | tf_op jit(solution)/shard_map/ppermute | solution.py:225
  7.1 6.6 %copy-start.4 = (f32[2,128,128]{2,1,0:T(8,128)}, f32[2,128,128]{2,1,0:T(8,128)S(1)}, u32[]{:S(2)}) copy-start(f32[2,128,128]{2,1,0:T(8,128)S(1)} %collective-permute-done.3.far_ref) | copy-start | bytes 393220
  7.1 6.5 %collective-permute-start.4 = (f32[2,128,128]{2,1,0:T(8,128)S(1)}, f32[2,128,128]{2,1,0:T(8,128)S(1)}, u32[]{:S(2)}, u32[]{:S(2)}) collective-permute-start(f32[2,128,128]{2,1,0:T(8,128)S(1)} %collective-permute-done.3.far_ref), channel_id=1, source_target_pairs={{0,1},{1,0},{2,3},{3,2},{4,5},{5,4},{6,7},{7,6},{8,9},{9,8},{10,11... | collective-permute-start | bytes 393224 | tf_op jit(solution)/shard_map/ppermute | solution.py:227
  12.3 1.4 %copy-start.5 = (f32[2,128,128]{2,1,0:T(8,128)}, f32[2,128,128]{2,1,0:T(8,128)S(1)}, u32[]{:S(2)}) copy-start(f32[2,128,128]{2,1,0:T(8,128)S(1)} %collective-permute-done.1.near_ref) | copy-start | bytes 393220
  12.3 1.4 %collective-permute-start.2 = (f32[2,128,128]{2,1,0:T(8,128)S(1)}, f32[2,128,128]{2,1,0:T(8,128)S(1)}, u32[]{:S(2)}, u32[]{:S(2)}) collective-permute-start(f32[2,128,128]{2,1,0:T(8,128)S(1)} %collective-permute-done.1.near_ref), channel_id=1, source_target_pairs={{0,1},{1,0},{2,3},{3,2},{4,5},{5,4},{6,7},{7,6},{8,9},{9,8},{10,11... | collective-permute-start | bytes 393224 | tf_op jit(solution)/shard_map/ppermute | solution.py:226
  13.7 0.7 %copy-start.6 = (f32[2,128,128]{2,1,0:T(8,128)}, f32[2,128,128]{2,1,0:T(8,128)S(1)}, u32[]{:S(2)}) copy-start(f32[2,128,128]{2,1,0:T(8,128)S(1)} %collective-permute-done.own_pair_ref) | copy-start | bytes 393220
  13.7 0.7 %copy-start.7 = (f32[2,128,128]{2,1,0:T(8,128)}, f32[2,128,128]{2,1,0:T(8,128)S(1)}, u32[]{:S(2)}) copy-start(f32[2,128,128]{2,1,0:T(8,128)S(1)} %collective-permute-done.4.far_pair_ref) | copy-start | bytes 393220
  14.4 0.7 %copy-start.8 = (f32[2,128,128]{2,1,0:T(8,128)}, f32[2,128,128]{2,1,0:T(8,128)S(1)}, u32[]{:S(2)}) copy-start(f32[2,128,128]{2,1,0:T(8,128)S(1)} %collective-permute-done.2.near_pair_ref) | copy-start | bytes 393220
  20.8 1.8 %collective-permute-start.8 = (f32[2,2,128,128]{3,2,1,0:T(8,128)}, f32[2,2,128,128]{3,2,1,0:T(8,128)S(1)}, u32[]{:S(2)}, u32[]{:S(2)}) collective-permute-start(f32[2,2,128,128]{3,2,1,0:T(8,128)} %get-tuple-element.11), channel_id=1, source_target_pairs={{0,1},{1,0},{2,3},{3,2},{4,5},{5,4},{6,7},{7,6},{8,9},{9,8},{10,11... | collective-permute-start | bytes 786440 | tf_op jit(solution)/shard_map/ppermute | solution.py:233
  24.4 5.9 %copy-start.3 = (f32[3,2,128,128]{3,2,1,0:T(8,128)S(1)}, f32[3,2,128,128]{3,2,1,0:T(8,128)}, u32[]{:S(2)}) copy-start(f32[3,2,128,128]{3,2,1,0:T(8,128)} %get-tuple-element.8) | copy-start | bytes 1179652
  24.4 15.4 %all-to-all-start = ((f32[8,64,128]{2,1,0:T(8,128)}), f32[8,64,128]{2,1,0:T(8,128)S(1)}, u32[]{:S(2)}, u32[]{:S(2)}) async-start(f32[8,64,128]{2,1,0:T(8,128)} %bitcast.6), calls=%async_computation | async-start | bytes 524288 | tf_op jit(solution)/shard_map/all_to_all | solution.py:236
  30.3 13.8 %collective-permute-start.5 = (f32[3,2,128,128]{3,2,1,0:T(8,128)S(1)}, f32[3,2,128,128]{3,2,1,0:T(8,128)S(1)}, u32[]{:S(2)}, u32[]{:S(2)}) collective-permute-start(f32[3,2,128,128]{3,2,1,0:T(8,128)S(1)} %copy-done.3), channel_id=1, source_target_pairs={{0,1},{1,0},{2,3},{3,2},{4,5},{5,4},{6,7},{7,6},{8,9},{9,8},{10,11... | collective-permute-start | bytes 1179656 | tf_op jit(solution)/shard_map/ppermute | solution.py:234
  39.7 4.3 %copy-start.1 = (f32[3,2,128,128]{3,2,1,0:T(8,128)S(1)}, f32[3,2,128,128]{3,2,1,0:T(8,128)}, u32[]{:S(2)}) copy-start(f32[3,2,128,128]{3,2,1,0:T(8,128)} %get-tuple-element.7) | copy-start | bytes 1179652
  40.5 13.4 %all-to-all-start.1 = ((f32[8,64,128]{2,1,0:T(8,128)}), f32[8,64,128]{2,1,0:T(8,128)S(1)}, u32[]{:S(2)}, u32[]{:S(2)}) async-start(f32[8,64,128]{2,1,0:T(8,128)} %broadcast_in_dim.2), calls=%async_computation.1 | async-start | bytes 524288 | tf_op jit(solution)/shard_map/all_to_all | solution.py:241
  44.1 11.0 %copy-start.2 = (f32[2,128,128]{2,1,0:T(8,128)S(1)}, f32[2,128,128]{2,1,0:T(8,128)}, u32[]{:S(2)}) copy-start(f32[2,128,128]{2,1,0:T(8,128)} %own_ref.1) | copy-start | bytes 393220
  44.1 12.3 %copy-start = (f32[4,2,128,128]{3,2,1,0:T(8,128)S(1)}, f32[4,2,128,128]{3,2,1,0:T(8,128)}, u32[]{:S(2)}) copy-start(f32[4,2,128,128]{3,2,1,0:T(8,128)} %probe_ref.1) | copy-start | bytes 1572868
  44.2 10.9 %collective-permute-start.6 = (f32[2,128,128]{2,1,0:T(8,128)S(1)}, f32[2,128,128]{2,1,0:T(8,128)S(1)}, u32[]{:S(2)}, u32[]{:S(2)}) collective-permute-start(f32[2,128,128]{2,1,0:T(8,128)S(1)} %get-tuple-element.12), channel_id=1, source_target_pairs={{0,2},{2,0},{4,6},{6,4},{8,10},{10,8},{12,14},{14,12},{1,3},{3,1},... | collective-permute-start | bytes 393224 | tf_op jit(solution)/shard_map/ppermute | solution.py:239
  46.3 8.9 %collective-permute-start.7 = (f32[2,128,128]{2,1,0:T(8,128)S(1)}, f32[2,128,128]{2,1,0:T(8,128)S(1)}, u32[]{:S(2)}, u32[]{:S(2)}) collective-permute-start(f32[2,128,128]{2,1,0:T(8,128)S(1)} %get-tuple-element.13), channel_id=1, source_target_pairs={{2,4},{6,8},{10,12},{4,2},{8,6},{12,10},{3,5},{7,9},{11,13},{5,3},... | collective-permute-start | bytes 393224 | tf_op jit(solution)/shard_map/ppermute | solution.py:240
  53.9 2.5 %collective-permute-start.9 = (f32[2,2,128,128]{3,2,1,0:T(8,128)S(1)}, f32[2,2,128,128]{3,2,1,0:T(8,128)S(1)}, u32[]{:S(2)}, u32[]{:S(2)}) collective-permute-start(f32[2,2,128,128]{3,2,1,0:T(8,128)S(1)} %bitcast.19), channel_id=1, source_target_pairs={{0,1},{1,0},{2,3},{3,2},{4,5},{5,4},{6,7},{7,6},{8,9},{9,8},{10,11... | collective-permute-start | bytes 786440 | tf_op jit(solution)/shard_map/ppermute | solution.py:242

commit v2 on v1

--- a/solution.py
+++ b/solution.py
@@ -5,8 +5,6 @@
 from jax.experimental import pallas as pl
 from jax.experimental.pallas import tpu as pltpu
 from jax.sharding import PartitionSpec as P
-
-H = 128
 
 
 object_rate = 1.0
@@ -33,9 +31,47 @@
     return np.concatenate([high, low])
 
 
+def stage_kernel(count, *refs):
+    sources, targets, power_of = refs[:count], refs[count : 2 * count], refs[count]
+    weight_ref, sems = refs[2 * count :]
+    copies = [
+        pltpu.make_async_copy(source, target, sems.at[index])
+        for index, (source, target) in enumerate(zip(sources, targets))
+    ]
+    for copy in copies:
+        copy.start()
+    for copy in copies:
+        copy.wait()
+    power = jnp.zeros(power_of.shape[2:], jnp.float32)
+    for k in range(power_of.shape[0]):
+        power = power + power_of[k, 0] * power_of[k, 0] + power_of[k, 1] * power_of[k, 1]
+    weight_ref[...] = jnp.full(weight_ref.shape, jnp.max(power) + epsilon, jnp.float32)
+
+
+def stage(probe, *others):
+    arrays = tuple(
+        pltpu.with_memory_space_constraint(a, pltpu.HBM) for a in (probe,) + others
+    )
+    count = len(arrays)
+    return pl.pallas_call(
+        lambda *refs: stage_kernel(count, *refs),
+        out_shape=tuple(jax.ShapeDtypeStruct(a.shape, a.dtype) for a in arrays)
+        + (jax.ShapeDtypeStruct((8, probe.shape[-1]), jnp.float32),),
+        in_specs=[pl.BlockSpec(memory_space=pltpu.HBM)] * count,
+        out_specs=(pl.BlockSpec(memory_space=pltpu.VMEM),) * (count + 1),
+        scratch_shapes=[pltpu.SemaphoreType.DMA((count,))],
+        cost_estimate=pl.CostEstimate(
+            flops=8 * probe.size,
+            bytes_accessed=sum(2 * a.size * a.dtype.itemsize for a in arrays),
+            transcendentals=0,
+        ),
+        compiler_params=pltpu.CompilerParams(vmem_limit_bytes=8 << 20),
+        name="stage",
+    )(*arrays)
+
+
 def slots_kernel(
-    place_ref,
-    offsets_ref,
+    offsets_hbm,
     counts_ref,
     own_ref,
     own_pair_ref,
@@ -50,17 +86,20 @@
     send_probe_ref,
     keep_grad_ref,
     send_grad_ref,
-    weight_ref,
+    offsets_ref,
+    offsets_sem,
     frame,
     grad,
     term,
 ):
+    fetch = pltpu.make_async_copy(offsets_hbm, offsets_ref, offsets_sem)
+    fetch.start()
     modes = probe_ref.shape[0]
     width = probe_ref.shape[-1]
     slots = patterns_ref.shape[2]
     half = modes // 2
-    core = place_ref[0]
-    odd = place_ref[1]
+    core = lax.axis_index("col")
+    odd = lax.rem(lax.axis_index("row"), 2)
     near_at = pl.multiple_of((1 - odd) * (2 * width), width)
     far_at = pl.multiple_of(odd * (2 * width), width)
     pair_at = 2 - 2 * core
@@ -77,10 +116,7 @@
     frame[pair_at, :, pl.ds(far_at, width), :] = far_pair_ref[...]
     grad[...] = jnp.zeros_like(grad)
 
-    power = jnp.zeros((width, width), jnp.float32)
-    for k in range(modes):
-        power = power + probe_ref[k, 0] * probe_ref[k, 0] + probe_ref[k, 1] * probe_ref[k, 1]
-    weight_ref[...] = jnp.full(weight_ref.shape, jnp.max(power) + epsilon, jnp.float32)
+    fetch.wait()
 
     lane = lax.broadcasted_iota(jnp.int32, (width, width), 1)
 
@@ -172,10 +208,9 @@
         send_grad_ref[index] = grad[pair_at, :, pl.ds(place, width), :]
 
 
-def run_slots(place, offsets, counts, blocks, probe, patterns):
+def run_slots(offsets, counts, blocks, probe, patterns, tables):
     modes, _, width, _ = probe.shape
     half = modes // 2
-    tables = jnp.asarray(host_tables(width))
     smem = pl.BlockSpec(memory_space=pltpu.SMEM)
     vmem = pl.BlockSpec(memory_space=pltpu.VMEM)
     probe_half = jax.ShapeDtypeStruct((half, 2, width, width), jnp.float32)
@@ -188,11 +223,12 @@
             probe_half,
             grad_rows,
             grad_rows,
-            jax.ShapeDtypeStruct((8, width), jnp.float32),
         ),
-        in_specs=[smem] * 3 + [vmem] * 9,
-        out_specs=(vmem,) * 5,
+        in_specs=[pl.BlockSpec(memory_space=pltpu.HBM), smem] + [vmem] * 9,
+        out_specs=(vmem,) * 4,
         scratch_shapes=[
+            pltpu.SMEM(offsets.shape, offsets.dtype),
+            pltpu.SemaphoreType.DMA,
             pltpu.VMEM((4, 2, 3 * width, width), jnp.float32),
             pltpu.VMEM((4, 2, 3 * width, width), jnp.float32),
             pltpu.VMEM((modes, 2, width, width), jnp.float32),
@@ -202,8 +238,9 @@
             bytes_accessed=40 * width * width * 4,
             transcendentals=0,
         ),
+        compiler_params=pltpu.CompilerParams(vmem_limit_bytes=16 << 20),
         name="slots",
-    )(place, offsets, counts, *blocks, probe, patterns, tables)
+    )(offsets, counts, *blocks, probe, patterns, tables)
 
 
 def body(object_field, probe, patterns, offsets, counts):
@@ -211,9 +248,7 @@
     tile_total = row_total * lax.axis_size("col")
     modes, _, width, _ = probe.shape
     half = modes // 2
-    row = lax.axis_index("row")
     core = lax.axis_index("col")
-    place = jnp.stack([core, row % 2]).astype(jnp.int32)
 
     pair = [(0, 1), (1, 0)]
     near = [(i, i ^ 1) for i in range(row_total)]
@@ -225,9 +260,17 @@
     own_pair = lax.ppermute(object_field, "col", pair)
     near_pair = lax.ppermute(near_block, "col", pair)
     far_pair = lax.ppermute(far_block, "col", pair)
-    blocks = (object_field, own_pair, near_block, near_pair, far_block, far_pair)
-    keep_probe, send_probe, keep_grad, send_grad, weight = run_slots(
-        place, offsets, counts, blocks, probe, patterns
+    probe_here, patterns_here, own, tables, weight = stage(
+        probe, patterns, object_field, jnp.asarray(host_tables(width))
+    )
+    blocks = (own, own_pair, near_block, near_pair, far_block, far_pair)
+    keep_probe, send_probe, keep_grad, send_grad = run_slots(
+        pltpu.with_memory_space_constraint(offsets, pltpu.HBM),
+        counts,
+        blocks,
+        probe_here,
+        patterns_here,
+        tables,
     )
 
     got_probe = lax.ppermute(send_probe, "col", pair)
@@ -246,8 +289,9 @@
         jnp.concatenate([other, mine], axis=0),
     )
     object_grad = strips[2] + near_strip + far_strip
-    object_field = object_field - object_rate * object_grad / weight[0, 0]
-    probe = probe - probe_rate * summed / tile_total
+    grouped = object_grad.reshape(2, -1, *weight.shape)
+    object_field = own - object_rate * (grouped / weight).reshape(object_field.shape)
+    probe = probe_here - probe_rate * summed / tile_total
     return (object_field, probe)
 
 
@@ -259,6 +303,7 @@
         P(("tilt", "row"), "col", None, None),
         P(("tilt", "row"), "col"),
     )
+
     return jax.shard_map(
         body,
         mesh=mesh,

time: 57.8 us -> 51.4 us (0.89)
  local copies, waits for them, and re-layouts: 3.26 us -> 0.75 us
  other arithmetic: 4.62 us -> 2.37 us
  waiting for transfers between devices: 22.3 us -> 21.7 us
    all_to_all x1, starting transfers between devices: 5.9 us -> 8.77 us  [body(): mine = lax.all_to_all(mine, 'row', 0, 0, tiled=True)]
    ppermute x1, starting transfers between devices: 5.82 us -> 3.03 us  [body(): near_block = lax.ppermute(object_field, 'row', near)]
    pallas_call x1, Pallas kernels: 5.83 us -> 3.86 us  [run_slots(): pl.pallas_call(slots_kernel, out_shape=(probe_half, probe_half, grad_rows...]
    ppermute x1, waiting for transfers between devices: 4.63 us -> 2.96 us  [body(): near_block = lax.ppermute(object_field, 'row', near)]
    pallas_call x0 -> x1, Pallas kernels: none -> 1.47 us  [stage(): pl.pallas_call(lambda *refs: stage_kernel(count, *refs), out_shape=tuple(...]
    unnamed x18 -> x0, local copies, waits for them, and re-layouts: 1.33 us -> none
    slice x1 -> x0, local copies, waits for them, and re-layouts: 1.19 us -> none  [body(): object_field = object_field - object_rate * object_grad / weight[0, 0]]
    add x1, other arithmetic: 1.71 us -> 0.73 us  [body(): mine = (keep_probe + got_probe).reshape(row_total, -1, width)]
  transfers between devices with their start and end apart: 12 -> 12, of which waited for: 4 -> 5; matrix products, arithmetic and copies ran while one was open for 7% -> 3% of each run, Pallas kernels for 0% -> 3%
where the time goes in v2:
time: 51.4 us; the launch traced here: 51.1 us
  waiting for transfers between devices  21.7 us (42%)
  starting transfers between devices  19.5 us (38%)
  Pallas kernels  5.33 us (10%)
  other arithmetic  2.37 us (5%)
  between operations  1.4 us (3%)
  local copies, waits for them, and re-layouts  0.75 us (1%)
    all_to_all x1, waiting for transfers between devices, body(): mine = lax.all_to_all(mine, 'row', 0, 0, tiled=True)  9.36 us
    all_to_all x1, starting transfers between devices, body(): mine = lax.all_to_all(mine, 'row', 0, 0, tiled=True)  8.77 us
    all_to_all x1, waiting for transfers between devices, body(): lax.all_to_all(mine, 'row', 0, 0, tiled=True).reshape(half, 2, width, width)  7.01 us
    pallas_call x1, Pallas kernels, run_slots(): pl.pallas_call(slots_kernel, out_shape=(probe_half, probe_half, grad_rows...  3.86 us
    all_to_all x1, starting transfers between devices, body(): lax.all_to_all(mine, 'row', 0, 0, tiled=True).reshape(half, 2, width, width)  3.59 us
    ppermute x1, starting transfers between devices, body(): near_block = lax.ppermute(object_field, 'row', near)  3.03 us
    ppermute x1, waiting for transfers between devices, body(): near_block = lax.ppermute(object_field, 'row', near)  2.96 us
    ppermute x1, starting transfers between devices, body(): near_strip = lax.ppermute(strips[0], 'row', near)  2.08 us
  transfers between devices with their start and end apart: 12, of which 5 were waited for; matrix products, arithmetic and copies ran while one was open for 3% of the time, Pallas kernels for 3%

profile of v2, /device:TPU:0, one launch (start us, length us, event | category | flops | bytes accessed | tf_op | source)
XLA Modules:
  0.0 51.1 jit_solution(8700420078129522526)
XLA Ops:
  0.6 3.0 %collective-permute-start.1 = (f32[2,128,128]{2,1,0:T(8,128)}, f32[2,128,128]{2,1,0:T(8,128)S(1)}, u32[]{:S(2)}, u32[]{:S(2)}) collective-permute-start(f32[2,128,128]{2,1,0:T(8,128)} %refs_2_.1), channel_id=1, source_target_pairs={{0,2},{2,0},{4,6},{6,4},{8,10},{10,8},{12,14},{14,12},{1,3},{3,1},... | collective-permute-start | bytes 393224 | tf_op jit(solution)/shard_map/ppermute | solution.py:258
  3.7 0.7 %collective-permute-start.3 = (f32[2,128,128]{2,1,0:T(8,128)}, f32[2,128,128]{2,1,0:T(8,128)S(1)}, u32[]{:S(2)}, u32[]{:S(2)}) collective-permute-start(f32[2,128,128]{2,1,0:T(8,128)} %refs_2_.1), channel_id=1, source_target_pairs={{2,4},{6,8},{10,12},{4,2},{8,6},{12,10},{3,5},{7,9},{11,13},{5,3},... | collective-permute-start | bytes 393224 | tf_op jit(solution)/shard_map/ppermute | solution.py:259
  4.3 0.1 collective-permute-start
  4.4 3.0 %collective-permute-done.1.near_ref = f32[2,128,128]{2,1,0:T(8,128)S(1)} collective-permute-done((f32[2,128,128]{2,1,0:T(8,128)}, f32[2,128,128]{2,1,0:T(8,128)S(1)}, u32[]{:S(2)}, u32[]{:S(2)}) %collective-permute-start.1) | collective-permute-done | bytes 131104 | tf_op jit(solution)/shard_map/ppermute | solution.py:258
  7.4 0.0 collective-permute-start.2
  7.4 0.0 collective-permute-done.3.far_ref
  7.4 0.5 collective-permute-start.4
  8.5 1.5 %stage.1 = (f32[4,2,128,128]{3,2,1,0:T(8,128)S(1)}, f32[1,1,2,128,128]{4,3,2,1,0:T(8,128)S(1)}, f32[2,128,128]{2,1,0:T(8,128)S(1)}, bf16[4,256,256]{2,1,0:T(8,128)(2,1)S(1)}, f32[8,128]{1,0:T(8,128)S(1)}) custom-call(f32[4,2,128,128]{3,2,1,0:T(8,128)} %refs_0_.1, f32[1,1,2,128,128]{4,3,2,1,0:T(8,128)} %refs_1_.1, f32[2,128,128]{2,1,0:T(8,128)} %refs_2_.1, ...), custom_call_target="tpu_custom_call" | custom-call | flops 1048576 | bytes 2621440 | tf_op jit(solution)/shard_map/stage/pallas_call | solution.py:56
  10.0 3.9 %slots.1 = (f32[2,2,128,128]{3,2,1,0:T(8,128)S(1)}, f32[2,2,128,128]{3,2,1,0:T(8,128)S(1)}, f32[3,2,128,128]{3,2,1,0:T(8,128)S(1)}, f32[3,2,128,128]{3,2,1,0:T(8,128)S(1)}) custom-call(s32[1,1,2,2]{3,2,1,0:T(2,128)} %offsets_hbm.1, s32[1,1]{1,0:T(1,128)S(6)} %copy.8.counts_ref, f32[2,128,128]{2,1,0:T(8,128)S(1)} %get-tuple-element.11.own_ref, ...), custom_call_target="tpu_custom_call" | custom-call | flops 1610612736 | bytes 2621440 | tf_op jit(solution)/shard_map/slots/pallas_call | solution.py:219
  13.9 0.1 collective-permute-start.8
  14.0 1.5 %collective-permute-done.8 = f32[2,2,128,128]{3,2,1,0:T(8,128)S(1)} collective-permute-done((f32[2,2,128,128]{3,2,1,0:T(8,128)S(1)}, f32[2,2,128,128]{3,2,1,0:T(8,128)S(1)}, u32[]{:S(2)}, u32[]{:S(2)}) %collective-permute-start.8) | collective-permute-done | bytes 262176 | tf_op jit(solution)/shard_map/ppermute | solution.py:276
  15.5 0.7 %add.15 = f32[2,2,128,128]{3,2,1,0:T(8,128)} add(f32[2,2,128,128]{3,2,1,0:T(8,128)S(1)} %get-tuple-element.18, f32[2,2,128,128]{3,2,1,0:T(8,128)S(1)} %collective-permute-done.8) | non-fusion elementwise | flops 65536 | bytes 786432 | tf_op jit(solution)/shard_map/add | solution.py:278
  16.2 8.8 %all-to-all-start = ((f32[8,64,128]{2,1,0:T(8,128)}), f32[8,64,128]{2,1,0:T(8,128)S(1)}, u32[]{:S(2)}, u32[]{:S(2)}) async-start(f32[8,64,128]{2,1,0:T(8,128)} %bitcast.4), calls=%async_computation | async-start | bytes 524288 | tf_op jit(solution)/shard_map/all_to_all | solution.py:279
  25.0 0.1 collective-permute-start.5
  25.1 9.4 %all-to-all-done = f32[8,64,128]{2,1,0:T(8,128)S(1)} async-done(((f32[8,64,128]{2,1,0:T(8,128)}), f32[8,64,128]{2,1,0:T(8,128)S(1)}, u32[]{:S(2)}, u32[]{:S(2)}) %all-to-all-start) | async-done | bytes 262176 | tf_op jit(solution)/shard_map/all_to_all | solution.py:279
  34.5 0.7 %broadcast_in_dim.2 = f32[8,64,128]{2,1,0:T(8,128)} broadcast(f32[64,128]{1,0:T(8,128)S(1)} %reduce_sum.9), dimensions={1,2} | broadcast | bytes 294912 | tf_op jit(solution)/shard_map/broadcast_in_dim | solution.py:280
  35.2 3.6 %all-to-all-start.1 = ((f32[8,64,128]{2,1,0:T(8,128)}), f32[8,64,128]{2,1,0:T(8,128)S(1)}, u32[]{:S(2)}, u32[]{:S(2)}) async-start(f32[8,64,128]{2,1,0:T(8,128)} %broadcast_in_dim.2), calls=%async_computation.1 | async-start | bytes 524288 | tf_op jit(solution)/shard_map/all_to_all | solution.py:284
  38.8 0.1 add.12
  38.9 2.1 %collective-permute-start.6 = (f32[2,128,128]{2,1,0:T(8,128)S(1)}, f32[2,128,128]{2,1,0:T(8,128)S(1)}, u32[]{:S(2)}, u32[]{:S(2)}) collective-permute-start(f32[2,128,128]{2,1,0:T(8,128)S(1)} %get-tuple-element.20), channel_id=1, source_target_pairs={{0,2},{2,0},{4,6},{6,4},{8,10},{10,8},{12,14},{14,12},{1,3},{3,1},... | collective-permute-start | bytes 393224 | tf_op jit(solution)/shard_map/ppermute | solution.py:282
  41.0 0.7 %collective-permute-start.7 = (f32[2,128,128]{2,1,0:T(8,128)S(1)}, f32[2,128,128]{2,1,0:T(8,128)S(1)}, u32[]{:S(2)}, u32[]{:S(2)}) collective-permute-start(f32[2,128,128]{2,1,0:T(8,128)S(1)} %get-tuple-element.21), channel_id=1, source_target_pairs={{2,4},{6,8},{10,12},{4,2},{8,6},{12,10},{3,5},{7,9},{11,13},{5,3},... | collective-permute-start | bytes 393224 | tf_op jit(solution)/shard_map/ppermute | solution.py:283
  41.6 7.0 %all-to-all-done.1 = f32[8,64,128]{2,1,0:T(8,128)S(1)} async-done(((f32[8,64,128]{2,1,0:T(8,128)}), f32[8,64,128]{2,1,0:T(8,128)S(1)}, u32[]{:S(2)}, u32[]{:S(2)}) %all-to-all-start.1) | async-done | bytes 262176 | tf_op jit(solution)/shard_map/all_to_all | solution.py:284
  48.7 0.7 %fusion.5 = f32[2,128,128]{2,1,0:T(8,128)} fusion(f32[2,128,128]{2,1,0:T(8,128)S(1)} %get-tuple-element.11.own_ref, f32[2,128,128]{2,1,0:T(8,128)S(1)} %collective-permute-done.7, f32[2,128,128]{2,1,0:T(8,128)S(1)} %collective-permute-done.6, f32[3,2,128,128]{3,2,1,0:T(8,128)S(1)} %add.12, f32[128,128]{1,0:T(8,128)S(1)} %broadcast_bitcast_fusion), kind=kLoop, calls=%fused_computation.9 | loop fusion | flops 131072 | bytes 720896 | tf_op jit(solution)/shard_map/sub | solution.py:293
  49.4 0.8 %collective-permute-done.9 = f32[2,2,128,128]{3,2,1,0:T(8,128)S(1)} collective-permute-done((f32[2,2,128,128]{3,2,1,0:T(8,128)S(1)}, f32[2,2,128,128]{3,2,1,0:T(8,128)S(1)}, u32[]{:S(2)}, u32[]{:S(2)}) %collective-permute-start.9) | collective-permute-done | bytes 262176 | tf_op jit(solution)/shard_map/ppermute | solution.py:285
  50.2 0.9 %fusion.1 = f32[4,2,128,128]{3,2,1,0:T(8,128)} fusion(f32[4,2,128,128]{3,2,1,0:T(8,128)S(1)} %get-tuple-element.12.probe_ref, f32[2,2,128,128]{3,2,1,0:T(8,128)S(1)} %collective-permute-done.9, f32[2,2,128,128]{3,2,1,0:T(8,128)S(1)} %bitcast.19, pred[]{:T(512)S(6)} %eq.3), kind=kLoop, calls=%fused_computation.2 | loop fusion | flops 655360 | bytes 1572865 | tf_op jit(solution)/shard_map/sub | solution.py:294
  (10 shorter events, 0.1 us)
Async XLA Ops:
  0.6 6.7 %collective-permute-start.1 = (f32[2,128,128]{2,1,0:T(8,128)}, f32[2,128,128]{2,1,0:T(8,128)S(1)}, u32[]{:S(2)}, u32[]{:S(2)}) collective-permute-start(f32[2,128,128]{2,1,0:T(8,128)} %refs_2_.1), channel_id=1, source_target_pairs={{0,2},{2,0},{4,6},{6,4},{8,10},{10,8},{12,14},{14,12},{1,3},{3,1},... | collective-permute-start | bytes 393224 | tf_op jit(solution)/shard_map/ppermute | solution.py:258
  3.7 3.7 %collective-permute-start.3 = (f32[2,128,128]{2,1,0:T(8,128)}, f32[2,128,128]{2,1,0:T(8,128)S(1)}, u32[]{:S(2)}, u32[]{:S(2)}) collective-permute-start(f32[2,128,128]{2,1,0:T(8,128)} %refs_2_.1), channel_id=1, source_target_pairs={{2,4},{6,8},{10,12},{4,2},{8,6},{12,10},{3,5},{7,9},{11,13},{5,3},... | collective-permute-start | bytes 393224 | tf_op jit(solution)/shard_map/ppermute | solution.py:259
  4.3 5.7 %collective-permute-start = (f32[2,128,128]{2,1,0:T(8,128)}, f32[2,128,128]{2,1,0:T(8,128)S(1)}, u32[]{:S(2)}, u32[]{:S(2)}) collective-permute-start(f32[2,128,128]{2,1,0:T(8,128)} %refs_2_.1), channel_id=1, source_target_pairs={{0,1},{1,0},{2,3},{3,2},{4,5},{5,4},{6,7},{7,6},{8,9},{9,8},{10,11... | collective-permute-start | bytes 393224 | tf_op jit(solution)/shard_map/ppermute | solution.py:260
  7.4 2.7 %collective-permute-start.2 = (f32[2,128,128]{2,1,0:T(8,128)S(1)}, f32[2,128,128]{2,1,0:T(8,128)S(1)}, u32[]{:S(2)}, u32[]{:S(2)}) collective-permute-start(f32[2,128,128]{2,1,0:T(8,128)S(1)} %collective-permute-done.1.near_ref), channel_id=1, source_target_pairs={{0,1},{1,0},{2,3},{3,2},{4,5},{5,4},{6,7},{7,6},{8,9},{9,8},{10,11... | collective-permute-start | bytes 393224 | tf_op jit(solution)/shard_map/ppermute | solution.py:261
  7.4 2.7 %collective-permute-start.4 = (f32[2,128,128]{2,1,0:T(8,128)S(1)}, f32[2,128,128]{2,1,0:T(8,128)S(1)}, u32[]{:S(2)}, u32[]{:S(2)}) collective-permute-start(f32[2,128,128]{2,1,0:T(8,128)S(1)} %collective-permute-done.3.far_ref), channel_id=1, source_target_pairs={{0,1},{1,0},{2,3},{3,2},{4,5},{5,4},{6,7},{7,6},{8,9},{9,8},{10,11... | collective-permute-start | bytes 393224 | tf_op jit(solution)/shard_map/ppermute | solution.py:262
  13.9 1.6 %collective-permute-start.8 = (f32[2,2,128,128]{3,2,1,0:T(8,128)S(1)}, f32[2,2,128,128]{3,2,1,0:T(8,128)S(1)}, u32[]{:S(2)}, u32[]{:S(2)}) collective-permute-start(f32[2,2,128,128]{3,2,1,0:T(8,128)S(1)} %get-tuple-element.19), channel_id=1, source_target_pairs={{0,1},{1,0},{2,3},{3,2},{4,5},{5,4},{6,7},{7,6},{8,9},{9,8},{10,11... | collective-permute-start | bytes 786440 | tf_op jit(solution)/shard_map/ppermute | solution.py:276
  16.2 18.2 %all-to-all-start = ((f32[8,64,128]{2,1,0:T(8,128)}), f32[8,64,128]{2,1,0:T(8,128)S(1)}, u32[]{:S(2)}, u32[]{:S(2)}) async-start(f32[8,64,128]{2,1,0:T(8,128)} %bitcast.4), calls=%async_computation | async-start | bytes 524288 | tf_op jit(solution)/shard_map/all_to_all | solution.py:279
  25.0 13.8 %collective-permute-start.5 = (f32[3,2,128,128]{3,2,1,0:T(8,128)S(1)}, f32[3,2,128,128]{3,2,1,0:T(8,128)S(1)}, u32[]{:S(2)}, u32[]{:S(2)}) collective-permute-start(f32[3,2,128,128]{3,2,1,0:T(8,128)S(1)} %get-tuple-element.16), channel_id=1, source_target_pairs={{0,1},{1,0},{2,3},{3,2},{4,5},{5,4},{6,7},{7,6},{8,9},{9,8},{10,11... | collective-permute-start | bytes 1179656 | tf_op jit(solution)/shard_map/ppermute | solution.py:277
  35.2 13.4 %all-to-all-start.1 = ((f32[8,64,128]{2,1,0:T(8,128)}), f32[8,64,128]{2,1,0:T(8,128)S(1)}, u32[]{:S(2)}, u32[]{:S(2)}) async-start(f32[8,64,128]{2,1,0:T(8,128)} %broadcast_in_dim.2), calls=%async_computation.1 | async-start | bytes 524288 | tf_op jit(solution)/shard_map/all_to_all | solution.py:284
  38.9 9.8 %collective-permute-start.6 = (f32[2,128,128]{2,1,0:T(8,128)S(1)}, f32[2,128,128]{2,1,0:T(8,128)S(1)}, u32[]{:S(2)}, u32[]{:S(2)}) collective-permute-start(f32[2,128,128]{2,1,0:T(8,128)S(1)} %get-tuple-element.20), channel_id=1, source_target_pairs={{0,2},{2,0},{4,6},{6,4},{8,10},{10,8},{12,14},{14,12},{1,3},{3,1},... | collective-permute-start | bytes 393224 | tf_op jit(solution)/shard_map/ppermute | solution.py:282
  41.0 7.7 %collective-permute-start.7 = (f32[2,128,128]{2,1,0:T(8,128)S(1)}, f32[2,128,128]{2,1,0:T(8,128)S(1)}, u32[]{:S(2)}, u32[]{:S(2)}) collective-permute-start(f32[2,128,128]{2,1,0:T(8,128)S(1)} %get-tuple-element.21), channel_id=1, source_target_pairs={{2,4},{6,8},{10,12},{4,2},{8,6},{12,10},{3,5},{7,9},{11,13},{5,3},... | collective-permute-start | bytes 393224 | tf_op jit(solution)/shard_map/ppermute | solution.py:283
  48.7 1.5 %collective-permute-start.9 = (f32[2,2,128,128]{3,2,1,0:T(8,128)S(1)}, f32[2,2,128,128]{3,2,1,0:T(8,128)S(1)}, u32[]{:S(2)}, u32[]{:S(2)}) collective-permute-start(f32[2,2,128,128]{3,2,1,0:T(8,128)S(1)} %bitcast.18), channel_id=1, source_target_pairs={{0,1},{1,0},{2,3},{3,2},{4,5},{5,4},{6,7},{7,6},{8,9},{9,8},{10,11... | collective-permute-start | bytes 786440 | tf_op jit(solution)/shard_map/ppermute | solution.py:285

commit v3 on v2

v3 whole, which is shorter than its diff:
```python
import jax
import jax.numpy as jnp
import numpy as np
from jax import lax
from jax.experimental import pallas as pl
from jax.experimental.pallas import tpu as pltpu
from jax.sharding import PartitionSpec as P


object_rate = 1.0
probe_rate = 1.0
epsilon = 1e-06


def split(value):
    high = value.astype(jnp.bfloat16)
    low = (value - high.astype(jnp.float32)).astype(jnp.bfloat16)
    return high, low


def host_tables(length):
    counter = np.arange(length)
    angle = -2.0 * np.pi / length * (counter[:, None] * counter[None, :] % length)
    cosine = (np.cos(angle) / np.sqrt(length)).astype(np.float32)
    sine = (np.sin(angle) / np.sqrt(length)).astype(np.float32)
    plain = np.block([[cosine, sine], [-sine, cosine]])
    conj = np.block([[cosine, -sine], [sine, cosine]])
    both = np.stack([plain, conj])
    high = both.astype(jnp.bfloat16)
    low = (both - high.astype(np.float32)).astype(jnp.bfloat16)
    return np.concatenate([high, low])


def stage_kernel(count, *refs):
    sources, targets, power_of = refs[:count], refs[count : 2 * count], refs[count]
    weight_ref, sems = refs[2 * count :]
    copies = [
        pltpu.make_async_copy(source, target, sems.at[index])
        for index, (source, target) in enumerate(zip(sources, targets))
    ]
    for copy in copies:
        copy.start()
    for copy in copies:
        copy.wait()
    power = jnp.zeros(power_of.shape[2:], jnp.float32)
    for k in range(power_of.shape[0]):
        power = power + power_of[k, 0] * power_of[k, 0] + power_of[k, 1] * power_of[k, 1]
    weight_ref[...] = jnp.full(weight_ref.shape, jnp.max(power) + epsilon, jnp.float32)


def stage(probe, *others):
    arrays = tuple(
        pltpu.with_memory_space_constraint(a, pltpu.HBM) for a in (probe,) + others
    )
    count = len(arrays)
    return pl.pallas_call(
        lambda *refs: stage_kernel(count, *refs),
        out_shape=tuple(jax.ShapeDtypeStruct(a.shape, a.dtype) for a in arrays)
        + (jax.ShapeDtypeStruct((8, probe.shape[-1]), jnp.float32),),
        in_specs=[pl.BlockSpec(memory_space=pltpu.HBM)] * count,
        out_specs=(pl.BlockSpec(memory_space=pltpu.VMEM),) * (count + 1),
        scratch_shapes=[pltpu.SemaphoreType.DMA((count,))],
        cost_estimate=pl.CostEstimate(
            flops=8 * probe.size,
            bytes_accessed=sum(2 * a.size * a.dtype.itemsize for a in arrays),
            transcendentals=0,
        ),
        compiler_params=pltpu.CompilerParams(vmem_limit_bytes=8 << 20),
        name="stage",
    )(*arrays)


def product(pieces, tables_ref, which, on_left):
    width = pieces[0][0].shape[0]
    inner, outer = (0, 1) if on_left else (1, 0)
    value = jnp.concatenate([jnp.concatenate(piece, axis=inner) for piece in pieces], axis=outer)
    high, low = split(value)
    if on_left:
        table = jnp.concatenate(
            [tables_ref[1 - which], tables_ref[3 - which], tables_ref[1 - which]], axis=1
        )
        out = jnp.dot(
            table, jnp.concatenate([high, high, low], axis=0), preferred_element_type=jnp.float32
        )
    else:
        table = jnp.concatenate(
            [tables_ref[which], tables_ref[which], tables_ref[2 + which]], axis=0
        )
        out = jnp.dot(
            jnp.concatenate([high, low, high], axis=1), table, preferred_element_type=jnp.float32
        )
    found = []
    for index in range(len(pieces)):
        part = lax.slice_in_dim(out, index * width, (index + 1) * width, axis=outer)
        found.append(
            (
                lax.slice_in_dim(part, 0, width, axis=inner),
                lax.slice_in_dim(part, width, 2 * width, axis=inner),
            )
        )
    return found


def columns_of(corner_x, width, core):
    column = corner_x // width
    shift = corner_x - column * width
    pair_column = 2 - 2 * core
    found = []
    for place in (column, column + 1):
        is_pair = (place == pair_column).astype(jnp.int32)
        valid = jnp.logical_or(place == 1, place == pair_column)
        found.append((is_pair, valid))
    lane = lax.broadcasted_iota(jnp.int32, (width, width), 1)
    in_left = lane >= shift
    return shift, in_left, found


def first_kernel(
    offsets_hbm,
    counts_ref,
    own_ref,
    own_pair_ref,
    near_ref,
    near_pair_ref,
    far_ref,
    far_pair_ref,
    probe_ref,
    patterns_ref,
    tables_ref,
    send_probe_ref,
    window_ref,
    kept_ref,
    grad_ref,
    offsets_ref,
    offsets_sem,
    frame,
):
    fetch = pltpu.make_async_copy(offsets_hbm, offsets_ref, offsets_sem)
    fetch.start()
    modes = probe_ref.shape[0]
    width = probe_ref.shape[-1]
    slots = patterns_ref.shape[2]
    half = modes // 2
    core = lax.axis_index("col")
    odd = lax.rem(lax.axis_index("row"), 2)
    near_at = pl.multiple_of((1 - odd) * (2 * width), width)
    far_at = pl.multiple_of(odd * (2 * width), width)
    for index, (own, near, far) in enumerate(
        ((own_ref, near_ref, far_ref), (own_pair_ref, near_pair_ref, far_pair_ref))
    ):
        frame[index, :, pl.ds(width, width), :] = own[...]
        frame[index, :, pl.ds(near_at, width), :] = near[...]
        frame[index, :, pl.ds(far_at, width), :] = far[...]
    fetch.wait()

    mine = core * half
    order = [half - mine + k for k in range(half)] + [mine + k for k in range(half)]
    windows = []
    for slot in range(slots):
        rows = pl.ds(offsets_ref[0, 0, slot, 0], width)
        shift, in_left, blocks = columns_of(offsets_ref[0, 0, slot, 1], width, core)
        back_shift = lax.rem(width - shift, width)
        (left, left_valid), (right, right_valid) = blocks
        valid = jnp.logical_or(
            jnp.logical_and(in_left, left_valid),
            jnp.logical_and(jnp.logical_not(in_left), right_valid),
        )
        window = []
        for part in range(2):
            both = jnp.where(in_left, frame[left, part, rows, :], frame[right, part, rows, :])
            value = pltpu.roll(jnp.where(valid, both, 0.0), back_shift, 1)
            window_ref[slot, part] = value
            window.append(value)
        windows.append(window)

    values = []
    for win_re, win_im in windows:
        exits = []
        for k in order:
            probe_re, probe_im = probe_ref[k, 0], probe_ref[k, 1]
            exits.append(
                (
                    probe_re * win_re - probe_im * win_im,
                    probe_re * win_im + probe_im * win_re,
                )
            )
        values.append(exits)
    values = [product(value, tables_ref, 0, False) for value in values]
    values = [product(value, tables_ref, 0, True) for value in values]
    backs = []
    for slot, far in enumerate(values):
        live = (slot < counts_ref[0, 0]).astype(jnp.float32)
        intensity = sum(re * re + im * im for re, im in far)
        misfit = (intensity - patterns_ref[0, 0, slot]) * live
        for k in range(half):
            for part in range(2):
                kept_ref[slot, k, part] = misfit * far[half + k][part]
        backs.append([(misfit * re, misfit * im) for re, im in far[:half]])
    backs = [product(back, tables_ref, 1, True) for back in backs]
    backs = [product(back, tables_ref, 1, False) for back in backs]
    grads = combine(backs, probe_ref, order[:half], windows, send_probe_ref)
    for slot in range(slots):
        for part in range(2):
            grad_ref[slot, part] = grads[slot][part]


def combine(backs, probe_ref, order, windows, term_ref):
    grads = [[jnp.zeros_like(part) for part in window] for window in windows]
    for index, k in enumerate(order):
        probe_re, probe_im = probe_ref[k, 0], probe_ref[k, 1]
        term_re, term_im = 0.0, 0.0
        for slot, (win_re, win_im) in enumerate(windows):
            back_re, back_im = backs[slot][index]
            grads[slot][0] += probe_re * back_re + probe_im * back_im
            grads[slot][1] += probe_re * back_im - probe_im * back_re
            term_re += win_re * back_re + win_im * back_im
            term_im += win_re * back_im - win_im * back_re
        term_ref[index, 0] = term_re
        term_ref[index, 1] = term_im
    return grads


def second_kernel(
    offsets_hbm,
    probe_ref,
    tables_ref,
    window_ref,
    kept_ref,
    part_ref,
    keep_probe_ref,
    grad_ref,
    offsets_ref,
    offsets_sem,
):
    fetch = pltpu.make_async_copy(offsets_hbm, offsets_ref, offsets_sem)
    fetch.start()
    modes = probe_ref.shape[0]
    width = probe_ref.shape[-1]
    slots = window_ref.shape[0]
    half = modes // 2
    core = lax.axis_index("col")
    order = [core * half + k for k in range(half)]
    grad_ref[...] = jnp.zeros_like(grad_ref)
    backs = [
        [(kept_ref[slot, k, 0], kept_ref[slot, k, 1]) for k in range(half)]
        for slot in range(slots)
    ]
    windows = [[window_ref[slot, 0], window_ref[slot, 1]] for slot in range(slots)]
    backs = [product(back, tables_ref, 1, True) for back in backs]
    backs = [product(back, tables_ref, 1, False) for back in backs]
    grads = combine(backs, probe_ref, order, windows, keep_probe_ref)
    fetch.wait()
    for slot in range(slots):
        rows = pl.ds(offsets_ref[0, 0, slot, 0], width)
        shift, in_left, blocks = columns_of(offsets_ref[0, 0, slot, 1], width, core)
        (left, left_valid), (right, right_valid) = blocks
        to_left = jnp.logical_and(in_left, left_valid)
        to_right = jnp.logical_and(jnp.logical_not(in_left), right_valid)
        for part in range(2):
            turned = pltpu.roll(grads[slot][part] + part_ref[slot, part], shift, 1)
            grad_ref[left, part, rows, :] += jnp.where(to_left, turned, 0.0)
            grad_ref[right, part, rows, :] += jnp.where(to_right, turned, 0.0)


def run_first(offsets, counts, blocks, probe, patterns, tables):
    modes, _, width, _ = probe.shape
    half = modes // 2
    slots = patterns.shape[2]
    vmem = pl.BlockSpec(memory_space=pltpu.VMEM)
    images = lambda *lead: jax.ShapeDtypeStruct((*lead, 2, width, width), jnp.float32)
    return pl.pallas_call(
        first_kernel,
        out_shape=(images(half), images(slots), images(slots, half), images(slots)),
        in_specs=[
            pl.BlockSpec(memory_space=pltpu.HBM),
            pl.BlockSpec(memory_space=pltpu.SMEM),
        ]
        + [vmem] * 9,
        out_specs=(vmem,) * 4,
        scratch_shapes=[
            pltpu.SMEM(offsets.shape, offsets.dtype),
            pltpu.SemaphoreType.DMA,
            pltpu.VMEM((2, 2, 3 * width, width), jnp.float32),
        ],
        cost_estimate=pl.CostEstimate(
            flops=slots * modes * 3 * 3 * 8 * width**3,
            bytes_accessed=40 * width * width * 4,
            transcendentals=0,
        ),
        compiler_params=pltpu.CompilerParams(vmem_limit_bytes=16 << 20),
        name="first",
    )(offsets, counts, *blocks, probe, patterns, tables)


def run_second(offsets, probe, tables, window, kept, part):
    modes, _, width, _ = probe.shape
    half = modes // 2
    slots = window.shape[0]
    vmem = pl.BlockSpec(memory_space=pltpu.VMEM)
    return pl.pallas_call(
        second_kernel,
        out_shape=(
            jax.ShapeDtypeStruct((half, 2, width, width), jnp.float32),
            jax.ShapeDtypeStruct((2, 2, 3 * width, width), jnp.float32),
        ),
        in_specs=[pl.BlockSpec(memory_space=pltpu.HBM)] + [vmem] * 5,
        out_specs=(vmem,) * 2,
        scratch_shapes=[
            pltpu.SMEM(offsets.shape, offsets.dtype),
            pltpu.SemaphoreType.DMA,
        ],
        cost_estimate=pl.CostEstimate(
            flops=slots * modes * 3 * 8 * width**3,
            bytes_accessed=30 * width * width * 4,
            transcendentals=0,
        ),
        compiler_params=pltpu.CompilerParams(vmem_limit_bytes=16 << 20),
        name="second",
    )(offsets, probe, tables, window, kept, part)


def member_order(count):
    pairs = count // 2
    middle = (pairs - 1) // 2
    order = []
    for step in range(pairs):
        near = (step + 1) // 2
        at = middle + near if step % 2 else middle - near
        order.extend((2 * at + 1, 2 * at))
    return order


def body(object_field, probe, patterns, offsets, counts):
    row_total = lax.axis_size("row")
    tile_total = row_total * lax.axis_size("col")
    modes, _, width, _ = probe.shape
    half = modes // 2
    core = lax.axis_index("col")

    pair = [(0, 1), (1, 0)]
    near = [(i, i ^ 1) for i in range(row_total)]
    far = [(i, i + 1) for i in range(1, row_total - 1, 2)]
    far = far + [(target, source) for source, target in far]

    near_block = lax.ppermute(object_field, "row", near)
    far_block = lax.ppermute(object_field, "row", far)
    own_pair = lax.ppermute(object_field, "col", pair)
    near_pair = lax.ppermute(near_block, "col", pair)
    far_pair = lax.ppermute(far_block, "col", pair)
    probe_here, patterns_here, own, tables, weight = stage(
        probe, patterns, object_field, jnp.asarray(host_tables(width))
    )
    blocks = (own, own_pair, near_block, near_pair, far_block, far_pair)
    offsets = pltpu.with_memory_space_constraint(offsets, pltpu.HBM)
    send_probe, window, kept, part = run_first(
        offsets, counts, blocks, probe_here, patterns_here, tables
    )
    got_probe = lax.ppermute(send_probe, "col", pair)
    keep_probe, grads = run_second(offsets, probe_here, tables, window, kept, part)
    got_grad = lax.ppermute(grads[1], "col", pair)

    members = [member_order(row_total)]
    mine = (keep_probe + got_probe).reshape(row_total, -1, width)
    mine = lax.all_to_all(mine, "row", 0, 0, tiled=True, axis_index_groups=members)
    mine = jnp.broadcast_to(jnp.sum(mine, axis=0, keepdims=True), mine.shape)
    strips = grads[0] + got_grad
    odd = lax.axis_index("row") % 2
    near_strip = lax.dynamic_slice_in_dim(strips, (1 - odd) * (2 * width), width, axis=1)
    far_strip = lax.dynamic_slice_in_dim(strips, odd * (2 * width), width, axis=1)
    near_strip = lax.ppermute(near_strip, "row", near)
    far_strip = lax.ppermute(far_strip, "row", far)
    mine = lax.all_to_all(mine, "row", 0, 0, tiled=True, axis_index_groups=members)
    mine = mine.reshape(half, 2, width, width)
    other = lax.ppermute(mine, "col", pair)
    summed = jnp.where(
        core == 0,
        jnp.concatenate([mine, other], axis=0),
        jnp.concatenate([other, mine], axis=0),
    )
    object_grad = strips[:, width : 2 * width] + near_strip + far_strip
    grouped = object_grad.reshape(2, -1, *weight.shape)
    object_field = own - object_rate * (grouped / weight).reshape(object_field.shape)
    probe = probe_here - probe_rate * summed / tile_total
    return (object_field, probe)


def solution(mesh):
    placed = (
        P(None, ("tilt", "row"), "col"),
        P("tilt", None, None, None),
        P(("tilt", "row"), "col", None, None, None),
        P(("tilt", "row"), "col", None, None),
        P(("tilt", "row"), "col"),
    )

    return jax.shard_map(
        body,
        mesh=mesh,
        in_specs=placed,
        out_specs=(P(None, ("tilt", "row"), "col"), P("tilt", None, None, None)),
        check_vma=False,
    )
```

time: 51.4 us -> 47.3 us (0.920)
  the two profiles are of different devices: /device:TPU:0 before, /device:TPU:2 now
where the time goes in v3:
time: 47.3 us; the launch traced here: 46.9 us
  starting transfers between devices  19.4 us (41%)
  waiting for transfers between devices  17.9 us (38%)
  Pallas kernels  5.03 us (11%)
  other arithmetic  2.37 us (5%)
  between operations  1.4 us (3%)
  local copies, waits for them, and re-layouts  0.78 us (2%)
    all_to_all x2, waiting for transfers between devices, body(): lax.all_to_all(mine, 'row', 0, 0, tiled=True, axis_index_groups=members)  12.7 us
    all_to_all x2, starting transfers between devices, body(): lax.all_to_all(mine, 'row', 0, 0, tiled=True, axis_index_groups=members)  10.1 us
    ppermute x1, starting transfers between devices, body(): far_block = lax.ppermute(object_field, 'row', far)  4.92 us
    ppermute x1, waiting for transfers between devices, body(): far_block = lax.ppermute(object_field, 'row', far)  2.83 us
    pallas_call x1, Pallas kernels, run_first(): pl.pallas_call(first_kernel, out_shape=(images(half), images(slots), imag...  2.59 us
    ppermute x1, starting transfers between devices, body(): far_strip = lax.ppermute(far_strip, 'row', far)  2.01 us
    ppermute x1, waiting for transfers between devices, body(): far_strip = lax.ppermute(far_strip, 'row', far)  1.58 us
    ppermute x1, starting transfers between devices, body(): near_strip = lax.ppermute(near_strip, 'row', near)  1.53 us
  transfers between devices with their start and end apart: 12, of which 7 were waited for; matrix products, arithmetic and copies ran while one was open for 3% of the time, Pallas kernels for 5%

profile of v3, /device:TPU:2, one launch (start us, length us, event | category | flops | bytes accessed | tf_op | source)
XLA Modules:
  0.0 46.9 jit_solution(4770716314767511452)
XLA Ops:
  0.6 0.1 collective-permute-start.1
  0.7 4.9 %collective-permute-start.3 = (f32[2,128,128]{2,1,0:T(8,128)}, f32[2,128,128]{2,1,0:T(8,128)S(1)}, u32[]{:S(2)}, u32[]{:S(2)}) collective-permute-start(f32[2,128,128]{2,1,0:T(8,128)} %refs_2_.1), channel_id=1, source_target_pairs={{2,4},{6,8},{10,12},{4,2},{8,6},{12,10},{3,5},{7,9},{11,13},{5,3},... | collective-permute-start | bytes 393224 | tf_op jit(solution)/shard_map/ppermute | solution.py:346
  5.6 0.1 collective-permute-start
  5.7 0.4 collective-permute-done.1.near_ref
  6.1 0.1 collective-permute-start.2
  6.2 2.8 %collective-permute-done.3.far_ref = f32[2,128,128]{2,1,0:T(8,128)S(1)} collective-permute-done((f32[2,128,128]{2,1,0:T(8,128)}, f32[2,128,128]{2,1,0:T(8,128)S(1)}, u32[]{:S(2)}, u32[]{:S(2)}) %collective-permute-start.3) | collective-permute-done | bytes 131104 | tf_op jit(solution)/shard_map/ppermute | solution.py:346
  9.7 1.5 %stage.1 = (f32[4,2,128,128]{3,2,1,0:T(8,128)S(1)}, f32[1,1,2,128,128]{4,3,2,1,0:T(8,128)S(1)}, f32[2,128,128]{2,1,0:T(8,128)S(1)}, bf16[4,256,256]{2,1,0:T(8,128)(2,1)S(1)}, f32[8,128]{1,0:T(8,128)S(1)}) custom-call(f32[4,2,128,128]{3,2,1,0:T(8,128)} %refs_0_.1, f32[1,1,2,128,128]{4,3,2,1,0:T(8,128)} %refs_1_.1, f32[2,128,128]{2,1,0:T(8,128)} %refs_2_.1, ...), custom_call_target="tpu_custom_call" | custom-call | flops 1048576 | bytes 2621440 | tf_op jit(solution)/shard_map/stage/pallas_call | solution.py:56
  11.2 2.6 %first.1 = (f32[2,2,128,128]{3,2,1,0:T(8,128)S(1)}, f32[2,2,128,128]{3,2,1,0:T(8,128)S(1)}, f32[2,2,2,128,128]{4,3,2,1,0:T(8,128)S(1)}, f32[2,2,128,128]{3,2,1,0:T(8,128)S(1)}) custom-call(s32[1,1,2,2]{3,2,1,0:T(2,128)} %offsets_hbm.3, s32[1,1]{1,0:T(1,128)S(6)} %copy.8.counts_ref, f32[2,128,128]{2,1,0:T(8,128)S(1)} %get-tuple-element.13.own_ref, ...), custom_call_target="tpu_custom_call" | custom-call | flops 1207959552 | bytes 2621440 | tf_op jit(solution)/shard_map/first/pallas_call | solution.py:271
  13.8 0.6 %collective-permute-start.8 = (f32[2,2,128,128]{3,2,1,0:T(8,128)S(1)}, f32[2,2,128,128]{3,2,1,0:T(8,128)S(1)}, u32[]{:S(2)}, u32[]{:S(2)}) collective-permute-start(f32[2,2,128,128]{3,2,1,0:T(8,128)S(1)} %get-tuple-element.23), channel_id=1, source_target_pairs={{0,1},{1,0},{2,3},{3,2},{4,5},{5,4},{6,7},{7,6},{8,9},{9,8},{10,11... | collective-permute-start | bytes 786440 | tf_op jit(solution)/shard_map/ppermute | solution.py:358
  14.4 1.0 %second.1 = (f32[2,2,128,128]{3,2,1,0:T(8,128)S(1)}, f32[2,2,384,128]{3,2,1,0:T(8,128)S(1)}) custom-call(s32[1,1,2,2]{3,2,1,0:T(2,128)} %offsets_hbm.3, f32[4,2,128,128]{3,2,1,0:T(8,128)S(1)} %get-tuple-element.14.probe_ref, bf16[4,256,256]{2,1,0:T(8,128)(2,1)S(1)} %get-tuple-element.15.tables_ref, f32[2,2,128,128]{3,2,1,0:T(8,128)S(1)} %get-tuple-element.17.window_ref, ...), custom_call_target="tpu_custom_call" | custom-call | flops 402653184 | bytes 1966080 | tf_op jit(solution)/shard_map/second/pallas_call | solution.py:300
  15.4 0.2 collective-permute-done.8
  15.6 0.7 %add.28 = f32[2,2,128,128]{3,2,1,0:T(8,128)} add(f32[2,2,128,128]{3,2,1,0:T(8,128)S(1)} %get-tuple-element.22, f32[2,2,128,128]{3,2,1,0:T(8,128)S(1)} %collective-permute-done.8) | non-fusion elementwise | flops 65536 | bytes 786432 | tf_op jit(solution)/shard_map/add | solution.py:363
  16.3 6.5 %all-to-all-start = ((f32[8,64,128]{2,1,0:T(8,128)}), f32[8,64,128]{2,1,0:T(8,128)S(1)}, u32[]{:S(2)}, u32[]{:S(2)}) async-start(f32[8,64,128]{2,1,0:T(8,128)} %bitcast.3), calls=%async_computation | async-start | bytes 524288 | tf_op jit(solution)/shard_map/all_to_all | solution.py:364
  22.8 0.1 collective-permute-start.5
  22.9 8.7 %all-to-all-done = f32[8,64,128]{2,1,0:T(8,128)S(1)} async-done(((f32[8,64,128]{2,1,0:T(8,128)}), f32[8,64,128]{2,1,0:T(8,128)S(1)}, u32[]{:S(2)}, u32[]{:S(2)}) %all-to-all-start) | async-done | bytes 262176 | tf_op jit(solution)/shard_map/all_to_all | solution.py:364
  31.7 0.7 %broadcast_in_dim.2 = f32[8,64,128]{2,1,0:T(8,128)} broadcast(f32[64,128]{1,0:T(8,128)S(1)} %reduce_sum.9), dimensions={1,2} | broadcast | bytes 294912 | tf_op jit(solution)/shard_map/broadcast_in_dim | solution.py:365
  32.4 3.5 %all-to-all-start.1 = ((f32[8,64,128]{2,1,0:T(8,128)}), f32[8,64,128]{2,1,0:T(8,128)S(1)}, u32[]{:S(2)}, u32[]{:S(2)}) async-start(f32[8,64,128]{2,1,0:T(8,128)} %broadcast_in_dim.2), calls=%async_computation.1 | async-start | bytes 524288 | tf_op jit(solution)/shard_map/all_to_all | solution.py:372
  36.0 1.5 %collective-permute-start.6 = (f32[2,128,128]{2,1,0:T(8,128)S(1)}, f32[2,128,128]{2,1,0:T(8,128)S(1)}, u32[]{:S(2)}, u32[]{:S(2)}) collective-permute-start(f32[2,128,128]{2,1,0:T(8,128)S(1)} %get-tuple-element.24), channel_id=1, source_target_pairs={{0,2},{2,0},{4,6},{6,4},{8,10},{10,8},{12,14},{14,12},{1,3},{3,1},... | collective-permute-start | bytes 393224 | tf_op jit(solution)/shard_map/ppermute | solution.py:370
  37.6 2.0 %collective-permute-start.7 = (f32[2,128,128]{2,1,0:T(8,128)S(1)}, f32[2,128,128]{2,1,0:T(8,128)S(1)}, u32[]{:S(2)}, u32[]{:S(2)}) collective-permute-start(f32[2,128,128]{2,1,0:T(8,128)S(1)} %get-tuple-element.25), channel_id=1, source_target_pairs={{2,4},{6,8},{10,12},{4,2},{8,6},{12,10},{3,5},{7,9},{11,13},{5,3},... | collective-permute-start | bytes 393224 | tf_op jit(solution)/shard_map/ppermute | solution.py:371
  39.6 3.9 %all-to-all-done.1 = f32[8,64,128]{2,1,0:T(8,128)S(1)} async-done(((f32[8,64,128]{2,1,0:T(8,128)}), f32[8,64,128]{2,1,0:T(8,128)S(1)}, u32[]{:S(2)}, u32[]{:S(2)}) %all-to-all-start.1) | async-done | bytes 262176 | tf_op jit(solution)/shard_map/all_to_all | solution.py:372
  43.5 0.2 collective-permute-done.6
  43.7 1.6 %collective-permute-done.7 = f32[2,128,128]{2,1,0:T(8,128)S(1)} collective-permute-done((f32[2,128,128]{2,1,0:T(8,128)S(1)}, f32[2,128,128]{2,1,0:T(8,128)S(1)}, u32[]{:S(2)}, u32[]{:S(2)}) %collective-permute-start.7) | collective-permute-done | bytes 131104 | tf_op jit(solution)/shard_map/ppermute | solution.py:371
  45.3 0.7 %fusion.4 = f32[2,128,128]{2,1,0:T(8,128)} fusion(f32[2,128,128]{2,1,0:T(8,128)S(1)} %get-tuple-element.13.own_ref, f32[2,128,128]{2,1,0:T(8,128)S(1)} %collective-permute-done.7, f32[2,128,128]{2,1,0:T(8,128)S(1)} %collective-permute-done.6, f32[2,384,128]{2,1,0:T(8,128)S(1)} %bitcast_add_fusion, f32[128,128]{1,0:T(8,128)S(1)} %broadcast_bitcast_fusion), kind=kLoop, calls=%fused_computation.8 | loop fusion | flops 131072 | bytes 720896 | tf_op jit(solution)/shard_map/sub | solution.py:382
  46.0 0.9 %fusion.1 = f32[4,2,128,128]{3,2,1,0:T(8,128)} fusion(f32[4,2,128,128]{3,2,1,0:T(8,128)S(1)} %get-tuple-element.14.probe_ref, f32[2,2,128,128]{3,2,1,0:T(8,128)S(1)} %collective-permute-done.9, f32[2,2,128,128]{3,2,1,0:T(8,128)S(1)} %bitcast.9, pred[]{:T(512)S(6)} %eq.5), kind=kLoop, calls=%fused_computation.2 | loop fusion | flops 655360 | bytes 1572865 | tf_op jit(solution)/shard_map/sub | solution.py:383
  (12 shorter events, 0.2 us)
Async XLA Ops:
  0.6 5.5 %collective-permute-start.1 = (f32[2,128,128]{2,1,0:T(8,128)}, f32[2,128,128]{2,1,0:T(8,128)S(1)}, u32[]{:S(2)}, u32[]{:S(2)}) collective-permute-start(f32[2,128,128]{2,1,0:T(8,128)} %refs_2_.1), channel_id=1, source_target_pairs={{0,2},{2,0},{4,6},{6,4},{8,10},{10,8},{12,14},{14,12},{1,3},{3,1},... | collective-permute-start | bytes 393224 | tf_op jit(solution)/shard_map/ppermute | solution.py:345
  0.7 8.3 %collective-permute-start.3 = (f32[2,128,128]{2,1,0:T(8,128)}, f32[2,128,128]{2,1,0:T(8,128)S(1)}, u32[]{:S(2)}, u32[]{:S(2)}) collective-permute-start(f32[2,128,128]{2,1,0:T(8,128)} %refs_2_.1), channel_id=1, source_target_pairs={{2,4},{6,8},{10,12},{4,2},{8,6},{12,10},{3,5},{7,9},{11,13},{5,3},... | collective-permute-start | bytes 393224 | tf_op jit(solution)/shard_map/ppermute | solution.py:346
  5.6 5.5 %collective-permute-start = (f32[2,128,128]{2,1,0:T(8,128)}, f32[2,128,128]{2,1,0:T(8,128)S(1)}, u32[]{:S(2)}, u32[]{:S(2)}) collective-permute-start(f32[2,128,128]{2,1,0:T(8,128)} %refs_2_.1), channel_id=1, source_target_pairs={{0,1},{1,0},{2,3},{3,2},{4,5},{5,4},{6,7},{7,6},{8,9},{9,8},{10,11... | collective-permute-start | bytes 393224 | tf_op jit(solution)/shard_map/ppermute | solution.py:347
  6.1 5.1 %collective-permute-start.2 = (f32[2,128,128]{2,1,0:T(8,128)S(1)}, f32[2,128,128]{2,1,0:T(8,128)S(1)}, u32[]{:S(2)}, u32[]{:S(2)}) collective-permute-start(f32[2,128,128]{2,1,0:T(8,128)S(1)} %collective-permute-done.1.near_ref), channel_id=1, source_target_pairs={{0,1},{1,0},{2,3},{3,2},{4,5},{5,4},{6,7},{7,6},{8,9},{9,8},{10,11... | collective-permute-start | bytes 393224 | tf_op jit(solution)/shard_map/ppermute | solution.py:348
  9.1 2.2 %collective-permute-start.4 = (f32[2,128,128]{2,1,0:T(8,128)S(1)}, f32[2,128,128]{2,1,0:T(8,128)S(1)}, u32[]{:S(2)}, u32[]{:S(2)}) collective-permute-start(f32[2,128,128]{2,1,0:T(8,128)S(1)} %collective-permute-done.3.far_ref), channel_id=1, source_target_pairs={{0,1},{1,0},{2,3},{3,2},{4,5},{5,4},{6,7},{7,6},{8,9},{9,8},{10,11... | collective-permute-start | bytes 393224 | tf_op jit(solution)/shard_map/ppermute | solution.py:349
  13.8 1.7 %collective-permute-start.8 = (f32[2,2,128,128]{3,2,1,0:T(8,128)S(1)}, f32[2,2,128,128]{3,2,1,0:T(8,128)S(1)}, u32[]{:S(2)}, u32[]{:S(2)}) collective-permute-start(f32[2,2,128,128]{3,2,1,0:T(8,128)S(1)} %get-tuple-element.23), channel_id=1, source_target_pairs={{0,1},{1,0},{2,3},{3,2},{4,5},{5,4},{6,7},{7,6},{8,9},{9,8},{10,11... | collective-permute-start | bytes 786440 | tf_op jit(solution)/shard_map/ppermute | solution.py:358
  16.3 15.4 %all-to-all-start = ((f32[8,64,128]{2,1,0:T(8,128)}), f32[8,64,128]{2,1,0:T(8,128)S(1)}, u32[]{:S(2)}, u32[]{:S(2)}) async-start(f32[8,64,128]{2,1,0:T(8,128)} %bitcast.3), calls=%async_computation | async-start | bytes 524288 | tf_op jit(solution)/shard_map/all_to_all | solution.py:364
  22.8 13.1 %collective-permute-start.5 = (f32[2,384,128]{2,1,0:T(8,128)S(1)}, f32[2,384,128]{2,1,0:T(8,128)S(1)}, u32[]{:S(2)}, u32[]{:S(2)}) collective-permute-start(f32[2,384,128]{2,1,0:T(8,128)S(1)} %slice_bitcast_fusion), channel_id=1, source_target_pairs={{0,1},{1,0},{2,3},{3,2},{4,5},{5,4},{6,7},{7,6},{8,9},{9,8},{10,11... | collective-permute-start | bytes 1179656 | tf_op jit(solution)/shard_map/ppermute | solution.py:360
  32.4 11.1 %all-to-all-start.1 = ((f32[8,64,128]{2,1,0:T(8,128)}), f32[8,64,128]{2,1,0:T(8,128)S(1)}, u32[]{:S(2)}, u32[]{:S(2)}) async-start(f32[8,64,128]{2,1,0:T(8,128)} %broadcast_in_dim.2), calls=%async_computation.1 | async-start | bytes 524288 | tf_op jit(solution)/shard_map/all_to_all | solution.py:372
  36.0 7.7 %collective-permute-start.6 = (f32[2,128,128]{2,1,0:T(8,128)S(1)}, f32[2,128,128]{2,1,0:T(8,128)S(1)}, u32[]{:S(2)}, u32[]{:S(2)}) collective-permute-start(f32[2,128,128]{2,1,0:T(8,128)S(1)} %get-tuple-element.24), channel_id=1, source_target_pairs={{0,2},{2,0},{4,6},{6,4},{8,10},{10,8},{12,14},{14,12},{1,3},{3,1},... | collective-permute-start | bytes 393224 | tf_op jit(solution)/shard_map/ppermute | solution.py:370
  37.6 7.7 %collective-permute-start.7 = (f32[2,128,128]{2,1,0:T(8,128)S(1)}, f32[2,128,128]{2,1,0:T(8,128)S(1)}, u32[]{:S(2)}, u32[]{:S(2)}) collective-permute-start(f32[2,128,128]{2,1,0:T(8,128)S(1)} %get-tuple-element.25), channel_id=1, source_target_pairs={{2,4},{6,8},{10,12},{4,2},{8,6},{12,10},{3,5},{7,9},{11,13},{5,3},... | collective-permute-start | bytes 393224 | tf_op jit(solution)/shard_map/ppermute | solution.py:371
  43.5 2.5 %collective-permute-start.9 = (f32[2,2,128,128]{3,2,1,0:T(8,128)S(1)}, f32[2,2,128,128]{3,2,1,0:T(8,128)S(1)}, u32[]{:S(2)}, u32[]{:S(2)}) collective-permute-start(f32[2,2,128,128]{3,2,1,0:T(8,128)S(1)} %bitcast.8), channel_id=1, source_target_pairs={{0,1},{1,0},{2,3},{3,2},{4,5},{5,4},{6,7},{7,6},{8,9},{9,8},{10,11... | collective-permute-start | bytes 786440 | tf_op jit(solution)/shard_map/ppermute | solution.py:374

commit v4 on v3

--- a/solution.py
+++ b/solution.py
@@ -1,3 +1,5 @@
+import functools
+
 import jax
 import jax.numpy as jnp
 import numpy as np
@@ -319,6 +321,53 @@
     )(offsets, probe, tables, window, kept, part)
 
 
+def total_kernel(parts_ref, out_ref):
+    total = parts_ref[0]
+    for index in range(1, parts_ref.shape[0]):
+        total = total + parts_ref[index]
+    for index in range(parts_ref.shape[0]):
+        out_ref[index] = total
+
+
+def strips_kernel(grads_ref, got_ref, middle_ref, near_ref, far_ref):
+    width = got_ref.shape[-1]
+    odd = lax.rem(lax.axis_index("row"), 2)
+    near_at = pl.multiple_of((1 - odd) * (2 * width), width)
+    far_at = pl.multiple_of(odd * (2 * width), width)
+    for out_ref, place in ((middle_ref, width), (near_ref, near_at), (far_ref, far_at)):
+        rows = pl.ds(place, width)
+        out_ref[...] = grads_ref[0, :, rows, :] + got_ref[:, rows, :]
+
+
+def object_kernel(own_ref, middle_ref, near_ref, far_ref, weight_ref, out_ref):
+    weight = weight_ref[...]
+    grad = (middle_ref[...] + near_ref[...] + far_ref[...]).reshape(-1, *weight.shape)
+    out = own_ref[...].reshape(grad.shape) - object_rate * (grad / weight)
+    out_ref[...] = out.reshape(own_ref.shape)
+
+
+def probe_kernel(tile_total, probe_ref, mine_ref, other_ref, out_ref):
+    half = mine_ref.shape[0]
+    core = lax.axis_index("col")
+    for part_ref, which in ((mine_ref, core), (other_ref, 1 - core)):
+        modes = pl.ds(which * half, half)
+        out_ref[modes] = probe_ref[modes] - probe_rate * part_ref[...] / tile_total
+
+
+def in_vmem(kernel, shapes, *operands):
+    vmem = pl.BlockSpec(memory_space=pltpu.VMEM)
+    out = tuple(jax.ShapeDtypeStruct(shape, jnp.float32) for shape in shapes)
+    size = sum(a.size for a in out + operands)
+    return pl.pallas_call(
+        kernel,
+        out_shape=out if len(out) > 1 else out[0],
+        in_specs=[vmem] * len(operands),
+        out_specs=(vmem,) * len(out) if len(out) > 1 else vmem,
+        cost_estimate=pl.CostEstimate(flops=size, bytes_accessed=4 * size, transcendentals=0),
+        compiler_params=pltpu.CompilerParams(vmem_limit_bytes=8 << 20),
+    )(*operands)
+
+
 def member_order(count):
     pairs = count // 2
     middle = (pairs - 1) // 2
@@ -335,7 +384,6 @@
     tile_total = row_total * lax.axis_size("col")
     modes, _, width, _ = probe.shape
     half = modes // 2
-    core = lax.axis_index("col")
 
     pair = [(0, 1), (1, 0)]
     near = [(i, i ^ 1) for i in range(row_total)]
@@ -362,25 +410,22 @@
     members = [member_order(row_total)]
     mine = (keep_probe + got_probe).reshape(row_total, -1, width)
     mine = lax.all_to_all(mine, "row", 0, 0, tiled=True, axis_index_groups=members)
-    mine = jnp.broadcast_to(jnp.sum(mine, axis=0, keepdims=True), mine.shape)
-    strips = grads[0] + got_grad
-    odd = lax.axis_index("row") % 2
-    near_strip = lax.dynamic_slice_in_dim(strips, (1 - odd) * (2 * width), width, axis=1)
-    far_strip = lax.dynamic_slice_in_dim(strips, odd * (2 * width), width, axis=1)
+    mine = in_vmem(total_kernel, [mine.shape], mine)
+    block = own.shape
+    middle, near_strip, far_strip = in_vmem(
+        strips_kernel, [block, block, block], grads, got_grad
+    )
     near_strip = lax.ppermute(near_strip, "row", near)
     far_strip = lax.ppermute(far_strip, "row", far)
     mine = lax.all_to_all(mine, "row", 0, 0, tiled=True, axis_index_groups=members)
     mine = mine.reshape(half, 2, width, width)
     other = lax.ppermute(mine, "col", pair)
-    summed = jnp.where(
-        core == 0,
-        jnp.concatenate([mine, other], axis=0),
-        jnp.concatenate([other, mine], axis=0),
-    )
-    object_grad = strips[:, width : 2 * width] + near_strip + far_strip
-    grouped = object_grad.reshape(2, -1, *weight.shape)
-    object_field = own - object_rate * (grouped / weight).reshape(object_field.shape)
-    probe = probe_here - probe_rate * summed / tile_total
+    object_field = in_vmem(
+        object_kernel, [block], own, middle, near_strip, far_strip, weight
+    )
+    probe = in_vmem(
+        functools.partial(probe_kernel, tile_total), [probe.shape], probe_here, mine, other
+    )
     return (object_field, probe)
 
 

time: 47.3 us -> 54.3 us (1.15)
  the two profiles are of different devices: /device:TPU:2 before, /device:TPU:8 now
where the time goes in v4:
time: 54.3 us; the launch traced here: 54 us
  waiting for transfers between devices  17 us (31%)
  starting transfers between devices  16.5 us (30%)
  blocking collectives  11.7 us (22%)
  Pallas kernels  7.35 us (14%)
  between operations  1.37 us (3%)
    all_to_all x1, blocking collectives, body(): lax.all_to_all(mine, 'row', 0, 0, tiled=True, axis_index_groups=members)  11.7 us
    all_to_all x1, starting transfers between devices, body(): lax.all_to_all(mine, 'row', 0, 0, tiled=True, axis_index_groups=members)  5.83 us
    all_to_all x1, waiting for transfers between devices, body(): lax.all_to_all(mine, 'row', 0, 0, tiled=True, axis_index_groups=members)  5.28 us
    ppermute x1, waiting for transfers between devices, body(): far_strip = lax.ppermute(far_strip, 'row', far)  4.24 us
    ppermute x1, waiting for transfers between devices, body(): far_block = lax.ppermute(object_field, 'row', far)  3.31 us
    ppermute x1, starting transfers between devices, body(): far_block = lax.ppermute(object_field, 'row', far)  3.28 us
    ppermute x1, starting transfers between devices, body(): far_strip = lax.ppermute(far_strip, 'row', far)  2.85 us
    ppermute x1, waiting for transfers between devices, body(): near_block = lax.ppermute(object_field, 'row', near)  2.71 us
  transfers between devices with their start and end apart: 11, of which 6 were waited for; matrix products, arithmetic and copies ran while one was open for 0% of the time, Pallas kernels for 6%

profile of v4, /device:TPU:8, one launch (start us, length us, event | category | flops | bytes accessed | tf_op | source)
XLA Modules:
  0.0 54.0 jit_solution(4298988822723311552)
XLA Ops:
  0.6 3.3 %collective-permute-start.3 = (f32[2,128,128]{2,1,0:T(8,128)}, f32[2,128,128]{2,1,0:T(8,128)S(1)}, u32[]{:S(2)}, u32[]{:S(2)}) collective-permute-start(f32[2,128,128]{2,1,0:T(8,128)} %refs_2_.1), channel_id=1, source_target_pairs={{2,4},{6,8},{10,12},{4,2},{8,6},{12,10},{3,5},{7,9},{11,13},{5,3},... | collective-permute-start | bytes 393224 | tf_op jit(solution)/shard_map/ppermute | solution.py:394
  3.9 1.7 %collective-permute-start.1 = (f32[2,128,128]{2,1,0:T(8,128)}, f32[2,128,128]{2,1,0:T(8,128)S(1)}, u32[]{:S(2)}, u32[]{:S(2)}) collective-permute-start(f32[2,128,128]{2,1,0:T(8,128)} %refs_2_.1), channel_id=1, source_target_pairs={{0,2},{2,0},{4,6},{6,4},{8,10},{10,8},{12,14},{14,12},{1,3},{3,1},... | collective-permute-start | bytes 393224 | tf_op jit(solution)/shard_map/ppermute | solution.py:393
  5.7 3.3 %collective-permute-done.3.far_ref = f32[2,128,128]{2,1,0:T(8,128)S(1)} collective-permute-done((f32[2,128,128]{2,1,0:T(8,128)}, f32[2,128,128]{2,1,0:T(8,128)S(1)}, u32[]{:S(2)}, u32[]{:S(2)}) %collective-permute-start.3) | collective-permute-done | bytes 131104 | tf_op jit(solution)/shard_map/ppermute | solution.py:394
  9.0 2.7 %collective-permute-done.1.near_ref = f32[2,128,128]{2,1,0:T(8,128)S(1)} collective-permute-done((f32[2,128,128]{2,1,0:T(8,128)}, f32[2,128,128]{2,1,0:T(8,128)S(1)}, u32[]{:S(2)}, u32[]{:S(2)}) %collective-permute-start.1) | collective-permute-done | bytes 131104 | tf_op jit(solution)/shard_map/ppermute | solution.py:393
  11.7 0.0 collective-permute-start.2
  12.3 1.5 %stage.1 = (f32[4,2,128,128]{3,2,1,0:T(8,128)S(1)}, f32[1,1,2,128,128]{4,3,2,1,0:T(8,128)S(1)}, f32[2,128,128]{2,1,0:T(8,128)S(1)}, bf16[4,256,256]{2,1,0:T(8,128)(2,1)S(1)}, f32[8,128]{1,0:T(8,128)S(1)}) custom-call(f32[4,2,128,128]{3,2,1,0:T(8,128)} %refs_0_.1, f32[1,1,2,128,128]{4,3,2,1,0:T(8,128)} %refs_1_.1, f32[2,128,128]{2,1,0:T(8,128)} %refs_2_.1, ...), custom_call_target="tpu_custom_call" | custom-call | flops 1048576 | bytes 2621440 | tf_op jit(solution)/shard_map/stage/pallas_call | solution.py:58
  13.8 0.0 collective-permute-done.own_pair_ref
  13.8 0.0 collective-permute-done.2.near_pair_ref
  13.9 2.6 %first.1 = (f32[2,2,128,128]{3,2,1,0:T(8,128)S(1)}, f32[2,2,128,128]{3,2,1,0:T(8,128)S(1)}, f32[2,2,2,128,128]{4,3,2,1,0:T(8,128)S(1)}, f32[2,2,128,128]{3,2,1,0:T(8,128)S(1)}) custom-call(s32[1,1,2,2]{3,2,1,0:T(2,128)} %offsets_hbm.3, s32[1,1]{1,0:T(1,128)S(6)} %copy.8.counts_ref, f32[2,128,128]{2,1,0:T(8,128)S(1)} %get-tuple-element.16.own_ref, ...), custom_call_target="tpu_custom_call" | custom-call | flops 1207959552 | bytes 2621440 | tf_op jit(solution)/shard_map/first/pallas_call | solution.py:273
  16.5 0.6 %collective-permute-start.8 = (f32[2,2,128,128]{3,2,1,0:T(8,128)S(1)}, f32[2,2,128,128]{3,2,1,0:T(8,128)S(1)}, u32[]{:S(2)}, u32[]{:S(2)}) collective-permute-start(f32[2,2,128,128]{3,2,1,0:T(8,128)S(1)} %get-tuple-element.29), channel_id=1, source_target_pairs={{0,1},{1,0},{2,3},{3,2},{4,5},{5,4},{6,7},{7,6},{8,9},{9,8},{10,11... | collective-permute-start | bytes 786440 | tf_op jit(solution)/shard_map/ppermute | solution.py:406
  17.0 1.0 %second.1 = (f32[2,2,128,128]{3,2,1,0:T(8,128)S(1)}, f32[2,2,384,128]{3,2,1,0:T(8,128)S(1)}) custom-call(s32[1,1,2,2]{3,2,1,0:T(2,128)} %offsets_hbm.3, f32[4,2,128,128]{3,2,1,0:T(8,128)S(1)} %get-tuple-element.17.probe_ref, bf16[4,256,256]{2,1,0:T(8,128)(2,1)S(1)} %get-tuple-element.18.tables_ref, f32[2,2,128,128]{3,2,1,0:T(8,128)S(1)} %get-tuple-element.20.window_ref, ...), custom_call_target="tpu_custom_call" | custom-call | flops 402653184 | bytes 1966080 | tf_op jit(solution)/shard_map/second/pallas_call | solution.py:302
  18.0 0.2 collective-permute-done.8
  18.2 11.7 %all_to_all.10.parts_ref = f32[8,64,128]{2,1,0:T(8,128)S(1)} all-to-all(f32[8,64,128]{2,1,0:T(8,128)S(1)} %bitcast.6), channel_id=1, replica_groups={{6,4,10,8,2,0,14,12},{7,5,11,9,3,1,15,13},{22,20,26,24,18,16,30,28},{23..., dimensions={0} | all-to-all | bytes 524288 | tf_op jit(solution)/shard_map/all_to_all | solution.py:412
  29.9 0.7 %shard_map.79 = f32[8,64,128]{2,1,0:T(8,128)} custom-call(f32[8,64,128]{2,1,0:T(8,128)S(1)} %all_to_all.10.parts_ref), custom_call_target="tpu_custom_call" | custom-call | flops 131072 | bytes 524288 | tf_op jit(solution)/shard_map/pallas_call | solution.py:361
  30.6 5.8 %all-to-all-start.1 = ((f32[8,64,128]{2,1,0:T(8,128)}), f32[8,64,128]{2,1,0:T(8,128)S(1)}, u32[]{:S(2)}, u32[]{:S(2)}) async-start(f32[8,64,128]{2,1,0:T(8,128)} %shard_map.79), calls=%async_computation.1 | async-start | bytes 524288 | tf_op jit(solution)/shard_map/all_to_all | solution.py:420
  36.5 0.1 collective-permute-start.5
  36.5 5.3 %all-to-all-done.1 = f32[8,64,128]{2,1,0:T(8,128)S(1)} async-done(((f32[8,64,128]{2,1,0:T(8,128)}), f32[8,64,128]{2,1,0:T(8,128)S(1)}, u32[]{:S(2)}, u32[]{:S(2)}) %all-to-all-start.1) | async-done | bytes 262176 | tf_op jit(solution)/shard_map/all_to_all | solution.py:420
  41.8 0.0 collective-permute-start.9
  41.9 2.1 %collective-permute-start.6 = (f32[2,128,128]{2,1,0:T(8,128)S(1)}, f32[2,128,128]{2,1,0:T(8,128)S(1)}, u32[]{:S(2)}, u32[]{:S(2)}) collective-permute-start(f32[2,128,128]{2,1,0:T(8,128)S(1)} %get-tuple-element.25), channel_id=1, source_target_pairs={{0,2},{2,0},{4,6},{6,4},{8,10},{10,8},{12,14},{14,12},{1,3},{3,1},... | collective-permute-start | bytes 393224 | tf_op jit(solution)/shard_map/ppermute | solution.py:418
  44.0 2.8 %collective-permute-start.7 = (f32[2,128,128]{2,1,0:T(8,128)S(1)}, f32[2,128,128]{2,1,0:T(8,128)S(1)}, u32[]{:S(2)}, u32[]{:S(2)}) collective-permute-start(f32[2,128,128]{2,1,0:T(8,128)S(1)} %get-tuple-element.26), channel_id=1, source_target_pairs={{2,4},{6,8},{10,12},{4,2},{8,6},{12,10},{3,5},{7,9},{11,13},{5,3},... | collective-permute-start | bytes 393224 | tf_op jit(solution)/shard_map/ppermute | solution.py:419
  46.9 1.3 %collective-permute-done.6.near_ref = f32[2,128,128]{2,1,0:T(8,128)S(1)} collective-permute-done((f32[2,128,128]{2,1,0:T(8,128)S(1)}, f32[2,128,128]{2,1,0:T(8,128)S(1)}, u32[]{:S(2)}, u32[]{:S(2)}) %collective-permute-start.6) | collective-permute-done | bytes 131104 | tf_op jit(solution)/shard_map/ppermute | solution.py:418
  48.2 4.2 %collective-permute-done.7.far_ref = f32[2,128,128]{2,1,0:T(8,128)S(1)} collective-permute-done((f32[2,128,128]{2,1,0:T(8,128)S(1)}, f32[2,128,128]{2,1,0:T(8,128)S(1)}, u32[]{:S(2)}, u32[]{:S(2)}) %collective-permute-start.7) | collective-permute-done | bytes 131104 | tf_op jit(solution)/shard_map/ppermute | solution.py:419
  52.4 0.7 %shard_map.78 = f32[2,128,128]{2,1,0:T(8,128)} custom-call(f32[2,128,128]{2,1,0:T(8,128)S(1)} %get-tuple-element.16.own_ref, f32[2,128,128]{2,1,0:T(8,128)S(1)} %get-tuple-element.24.middle_ref, f32[2,128,128]{2,1,0:T(8,128)S(1)} %collective-permute-done.6.near_ref, f32[2,128,128]{2,1,0:T(8,128)S(1)} %collective-permute-done.7.far_ref, ...), custom_call_target="tpu_custom_call" | custom-call | flops 164864 | bytes 659456 | tf_op jit(solution)/shard_map/pallas_call | solution.py:361
  53.1 0.8 %shard_map.80 = f32[4,2,128,128]{3,2,1,0:T(8,128)} custom-call(f32[4,2,128,128]{3,2,1,0:T(8,128)S(1)} %get-tuple-element.17.probe_ref, f32[2,2,128,128]{3,2,1,0:T(8,128)S(1)} %bitcast.5, f32[2,2,128,128]{3,2,1,0:T(8,128)S(1)} %collective-permute-done.9.other_ref), custom_call_target="tpu_custom_call" | custom-call | flops 393216 | bytes 1572864 | tf_op jit(solution)/shard_map/pallas_call | solution.py:361
  (8 shorter events, 0.1 us)
Async XLA Ops:
  0.6 8.3 %collective-permute-start.3 = (f32[2,128,128]{2,1,0:T(8,128)}, f32[2,128,128]{2,1,0:T(8,128)S(1)}, u32[]{:S(2)}, u32[]{:S(2)}) collective-permute-start(f32[2,128,128]{2,1,0:T(8,128)} %refs_2_.1), channel_id=1, source_target_pairs={{2,4},{6,8},{10,12},{4,2},{8,6},{12,10},{3,5},{7,9},{11,13},{5,3},... | collective-permute-start | bytes 393224 | tf_op jit(solution)/shard_map/ppermute | solution.py:394
  3.9 7.8 %collective-permute-start.1 = (f32[2,128,128]{2,1,0:T(8,128)}, f32[2,128,128]{2,1,0:T(8,128)S(1)}, u32[]{:S(2)}, u32[]{:S(2)}) collective-permute-start(f32[2,128,128]{2,1,0:T(8,128)} %refs_2_.1), channel_id=1, source_target_pairs={{0,2},{2,0},{4,6},{6,4},{8,10},{10,8},{12,14},{14,12},{1,3},{3,1},... | collective-permute-start | bytes 393224 | tf_op jit(solution)/shard_map/ppermute | solution.py:393
  5.7 8.2 %collective-permute-start = (f32[2,128,128]{2,1,0:T(8,128)}, f32[2,128,128]{2,1,0:T(8,128)S(1)}, u32[]{:S(2)}, u32[]{:S(2)}) collective-permute-start(f32[2,128,128]{2,1,0:T(8,128)} %refs_2_.1), channel_id=1, source_target_pairs={{0,1},{1,0},{2,3},{3,2},{4,5},{5,4},{6,7},{7,6},{8,9},{9,8},{10,11... | collective-permute-start | bytes 393224 | tf_op jit(solution)/shard_map/ppermute | solution.py:395
  9.0 4.9 %collective-permute-start.4 = (f32[2,128,128]{2,1,0:T(8,128)S(1)}, f32[2,128,128]{2,1,0:T(8,128)S(1)}, u32[]{:S(2)}, u32[]{:S(2)}) collective-permute-start(f32[2,128,128]{2,1,0:T(8,128)S(1)} %collective-permute-done.3.far_ref), channel_id=1, source_target_pairs={{0,1},{1,0},{2,3},{3,2},{4,5},{5,4},{6,7},{7,6},{8,9},{9,8},{10,11... | collective-permute-start | bytes 393224 | tf_op jit(solution)/shard_map/ppermute | solution.py:397
  11.7 2.2 %collective-permute-start.2 = (f32[2,128,128]{2,1,0:T(8,128)S(1)}, f32[2,128,128]{2,1,0:T(8,128)S(1)}, u32[]{:S(2)}, u32[]{:S(2)}) collective-permute-start(f32[2,128,128]{2,1,0:T(8,128)S(1)} %collective-permute-done.1.near_ref), channel_id=1, source_target_pairs={{0,1},{1,0},{2,3},{3,2},{4,5},{5,4},{6,7},{7,6},{8,9},{9,8},{10,11... | collective-permute-start | bytes 393224 | tf_op jit(solution)/shard_map/ppermute | solution.py:396
  16.5 1.7 %collective-permute-start.8 = (f32[2,2,128,128]{3,2,1,0:T(8,128)S(1)}, f32[2,2,128,128]{3,2,1,0:T(8,128)S(1)}, u32[]{:S(2)}, u32[]{:S(2)}) collective-permute-start(f32[2,2,128,128]{3,2,1,0:T(8,128)S(1)} %get-tuple-element.29), channel_id=1, source_target_pairs={{0,1},{1,0},{2,3},{3,2},{4,5},{5,4},{6,7},{7,6},{8,9},{9,8},{10,11... | collective-permute-start | bytes 786440 | tf_op jit(solution)/shard_map/ppermute | solution.py:406
  30.6 11.2 %all-to-all-start.1 = ((f32[8,64,128]{2,1,0:T(8,128)}), f32[8,64,128]{2,1,0:T(8,128)S(1)}, u32[]{:S(2)}, u32[]{:S(2)}) async-start(f32[8,64,128]{2,1,0:T(8,128)} %shard_map.79), calls=%async_computation.1 | async-start | bytes 524288 | tf_op jit(solution)/shard_map/all_to_all | solution.py:420
  36.5 5.4 %collective-permute-start.5 = (f32[2,384,128]{2,1,0:T(8,128)S(1)}, f32[2,384,128]{2,1,0:T(8,128)S(1)}, u32[]{:S(2)}, u32[]{:S(2)}) collective-permute-start(f32[2,384,128]{2,1,0:T(8,128)S(1)} %slice_bitcast_fusion), channel_id=1, source_target_pairs={{0,1},{1,0},{2,3},{3,2},{4,5},{5,4},{6,7},{7,6},{8,9},{9,8},{10,11... | collective-permute-start | bytes 1179656 | tf_op jit(solution)/shard_map/ppermute | solution.py:408
  41.8 11.3 %collective-permute-start.9 = (f32[2,2,128,128]{3,2,1,0:T(8,128)S(1)}, f32[2,2,128,128]{3,2,1,0:T(8,128)S(1)}, u32[]{:S(2)}, u32[]{:S(2)}) collective-permute-start(f32[2,2,128,128]{3,2,1,0:T(8,128)S(1)} %bitcast.4), channel_id=1, source_target_pairs={{0,1},{1,0},{2,3},{3,2},{4,5},{5,4},{6,7},{7,6},{8,9},{9,8},{10,11... | collective-permute-start | bytes 786440 | tf_op jit(solution)/shard_map/ppermute | solution.py:422
  41.9 6.3 %collective-permute-start.6 = (f32[2,128,128]{2,1,0:T(8,128)S(1)}, f32[2,128,128]{2,1,0:T(8,128)S(1)}, u32[]{:S(2)}, u32[]{:S(2)}) collective-permute-start(f32[2,128,128]{2,1,0:T(8,128)S(1)} %get-tuple-element.25), channel_id=1, source_target_pairs={{0,2},{2,0},{4,6},{6,4},{8,10},{10,8},{12,14},{14,12},{1,3},{3,1},... | collective-permute-start | bytes 393224 | tf_op jit(solution)/shard_map/ppermute | solution.py:418
  44.0 8.4 %collective-permute-start.7 = (f32[2,128,128]{2,1,0:T(8,128)S(1)}, f32[2,128,128]{2,1,0:T(8,128)S(1)}, u32[]{:S(2)}, u32[]{:S(2)}) collective-permute-start(f32[2,128,128]{2,1,0:T(8,128)S(1)} %get-tuple-element.26), channel_id=1, source_target_pairs={{2,4},{6,8},{10,12},{4,2},{8,6},{12,10},{3,5},{7,9},{11,13},{5,3},... | collective-permute-start | bytes 393224 | tf_op jit(solution)/shard_map/ppermute | solution.py:419

commit v5 on v4

--- a/solution.py
+++ b/solution.py
@@ -79,17 +79,17 @@
     high, low = split(value)
     if on_left:
         table = jnp.concatenate(
-            [tables_ref[1 - which], tables_ref[3 - which], tables_ref[1 - which]], axis=1
+            [tables_ref[1 - which], tables_ref[1 - which], tables_ref[3 - which]], axis=1
         )
         out = jnp.dot(
-            table, jnp.concatenate([high, high, low], axis=0), preferred_element_type=jnp.float32
+            table, jnp.concatenate([high, low, high], axis=0), preferred_element_type=jnp.float32
         )
     else:
         table = jnp.concatenate(
-            [tables_ref[which], tables_ref[which], tables_ref[2 + which]], axis=0
+            [tables_ref[which], tables_ref[2 + which], tables_ref[which]], axis=0
         )
         out = jnp.dot(
-            jnp.concatenate([high, low, high], axis=1), table, preferred_element_type=jnp.float32
+            jnp.concatenate([high, high, low], axis=1), table, preferred_element_type=jnp.float32
         )
     found = []
     for index in range(len(pieces)):
@@ -100,6 +100,13 @@
                 lax.slice_in_dim(part, width, 2 * width, axis=inner),
             )
         )
+    return found
+
+
+def in_groups(value, size, *rest):
+    found = []
+    for at in range(0, len(value), size):
+        found += product(value[at : at + size], *rest)
     return found
 
 
@@ -187,8 +194,8 @@
                 )
             )
         values.append(exits)
-    values = [product(value, tables_ref, 0, False) for value in values]
-    values = [product(value, tables_ref, 0, True) for value in values]
+    values = [in_groups(value, 2, tables_ref, 0, False) for value in values]
+    values = [in_groups(value, 4, tables_ref, 0, True) for value in values]
     backs = []
     for slot, far in enumerate(values):
         live = (slot < counts_ref[0, 0]).astype(jnp.float32)
@@ -198,8 +205,8 @@
             for part in range(2):
                 kept_ref[slot, k, part] = misfit * far[half + k][part]
         backs.append([(misfit * re, misfit * im) for re, im in far[:half]])
-    backs = [product(back, tables_ref, 1, True) for back in backs]
-    backs = [product(back, tables_ref, 1, False) for back in backs]
+    backs = [in_groups(back, 2, tables_ref, 1, True) for back in backs]
+    backs = [in_groups(back, 2, tables_ref, 1, False) for back in backs]
     grads = combine(backs, probe_ref, order[:half], windows, send_probe_ref)
     for slot in range(slots):
         for part in range(2):
@@ -248,8 +255,8 @@
         for slot in range(slots)
     ]
     windows = [[window_ref[slot, 0], window_ref[slot, 1]] for slot in range(slots)]
-    backs = [product(back, tables_ref, 1, True) for back in backs]
-    backs = [product(back, tables_ref, 1, False) for back in backs]
+    backs = [in_groups(back, 2, tables_ref, 1, True) for back in backs]
+    backs = [in_groups(back, 2, tables_ref, 1, False) for back in backs]
     grads = combine(backs, probe_ref, order, windows, keep_probe_ref)
     fetch.wait()
     for slot in range(slots):
@@ -369,12 +376,9 @@
 
 
 def member_order(count):
-    pairs = count // 2
-    middle = (pairs - 1) // 2
+    pairs = list(range(count // 2))
     order = []
-    for step in range(pairs):
-        near = (step + 1) // 2
-        at = middle + near if step % 2 else middle - near
+    for at in pairs[0::2][::-1] + pairs[1::2][::-1]:
         order.extend((2 * at + 1, 2 * at))
     return order
 

time: 54.3 us -> 54.5 us (level)
  the two profiles are of different devices: /device:TPU:8 before, /device:TPU:16 now
where the time goes in v5:
time: 54.5 us; the launch traced here: 54.2 us
  waiting for transfers between devices  18.7 us (34%)
  starting transfers between devices  15.4 us (28%)
  blocking collectives  11.4 us (21%)
  Pallas kernels  7.23 us (13%)
  between operations  1.37 us (3%)
    all_to_all x1, blocking collectives, body(): lax.all_to_all(mine, 'row', 0, 0, tiled=True, axis_index_groups=members)  11.4 us
    all_to_all x1, waiting for transfers between devices, body(): lax.all_to_all(mine, 'row', 0, 0, tiled=True, axis_index_groups=members)  6.11 us
    all_to_all x1, starting transfers between devices, body(): lax.all_to_all(mine, 'row', 0, 0, tiled=True, axis_index_groups=members)  5.48 us
    ppermute x1, waiting for transfers between devices, body(): far_strip = lax.ppermute(far_strip, 'row', far)  4.24 us
    ppermute x1, waiting for transfers between devices, body(): far_block = lax.ppermute(object_field, 'row', far)  3.31 us
    ppermute x1, starting transfers between devices, body(): far_block = lax.ppermute(object_field, 'row', far)  3.28 us
    ppermute x1, waiting for transfers between devices, body(): near_block = lax.ppermute(object_field, 'row', near)  2.71 us
    pallas_call x1, Pallas kernels, run_first(): pl.pallas_call(first_kernel, out_shape=(images(half), images(slots), imag...  2.47 us
  transfers between devices with their start and end apart: 11, of which 6 were waited for; matrix products, arithmetic and copies ran while one was open for 0% of the time, Pallas kernels for 6%

profile of v5, /device:TPU:16, one launch (start us, length us, event | category | flops | bytes accessed | tf_op | source)
XLA Modules:
  0.0 54.2 jit_solution(15883549226652217037)
XLA Ops:
  0.6 3.3 %collective-permute-start.3 = (f32[2,128,128]{2,1,0:T(8,128)}, f32[2,128,128]{2,1,0:T(8,128)S(1)}, u32[]{:S(2)}, u32[]{:S(2)}) collective-permute-start(f32[2,128,128]{2,1,0:T(8,128)} %refs_2_.1), channel_id=1, source_target_pairs={{2,4},{6,8},{10,12},{4,2},{8,6},{12,10},{3,5},{7,9},{11,13},{5,3},... | collective-permute-start | bytes 393224 | tf_op jit(solution)/shard_map/ppermute | solution.py:398
  3.9 1.7 %collective-permute-start.1 = (f32[2,128,128]{2,1,0:T(8,128)}, f32[2,128,128]{2,1,0:T(8,128)S(1)}, u32[]{:S(2)}, u32[]{:S(2)}) collective-permute-start(f32[2,128,128]{2,1,0:T(8,128)} %refs_2_.1), channel_id=1, source_target_pairs={{0,2},{2,0},{4,6},{6,4},{8,10},{10,8},{12,14},{14,12},{1,3},{3,1},... | collective-permute-start | bytes 393224 | tf_op jit(solution)/shard_map/ppermute | solution.py:397
  5.7 3.3 %collective-permute-done.3.far_ref = f32[2,128,128]{2,1,0:T(8,128)S(1)} collective-permute-done((f32[2,128,128]{2,1,0:T(8,128)}, f32[2,128,128]{2,1,0:T(8,128)S(1)}, u32[]{:S(2)}, u32[]{:S(2)}) %collective-permute-start.3) | collective-permute-done | bytes 131104 | tf_op jit(solution)/shard_map/ppermute | solution.py:398
  9.0 2.7 %collective-permute-done.1.near_ref = f32[2,128,128]{2,1,0:T(8,128)S(1)} collective-permute-done((f32[2,128,128]{2,1,0:T(8,128)}, f32[2,128,128]{2,1,0:T(8,128)S(1)}, u32[]{:S(2)}, u32[]{:S(2)}) %collective-permute-start.1) | collective-permute-done | bytes 131104 | tf_op jit(solution)/shard_map/ppermute | solution.py:397
  11.7 0.0 collective-permute-start.2
  12.3 1.5 %stage.1 = (f32[4,2,128,128]{3,2,1,0:T(8,128)S(1)}, f32[1,1,2,128,128]{4,3,2,1,0:T(8,128)S(1)}, f32[2,128,128]{2,1,0:T(8,128)S(1)}, bf16[4,256,256]{2,1,0:T(8,128)(2,1)S(1)}, f32[8,128]{1,0:T(8,128)S(1)}) custom-call(f32[4,2,128,128]{3,2,1,0:T(8,128)} %refs_0_.1, f32[1,1,2,128,128]{4,3,2,1,0:T(8,128)} %refs_1_.1, f32[2,128,128]{2,1,0:T(8,128)} %refs_2_.1, ...), custom_call_target="tpu_custom_call" | custom-call | flops 1048576 | bytes 2621440 | tf_op jit(solution)/shard_map/stage/pallas_call | solution.py:58
  13.8 0.0 collective-permute-done.own_pair_ref
  13.9 2.5 %first.1 = (f32[2,2,128,128]{3,2,1,0:T(8,128)S(1)}, f32[2,2,128,128]{3,2,1,0:T(8,128)S(1)}, f32[2,2,2,128,128]{4,3,2,1,0:T(8,128)S(1)}, f32[2,2,128,128]{3,2,1,0:T(8,128)S(1)}) custom-call(s32[1,1,2,2]{3,2,1,0:T(2,128)} %offsets_hbm.3, s32[1,1]{1,0:T(1,128)S(6)} %copy.8.counts_ref, f32[2,128,128]{2,1,0:T(8,128)S(1)} %get-tuple-element.16.own_ref, ...), custom_call_target="tpu_custom_call" | custom-call | flops 1207959552 | bytes 2621440 | tf_op jit(solution)/shard_map/first/pallas_call | solution.py:280
  16.3 0.6 %collective-permute-start.8 = (f32[2,2,128,128]{3,2,1,0:T(8,128)S(1)}, f32[2,2,128,128]{3,2,1,0:T(8,128)S(1)}, u32[]{:S(2)}, u32[]{:S(2)}) collective-permute-start(f32[2,2,128,128]{3,2,1,0:T(8,128)S(1)} %get-tuple-element.29), channel_id=1, source_target_pairs={{0,1},{1,0},{2,3},{3,2},{4,5},{5,4},{6,7},{7,6},{8,9},{9,8},{10,11... | collective-permute-start | bytes 786440 | tf_op jit(solution)/shard_map/ppermute | solution.py:410
  16.9 1.0 %second.1 = (f32[2,2,128,128]{3,2,1,0:T(8,128)S(1)}, f32[2,2,384,128]{3,2,1,0:T(8,128)S(1)}) custom-call(s32[1,1,2,2]{3,2,1,0:T(2,128)} %offsets_hbm.3, f32[4,2,128,128]{3,2,1,0:T(8,128)S(1)} %get-tuple-element.17.probe_ref, bf16[4,256,256]{2,1,0:T(8,128)(2,1)S(1)} %get-tuple-element.18.tables_ref, f32[2,2,128,128]{3,2,1,0:T(8,128)S(1)} %get-tuple-element.20.window_ref, ...), custom_call_target="tpu_custom_call" | custom-call | flops 402653184 | bytes 1966080 | tf_op jit(solution)/shard_map/second/pallas_call | solution.py:309
  17.9 0.2 collective-permute-done.8
  18.1 11.4 %all_to_all.10.parts_ref = f32[8,64,128]{2,1,0:T(8,128)S(1)} all-to-all(f32[8,64,128]{2,1,0:T(8,128)S(1)} %bitcast.6), channel_id=1, replica_groups={{10,8,2,0,14,12,6,4},{11,9,3,1,15,13,7,5},{26,24,18,16,30,28,22,20},{27..., dimensions={0} | all-to-all | bytes 524288 | tf_op jit(solution)/shard_map/all_to_all | solution.py:416
  29.5 0.7 %shard_map.79 = f32[8,64,128]{2,1,0:T(8,128)} custom-call(f32[8,64,128]{2,1,0:T(8,128)S(1)} %all_to_all.10.parts_ref), custom_call_target="tpu_custom_call" | custom-call | flops 131072 | bytes 524288 | tf_op jit(solution)/shard_map/pallas_call | solution.py:368
  30.2 5.5 %all-to-all-start.1 = ((f32[8,64,128]{2,1,0:T(8,128)}), f32[8,64,128]{2,1,0:T(8,128)S(1)}, u32[]{:S(2)}, u32[]{:S(2)}) async-start(f32[8,64,128]{2,1,0:T(8,128)} %shard_map.79), calls=%async_computation.1 | async-start | bytes 524288 | tf_op jit(solution)/shard_map/all_to_all | solution.py:424
  35.8 0.1 collective-permute-start.5
  35.8 6.1 %all-to-all-done.1 = f32[8,64,128]{2,1,0:T(8,128)S(1)} async-done(((f32[8,64,128]{2,1,0:T(8,128)}), f32[8,64,128]{2,1,0:T(8,128)S(1)}, u32[]{:S(2)}, u32[]{:S(2)}) %all-to-all-start.1) | async-done | bytes 262176 | tf_op jit(solution)/shard_map/all_to_all | solution.py:424
  41.9 0.0 collective-permute-start.9
  41.9 0.0 collective-permute-done.5.got_ref
  42.0 2.2 %collective-permute-start.6 = (f32[2,128,128]{2,1,0:T(8,128)S(1)}, f32[2,128,128]{2,1,0:T(8,128)S(1)}, u32[]{:S(2)}, u32[]{:S(2)}) collective-permute-start(f32[2,128,128]{2,1,0:T(8,128)S(1)} %get-tuple-element.25), channel_id=1, source_target_pairs={{0,2},{2,0},{4,6},{6,4},{8,10},{10,8},{12,14},{14,12},{1,3},{3,1},... | collective-permute-start | bytes 393224 | tf_op jit(solution)/shard_map/ppermute | solution.py:422
  44.2 2.0 %collective-permute-start.7 = (f32[2,128,128]{2,1,0:T(8,128)S(1)}, f32[2,128,128]{2,1,0:T(8,128)S(1)}, u32[]{:S(2)}, u32[]{:S(2)}) collective-permute-start(f32[2,128,128]{2,1,0:T(8,128)S(1)} %get-tuple-element.26), channel_id=1, source_target_pairs={{2,4},{6,8},{10,12},{4,2},{8,6},{12,10},{3,5},{7,9},{11,13},{5,3},... | collective-permute-start | bytes 393224 | tf_op jit(solution)/shard_map/ppermute | solution.py:423
  46.2 2.1 %collective-permute-done.6.near_ref = f32[2,128,128]{2,1,0:T(8,128)S(1)} collective-permute-done((f32[2,128,128]{2,1,0:T(8,128)S(1)}, f32[2,128,128]{2,1,0:T(8,128)S(1)}, u32[]{:S(2)}, u32[]{:S(2)}) %collective-permute-start.6) | collective-permute-done | bytes 131104 | tf_op jit(solution)/shard_map/ppermute | solution.py:422
  48.4 4.2 %collective-permute-done.7.far_ref = f32[2,128,128]{2,1,0:T(8,128)S(1)} collective-permute-done((f32[2,128,128]{2,1,0:T(8,128)S(1)}, f32[2,128,128]{2,1,0:T(8,128)S(1)}, u32[]{:S(2)}, u32[]{:S(2)}) %collective-permute-start.7) | collective-permute-done | bytes 131104 | tf_op jit(solution)/shard_map/ppermute | solution.py:423
  52.6 0.7 %shard_map.78 = f32[2,128,128]{2,1,0:T(8,128)} custom-call(f32[2,128,128]{2,1,0:T(8,128)S(1)} %get-tuple-element.16.own_ref, f32[2,128,128]{2,1,0:T(8,128)S(1)} %get-tuple-element.24.middle_ref, f32[2,128,128]{2,1,0:T(8,128)S(1)} %collective-permute-done.6.near_ref, f32[2,128,128]{2,1,0:T(8,128)S(1)} %collective-permute-done.7.far_ref, ...), custom_call_target="tpu_custom_call" | custom-call | flops 164864 | bytes 659456 | tf_op jit(solution)/shard_map/pallas_call | solution.py:368
  53.3 0.8 %shard_map.80 = f32[4,2,128,128]{3,2,1,0:T(8,128)} custom-call(f32[4,2,128,128]{3,2,1,0:T(8,128)S(1)} %get-tuple-element.17.probe_ref, f32[2,2,128,128]{3,2,1,0:T(8,128)S(1)} %bitcast.5, f32[2,2,128,128]{3,2,1,0:T(8,128)S(1)} %collective-permute-done.9.other_ref), custom_call_target="tpu_custom_call" | custom-call | flops 393216 | bytes 1572864 | tf_op jit(solution)/shard_map/pallas_call | solution.py:368
  (8 shorter events, 0.1 us)
Async XLA Ops:
  0.6 8.3 %collective-permute-start.3 = (f32[2,128,128]{2,1,0:T(8,128)}, f32[2,128,128]{2,1,0:T(8,128)S(1)}, u32[]{:S(2)}, u32[]{:S(2)}) collective-permute-start(f32[2,128,128]{2,1,0:T(8,128)} %refs_2_.1), channel_id=1, source_target_pairs={{2,4},{6,8},{10,12},{4,2},{8,6},{12,10},{3,5},{7,9},{11,13},{5,3},... | collective-permute-start | bytes 393224 | tf_op jit(solution)/shard_map/ppermute | solution.py:398
  3.9 7.8 %collective-permute-start.1 = (f32[2,128,128]{2,1,0:T(8,128)}, f32[2,128,128]{2,1,0:T(8,128)S(1)}, u32[]{:S(2)}, u32[]{:S(2)}) collective-permute-start(f32[2,128,128]{2,1,0:T(8,128)} %refs_2_.1), channel_id=1, source_target_pairs={{0,2},{2,0},{4,6},{6,4},{8,10},{10,8},{12,14},{14,12},{1,3},{3,1},... | collective-permute-start | bytes 393224 | tf_op jit(solution)/shard_map/ppermute | solution.py:397
  5.7 8.2 %collective-permute-start = (f32[2,128,128]{2,1,0:T(8,128)}, f32[2,128,128]{2,1,0:T(8,128)S(1)}, u32[]{:S(2)}, u32[]{:S(2)}) collective-permute-start(f32[2,128,128]{2,1,0:T(8,128)} %refs_2_.1), channel_id=1, source_target_pairs={{0,1},{1,0},{2,3},{3,2},{4,5},{5,4},{6,7},{7,6},{8,9},{9,8},{10,11... | collective-permute-start | bytes 393224 | tf_op jit(solution)/shard_map/ppermute | solution.py:399
  9.0 4.9 %collective-permute-start.4 = (f32[2,128,128]{2,1,0:T(8,128)S(1)}, f32[2,128,128]{2,1,0:T(8,128)S(1)}, u32[]{:S(2)}, u32[]{:S(2)}) collective-permute-start(f32[2,128,128]{2,1,0:T(8,128)S(1)} %collective-permute-done.3.far_ref), channel_id=1, source_target_pairs={{0,1},{1,0},{2,3},{3,2},{4,5},{5,4},{6,7},{7,6},{8,9},{9,8},{10,11... | collective-permute-start | bytes 393224 | tf_op jit(solution)/shard_map/ppermute | solution.py:401
  11.7 2.2 %collective-permute-start.2 = (f32[2,128,128]{2,1,0:T(8,128)S(1)}, f32[2,128,128]{2,1,0:T(8,128)S(1)}, u32[]{:S(2)}, u32[]{:S(2)}) collective-permute-start(f32[2,128,128]{2,1,0:T(8,128)S(1)} %collective-permute-done.1.near_ref), channel_id=1, source_target_pairs={{0,1},{1,0},{2,3},{3,2},{4,5},{5,4},{6,7},{7,6},{8,9},{9,8},{10,11... | collective-permute-start | bytes 393224 | tf_op jit(solution)/shard_map/ppermute | solution.py:400
  16.3 1.7 %collective-permute-start.8 = (f32[2,2,128,128]{3,2,1,0:T(8,128)S(1)}, f32[2,2,128,128]{3,2,1,0:T(8,128)S(1)}, u32[]{:S(2)}, u32[]{:S(2)}) collective-permute-start(f32[2,2,128,128]{3,2,1,0:T(8,128)S(1)} %get-tuple-element.29), channel_id=1, source_target_pairs={{0,1},{1,0},{2,3},{3,2},{4,5},{5,4},{6,7},{7,6},{8,9},{9,8},{10,11... | collective-permute-start | bytes 786440 | tf_op jit(solution)/shard_map/ppermute | solution.py:410
  30.2 11.7 %all-to-all-start.1 = ((f32[8,64,128]{2,1,0:T(8,128)}), f32[8,64,128]{2,1,0:T(8,128)S(1)}, u32[]{:S(2)}, u32[]{:S(2)}) async-start(f32[8,64,128]{2,1,0:T(8,128)} %shard_map.79), calls=%async_computation.1 | async-start | bytes 524288 | tf_op jit(solution)/shard_map/all_to_all | solution.py:424
  35.8 6.2 %collective-permute-start.5 = (f32[2,384,128]{2,1,0:T(8,128)S(1)}, f32[2,384,128]{2,1,0:T(8,128)S(1)}, u32[]{:S(2)}, u32[]{:S(2)}) collective-permute-start(f32[2,384,128]{2,1,0:T(8,128)S(1)} %slice_bitcast_fusion), channel_id=1, source_target_pairs={{0,1},{1,0},{2,3},{3,2},{4,5},{5,4},{6,7},{7,6},{8,9},{9,8},{10,11... | collective-permute-start | bytes 1179656 | tf_op jit(solution)/shard_map/ppermute | solution.py:412
  41.9 11.4 %collective-permute-start.9 = (f32[2,2,128,128]{3,2,1,0:T(8,128)S(1)}, f32[2,2,128,128]{3,2,1,0:T(8,128)S(1)}, u32[]{:S(2)}, u32[]{:S(2)}) collective-permute-start(f32[2,2,128,128]{3,2,1,0:T(8,128)S(1)} %bitcast.4), channel_id=1, source_target_pairs={{0,1},{1,0},{2,3},{3,2},{4,5},{5,4},{6,7},{7,6},{8,9},{9,8},{10,11... | collective-permute-start | bytes 786440 | tf_op jit(solution)/shard_map/ppermute | solution.py:426
  42.0 6.4 %collective-permute-start.6 = (f32[2,128,128]{2,1,0:T(8,128)S(1)}, f32[2,128,128]{2,1,0:T(8,128)S(1)}, u32[]{:S(2)}, u32[]{:S(2)}) collective-permute-start(f32[2,128,128]{2,1,0:T(8,128)S(1)} %get-tuple-element.25), channel_id=1, source_target_pairs={{0,2},{2,0},{4,6},{6,4},{8,10},{10,8},{12,14},{14,12},{1,3},{3,1},... | collective-permute-start | bytes 393224 | tf_op jit(solution)/shard_map/ppermute | solution.py:422
  44.2 8.4 %collective-permute-start.7 = (f32[2,128,128]{2,1,0:T(8,128)S(1)}, f32[2,128,128]{2,1,0:T(8,128)S(1)}, u32[]{:S(2)}, u32[]{:S(2)}) collective-permute-start(f32[2,128,128]{2,1,0:T(8,128)S(1)} %get-tuple-element.26), channel_id=1, source_target_pairs={{2,4},{6,8},{10,12},{4,2},{8,6},{12,10},{3,5},{7,9},{11,13},{5,3},... | collective-permute-start | bytes 393224 | tf_op jit(solution)/shard_map/ppermute | solution.py:423

commit v6 on v5

--- a/solution.py
+++ b/solution.py
@@ -125,7 +125,7 @@
 
 
 def first_kernel(
-    offsets_hbm,
+    offsets_ref,
     counts_ref,
     own_ref,
     own_pair_ref,
@@ -140,12 +140,8 @@
     window_ref,
     kept_ref,
     grad_ref,
-    offsets_ref,
-    offsets_sem,
     frame,
 ):
-    fetch = pltpu.make_async_copy(offsets_hbm, offsets_ref, offsets_sem)
-    fetch.start()
     modes = probe_ref.shape[0]
     width = probe_ref.shape[-1]
     slots = patterns_ref.shape[2]
@@ -160,7 +156,6 @@
         frame[index, :, pl.ds(width, width), :] = own[...]
         frame[index, :, pl.ds(near_at, width), :] = near[...]
         frame[index, :, pl.ds(far_at, width), :] = far[...]
-    fetch.wait()
 
     mine = core * half
     order = [half - mine + k for k in range(half)] + [mine + k for k in range(half)]
@@ -204,8 +199,8 @@
         for k in range(half):
             for part in range(2):
                 kept_ref[slot, k, part] = misfit * far[half + k][part]
-        backs.append([(misfit * re, misfit * im) for re, im in far[:half]])
-    backs = [in_groups(back, 2, tables_ref, 1, True) for back in backs]
+        back = [(misfit * re, misfit * im) for re, im in far[:half]]
+        backs.append(in_groups(back, 2, tables_ref, 1, True))
     backs = [in_groups(back, 2, tables_ref, 1, False) for back in backs]
     grads = combine(backs, probe_ref, order[:half], windows, send_probe_ref)
     for slot in range(slots):
@@ -230,7 +225,7 @@
 
 
 def second_kernel(
-    offsets_hbm,
+    offsets_ref,
     probe_ref,
     tables_ref,
     window_ref,
@@ -238,11 +233,7 @@
     part_ref,
     keep_probe_ref,
     grad_ref,
-    offsets_ref,
-    offsets_sem,
 ):
-    fetch = pltpu.make_async_copy(offsets_hbm, offsets_ref, offsets_sem)
-    fetch.start()
     modes = probe_ref.shape[0]
     width = probe_ref.shape[-1]
     slots = window_ref.shape[0]
@@ -258,7 +249,6 @@
     backs = [in_groups(back, 2, tables_ref, 1, True) for back in backs]
     backs = [in_groups(back, 2, tables_ref, 1, False) for back in backs]
     grads = combine(backs, probe_ref, order, windows, keep_probe_ref)
-    fetch.wait()
     for slot in range(slots):
         rows = pl.ds(offsets_ref[0, 0, slot, 0], width)
         shift, in_left, blocks = columns_of(offsets_ref[0, 0, slot, 1], width, core)
@@ -281,14 +271,12 @@
         first_kernel,
         out_shape=(images(half), images(slots), images(slots, half), images(slots)),
         in_specs=[
-            pl.BlockSpec(memory_space=pltpu.HBM),
+            pl.BlockSpec(memory_space=pltpu.VMEM),
             pl.BlockSpec(memory_space=pltpu.SMEM),
         ]
         + [vmem] * 9,
         out_specs=(vmem,) * 4,
         scratch_shapes=[
-            pltpu.SMEM(offsets.shape, offsets.dtype),
-            pltpu.SemaphoreType.DMA,
             pltpu.VMEM((2, 2, 3 * width, width), jnp.float32),
         ],
         cost_estimate=pl.CostEstimate(
@@ -312,11 +300,9 @@
             jax.ShapeDtypeStruct((half, 2, width, width), jnp.float32),
             jax.ShapeDtypeStruct((2, 2, 3 * width, width), jnp.float32),
         ),
-        in_specs=[pl.BlockSpec(memory_space=pltpu.HBM)] + [vmem] * 5,
+        in_specs=[vmem] * 6,
         out_specs=(vmem,) * 2,
         scratch_shapes=[
-            pltpu.SMEM(offsets.shape, offsets.dtype),
-            pltpu.SemaphoreType.DMA,
         ],
         cost_estimate=pl.CostEstimate(
             flops=slots * modes * 3 * 8 * width**3,
@@ -399,11 +385,10 @@
     own_pair = lax.ppermute(object_field, "col", pair)
     near_pair = lax.ppermute(near_block, "col", pair)
     far_pair = lax.ppermute(far_block, "col", pair)
-    probe_here, patterns_here, own, tables, weight = stage(
-        probe, patterns, object_field, jnp.asarray(host_tables(width))
+    probe_here, patterns_here, own, tables, offsets, weight = stage(
+        probe, patterns, object_field, jnp.asarray(host_tables(width)), offsets
     )
     blocks = (own, own_pair, near_block, near_pair, far_block, far_pair)
-    offsets = pltpu.with_memory_space_constraint(offsets, pltpu.HBM)
     send_probe, window, kept, part = run_first(
         offsets, counts, blocks, probe_here, patterns_here, tables
     )

time: 54.5 us -> 53.9 us (0.989)
  Pallas kernels: 7.23 us -> 6.61 us
    pallas_call x1, Pallas kernels: 2.47 us -> 1.86 us  [run_first(): pl.pallas_call(first_kernel, out_shape=(images(half), images(slots), imag...]
where the time goes in v6:
time: 53.9 us; the launch traced here: 53.6 us
  waiting for transfers between devices  18.7 us (35%)
  starting transfers between devices  15.4 us (29%)
  blocking collectives  11.4 us (21%)
  Pallas kernels  6.61 us (12%)
  between operations  1.37 us (3%)
    all_to_all x1, blocking collectives, body(): lax.all_to_all(mine, 'row', 0, 0, tiled=True, axis_index_groups=members)  11.4 us
    all_to_all x1, waiting for transfers between devices, body(): lax.all_to_all(mine, 'row', 0, 0, tiled=True, axis_index_groups=members)  6.1 us
    all_to_all x1, starting transfers between devices, body(): lax.all_to_all(mine, 'row', 0, 0, tiled=True, axis_index_groups=members)  5.48 us
    ppermute x1, waiting for transfers between devices, body(): far_strip = lax.ppermute(far_strip, 'row', far)  4.24 us
    ppermute x1, waiting for transfers between devices, body(): far_block = lax.ppermute(object_field, 'row', far)  3.31 us
    ppermute x1, starting transfers between devices, body(): far_block = lax.ppermute(object_field, 'row', far)  3.28 us
    ppermute x1, waiting for transfers between devices, body(): near_block = lax.ppermute(object_field, 'row', near)  2.71 us
    pallas_call x4, Pallas kernels, in_vmem(): pl.pallas_call(kernel, out_shape=out if len(out) > 1 else out[0], in_spec...  2.32 us
  transfers between devices with their start and end apart: 11, of which 6 were waited for; matrix products, arithmetic and copies ran while one was open for 0% of the time, Pallas kernels for 6%

profile of v6, /device:TPU:16, one launch (start us, length us, event | category | flops | bytes accessed | tf_op | source)
XLA Modules:
  0.0 53.6 jit_solution(5249526581195301248)
XLA Ops:
  0.6 3.3 %collective-permute-start.3 = (f32[2,128,128]{2,1,0:T(8,128)}, f32[2,128,128]{2,1,0:T(8,128)S(1)}, u32[]{:S(2)}, u32[]{:S(2)}) collective-permute-start(f32[2,128,128]{2,1,0:T(8,128)} %refs_2_.1), channel_id=1, source_target_pairs={{2,4},{6,8},{10,12},{4,2},{8,6},{12,10},{3,5},{7,9},{11,13},{5,3},... | collective-permute-start | bytes 393224 | tf_op jit(solution)/shard_map/ppermute | solution.py:384
  3.9 1.7 %collective-permute-start.1 = (f32[2,128,128]{2,1,0:T(8,128)}, f32[2,128,128]{2,1,0:T(8,128)S(1)}, u32[]{:S(2)}, u32[]{:S(2)}) collective-permute-start(f32[2,128,128]{2,1,0:T(8,128)} %refs_2_.1), channel_id=1, source_target_pairs={{0,2},{2,0},{4,6},{6,4},{8,10},{10,8},{12,14},{14,12},{1,3},{3,1},... | collective-permute-start | bytes 393224 | tf_op jit(solution)/shard_map/ppermute | solution.py:383
  5.7 0.0 collective-permute-start
  5.7 3.3 %collective-permute-done.3.far_ref = f32[2,128,128]{2,1,0:T(8,128)S(1)} collective-permute-done((f32[2,128,128]{2,1,0:T(8,128)}, f32[2,128,128]{2,1,0:T(8,128)S(1)}, u32[]{:S(2)}, u32[]{:S(2)}) %collective-permute-start.3) | collective-permute-done | bytes 131104 | tf_op jit(solution)/shard_map/ppermute | solution.py:384
  9.0 0.0 collective-permute-start.4
  9.0 2.7 %collective-permute-done.1.near_ref = f32[2,128,128]{2,1,0:T(8,128)S(1)} collective-permute-done((f32[2,128,128]{2,1,0:T(8,128)}, f32[2,128,128]{2,1,0:T(8,128)S(1)}, u32[]{:S(2)}, u32[]{:S(2)}) %collective-permute-start.1) | collective-permute-done | bytes 131104 | tf_op jit(solution)/shard_map/ppermute | solution.py:383
  11.7 0.0 collective-permute-start.2
  12.3 1.5 %stage.1 = (f32[4,2,128,128]{3,2,1,0:T(8,128)S(1)}, f32[1,1,2,128,128]{4,3,2,1,0:T(8,128)S(1)}, f32[2,128,128]{2,1,0:T(8,128)S(1)}, bf16[4,256,256]{2,1,0:T(8,12...) custom-call(f32[4,2,128,128]{3,2,1,0:T(8,128)} %refs_0_.1, f32[1,1,2,128,128]{4,3,2,1,0:T(8,128)} %refs_1_.1, ...), custom_call_target="tpu_custom_call" | custom-call | flops 1048576 | bytes 2621472 | tf_op jit(solution)/shard_map/stage/pallas_call | solution.py:58
  13.8 0.0 collective-permute-done.4.far_pair_ref
  13.9 1.9 %first.1 = (f32[2,2,128,128]{3,2,1,0:T(8,128)S(1)}, f32[2,2,128,128]{3,2,1,0:T(8,128)S(1)}, f32[2,2,2,128,128]{4,3,2,1,0:T(8,128)S(1)}, f32[2,2,128,128]{3,2,1,0:T(8,128)S(1)}) custom-call(s32[1,1,2,2]{3,2,1,0:T(2,128)S(1)} %get-tuple-element.18.offsets_ref, s32[1,1]{1,0:T(1,128)S(6)} %copy.8.counts_ref, f32[2,128,128]{2,1,0:T(8,128)S(1)} %get-tuple-element.17.own_ref, ...), custom_call_target="tpu_custom_call" | custom-call | flops 1207959552 | bytes 2621440 | tf_op jit(solution)/shard_map/first/pallas_call | solution.py:270
  15.7 0.6 %collective-permute-start.8 = (f32[2,2,128,128]{3,2,1,0:T(8,128)S(1)}, f32[2,2,128,128]{3,2,1,0:T(8,128)S(1)}, u32[]{:S(2)}, u32[]{:S(2)}) collective-permute-start(f32[2,2,128,128]{3,2,1,0:T(8,128)S(1)} %get-tuple-element.31), channel_id=1, source_target_pairs={{0,1},{1,0},{2,3},{3,2},{4,5},{5,4},{6,7},{7,6},{8,9},{9,8},{10,11... | collective-permute-start | bytes 786440 | tf_op jit(solution)/shard_map/ppermute | solution.py:395
  16.3 0.9 %second.1 = (f32[2,2,128,128]{3,2,1,0:T(8,128)S(1)}, f32[2,2,384,128]{3,2,1,0:T(8,128)S(1)}) custom-call(s32[1,1,2,2]{3,2,1,0:T(2,128)S(1)} %get-tuple-element.18.offsets_ref, f32[4,2,128,128]{3,2,1,0:T(8,128)S(1)} %get-tuple-element.19.probe_ref, bf16[4,256,256]{2,1,0:T(8,128)(2,1)S(1)} %get-tuple-element.20.tables_ref, ...), custom_call_target="tpu_custom_call" | custom-call | flops 402653184 | bytes 1966080 | tf_op jit(solution)/shard_map/second/pallas_call | solution.py:297
  17.2 0.2 collective-permute-done.8
  17.5 11.4 %all_to_all.10.parts_ref = f32[8,64,128]{2,1,0:T(8,128)S(1)} all-to-all(f32[8,64,128]{2,1,0:T(8,128)S(1)} %bitcast.6), channel_id=1, replica_groups={{10,8,2,0,14,12,6,4},{11,9,3,1,15,13,7,5},{26,24,18,16,30,28,22,20},{27..., dimensions={0} | all-to-all | bytes 524288 | tf_op jit(solution)/shard_map/all_to_all | solution.py:401
  28.9 0.7 %shard_map.79 = f32[8,64,128]{2,1,0:T(8,128)} custom-call(f32[8,64,128]{2,1,0:T(8,128)S(1)} %all_to_all.10.parts_ref), custom_call_target="tpu_custom_call" | custom-call | flops 131072 | bytes 524288 | tf_op jit(solution)/shard_map/pallas_call | solution.py:354
  29.7 5.5 %all-to-all-start.1 = ((f32[8,64,128]{2,1,0:T(8,128)}), f32[8,64,128]{2,1,0:T(8,128)S(1)}, u32[]{:S(2)}, u32[]{:S(2)}) async-start(f32[8,64,128]{2,1,0:T(8,128)} %shard_map.79), calls=%async_computation.1 | async-start | bytes 524288 | tf_op jit(solution)/shard_map/all_to_all | solution.py:409
  35.2 0.1 collective-permute-start.5
  35.2 6.1 %all-to-all-done.1 = f32[8,64,128]{2,1,0:T(8,128)S(1)} async-done(((f32[8,64,128]{2,1,0:T(8,128)}), f32[8,64,128]{2,1,0:T(8,128)S(1)}, u32[]{:S(2)}, u32[]{:S(2)}) %all-to-all-start.1) | async-done | bytes 262176 | tf_op jit(solution)/shard_map/all_to_all | solution.py:409
  41.4 2.2 %collective-permute-start.6 = (f32[2,128,128]{2,1,0:T(8,128)S(1)}, f32[2,128,128]{2,1,0:T(8,128)S(1)}, u32[]{:S(2)}, u32[]{:S(2)}) collective-permute-start(f32[2,128,128]{2,1,0:T(8,128)S(1)} %get-tuple-element.27), channel_id=1, source_target_pairs={{0,2},{2,0},{4,6},{6,4},{8,10},{10,8},{12,14},{14,12},{1,3},{3,1},... | collective-permute-start | bytes 393224 | tf_op jit(solution)/shard_map/ppermute | solution.py:407
  43.6 2.0 %collective-permute-start.7 = (f32[2,128,128]{2,1,0:T(8,128)S(1)}, f32[2,128,128]{2,1,0:T(8,128)S(1)}, u32[]{:S(2)}, u32[]{:S(2)}) collective-permute-start(f32[2,128,128]{2,1,0:T(8,128)S(1)} %get-tuple-element.28), channel_id=1, source_target_pairs={{2,4},{6,8},{10,12},{4,2},{8,6},{12,10},{3,5},{7,9},{11,13},{5,3},... | collective-permute-start | bytes 393224 | tf_op jit(solution)/shard_map/ppermute | solution.py:408
  45.7 2.1 %collective-permute-done.6.near_ref = f32[2,128,128]{2,1,0:T(8,128)S(1)} collective-permute-done((f32[2,128,128]{2,1,0:T(8,128)S(1)}, f32[2,128,128]{2,1,0:T(8,128)S(1)}, u32[]{:S(2)}, u32[]{:S(2)}) %collective-permute-start.6) | collective-permute-done | bytes 131104 | tf_op jit(solution)/shard_map/ppermute | solution.py:407
  47.8 4.2 %collective-permute-done.7.far_ref = f32[2,128,128]{2,1,0:T(8,128)S(1)} collective-permute-done((f32[2,128,128]{2,1,0:T(8,128)S(1)}, f32[2,128,128]{2,1,0:T(8,128)S(1)}, u32[]{:S(2)}, u32[]{:S(2)}) %collective-permute-start.7) | collective-permute-done | bytes 131104 | tf_op jit(solution)/shard_map/ppermute | solution.py:408
  52.0 0.7 %shard_map.78 = f32[2,128,128]{2,1,0:T(8,128)} custom-call(f32[2,128,128]{2,1,0:T(8,128)S(1)} %get-tuple-element.17.own_ref, f32[2,128,128]{2,1,0:T(8,128)S(1)} %get-tuple-element.26.middle_ref, f32[2,128,128]{2,1,0:T(8,128)S(1)} %collective-permute-done.6.near_ref, f32[2,128,128]{2,1,0:T(8,128)S(1)} %collective-permute-done.7.far_ref, ...), custom_call_target="tpu_custom_call" | custom-call | flops 164864 | bytes 659456 | tf_op jit(solution)/shard_map/pallas_call | solution.py:354
  52.7 0.8 %shard_map.80 = f32[4,2,128,128]{3,2,1,0:T(8,128)} custom-call(f32[4,2,128,128]{3,2,1,0:T(8,128)S(1)} %get-tuple-element.19.probe_ref, f32[2,2,128,128]{3,2,1,0:T(8,128)S(1)} %bitcast.5, f32[2,2,128,128]{3,2,1,0:T(8,128)S(1)} %collective-permute-done.9.other_ref), custom_call_target="tpu_custom_call" | custom-call | flops 393216 | bytes 1572864 | tf_op jit(solution)/shard_map/pallas_call | solution.py:354
  (8 shorter events, 0.1 us)
Async XLA Ops:
  0.6 8.3 %collective-permute-start.3 = (f32[2,128,128]{2,1,0:T(8,128)}, f32[2,128,128]{2,1,0:T(8,128)S(1)}, u32[]{:S(2)}, u32[]{:S(2)}) collective-permute-start(f32[2,128,128]{2,1,0:T(8,128)} %refs_2_.1), channel_id=1, source_target_pairs={{2,4},{6,8},{10,12},{4,2},{8,6},{12,10},{3,5},{7,9},{11,13},{5,3},... | collective-permute-start | bytes 393224 | tf_op jit(solution)/shard_map/ppermute | solution.py:384
  3.9 7.8 %collective-permute-start.1 = (f32[2,128,128]{2,1,0:T(8,128)}, f32[2,128,128]{2,1,0:T(8,128)S(1)}, u32[]{:S(2)}, u32[]{:S(2)}) collective-permute-start(f32[2,128,128]{2,1,0:T(8,128)} %refs_2_.1), channel_id=1, source_target_pairs={{0,2},{2,0},{4,6},{6,4},{8,10},{10,8},{12,14},{14,12},{1,3},{3,1},... | collective-permute-start | bytes 393224 | tf_op jit(solution)/shard_map/ppermute | solution.py:383
  5.7 8.2 %collective-permute-start = (f32[2,128,128]{2,1,0:T(8,128)}, f32[2,128,128]{2,1,0:T(8,128)S(1)}, u32[]{:S(2)}, u32[]{:S(2)}) collective-permute-start(f32[2,128,128]{2,1,0:T(8,128)} %refs_2_.1), channel_id=1, source_target_pairs={{0,1},{1,0},{2,3},{3,2},{4,5},{5,4},{6,7},{7,6},{8,9},{9,8},{10,11... | collective-permute-start | bytes 393224 | tf_op jit(solution)/shard_map/ppermute | solution.py:385
  9.0 4.9 %collective-permute-start.4 = (f32[2,128,128]{2,1,0:T(8,128)S(1)}, f32[2,128,128]{2,1,0:T(8,128)S(1)}, u32[]{:S(2)}, u32[]{:S(2)}) collective-permute-start(f32[2,128,128]{2,1,0:T(8,128)S(1)} %collective-permute-done.3.far_ref), channel_id=1, source_target_pairs={{0,1},{1,0},{2,3},{3,2},{4,5},{5,4},{6,7},{7,6},{8,9},{9,8},{10,11... | collective-permute-start | bytes 393224 | tf_op jit(solution)/shard_map/ppermute | solution.py:387
  11.7 2.2 %collective-permute-start.2 = (f32[2,128,128]{2,1,0:T(8,128)S(1)}, f32[2,128,128]{2,1,0:T(8,128)S(1)}, u32[]{:S(2)}, u32[]{:S(2)}) collective-permute-start(f32[2,128,128]{2,1,0:T(8,128)S(1)} %collective-permute-done.1.near_ref), channel_id=1, source_target_pairs={{0,1},{1,0},{2,3},{3,2},{4,5},{5,4},{6,7},{7,6},{8,9},{9,8},{10,11... | collective-permute-start | bytes 393224 | tf_op jit(solution)/shard_map/ppermute | solution.py:386
  15.7 1.7 %collective-permute-start.8 = (f32[2,2,128,128]{3,2,1,0:T(8,128)S(1)}, f32[2,2,128,128]{3,2,1,0:T(8,128)S(1)}, u32[]{:S(2)}, u32[]{:S(2)}) collective-permute-start(f32[2,2,128,128]{3,2,1,0:T(8,128)S(1)} %get-tuple-element.31), channel_id=1, source_target_pairs={{0,1},{1,0},{2,3},{3,2},{4,5},{5,4},{6,7},{7,6},{8,9},{9,8},{10,11... | collective-permute-start | bytes 786440 | tf_op jit(solution)/shard_map/ppermute | solution.py:395
  29.7 11.7 %all-to-all-start.1 = ((f32[8,64,128]{2,1,0:T(8,128)}), f32[8,64,128]{2,1,0:T(8,128)S(1)}, u32[]{:S(2)}, u32[]{:S(2)}) async-start(f32[8,64,128]{2,1,0:T(8,128)} %shard_map.79), calls=%async_computation.1 | async-start | bytes 524288 | tf_op jit(solution)/shard_map/all_to_all | solution.py:409
  35.2 6.2 %collective-permute-start.5 = (f32[2,384,128]{2,1,0:T(8,128)S(1)}, f32[2,384,128]{2,1,0:T(8,128)S(1)}, u32[]{:S(2)}, u32[]{:S(2)}) collective-permute-start(f32[2,384,128]{2,1,0:T(8,128)S(1)} %slice_bitcast_fusion), channel_id=1, source_target_pairs={{0,1},{1,0},{2,3},{3,2},{4,5},{5,4},{6,7},{7,6},{8,9},{9,8},{10,11... | collective-permute-start | bytes 1179656 | tf_op jit(solution)/shard_map/ppermute | solution.py:397
  41.4 11.4 %collective-permute-start.9 = (f32[2,2,128,128]{3,2,1,0:T(8,128)S(1)}, f32[2,2,128,128]{3,2,1,0:T(8,128)S(1)}, u32[]{:S(2)}, u32[]{:S(2)}) collective-permute-start(f32[2,2,128,128]{3,2,1,0:T(8,128)S(1)} %bitcast.4), channel_id=1, source_target_pairs={{0,1},{1,0},{2,3},{3,2},{4,5},{5,4},{6,7},{7,6},{8,9},{9,8},{10,11... | collective-permute-start | bytes 786440 | tf_op jit(solution)/shard_map/ppermute | solution.py:411
  41.4 6.4 %collective-permute-start.6 = (f32[2,128,128]{2,1,0:T(8,128)S(1)}, f32[2,128,128]{2,1,0:T(8,128)S(1)}, u32[]{:S(2)}, u32[]{:S(2)}) collective-permute-start(f32[2,128,128]{2,1,0:T(8,128)S(1)} %get-tuple-element.27), channel_id=1, source_target_pairs={{0,2},{2,0},{4,6},{6,4},{8,10},{10,8},{12,14},{14,12},{1,3},{3,1},... | collective-permute-start | bytes 393224 | tf_op jit(solution)/shard_map/ppermute | solution.py:407
  43.6 8.4 %collective-permute-start.7 = (f32[2,128,128]{2,1,0:T(8,128)S(1)}, f32[2,128,128]{2,1,0:T(8,128)S(1)}, u32[]{:S(2)}, u32[]{:S(2)}) collective-permute-start(f32[2,128,128]{2,1,0:T(8,128)S(1)} %get-tuple-element.28), channel_id=1, source_target_pairs={{2,4},{6,8},{10,12},{4,2},{8,6},{12,10},{3,5},{7,9},{11,13},{5,3},... | collective-permute-start | bytes 393224 | tf_op jit(solution)/shard_map/ppermute | solution.py:408

commit v7 on v6

--- a/solution.py
+++ b/solution.py
@@ -199,8 +199,8 @@
         for k in range(half):
             for part in range(2):
                 kept_ref[slot, k, part] = misfit * far[half + k][part]
-        back = [(misfit * re, misfit * im) for re, im in far[:half]]
-        backs.append(in_groups(back, 2, tables_ref, 1, True))
+        backs.append([(misfit * re, misfit * im) for re, im in far[:half]])
+    backs = [in_groups(back, 2, tables_ref, 1, True) for back in backs]
     backs = [in_groups(back, 2, tables_ref, 1, False) for back in backs]
     grads = combine(backs, probe_ref, order[:half], windows, send_probe_ref)
     for slot in range(slots):
@@ -339,12 +339,39 @@
     out_ref[...] = out.reshape(own_ref.shape)
 
 
-def probe_kernel(tile_total, probe_ref, mine_ref, other_ref, out_ref):
-    half = mine_ref.shape[0]
+def probe_kernel(tile_total, is_mine, probe_ref, part_ref, *refs):
+    out_ref, staged, sems = refs[-3:]
+    half = part_ref.shape[0]
     core = lax.axis_index("col")
-    for part_ref, which in ((mine_ref, core), (other_ref, 1 - core)):
-        modes = pl.ds(which * half, half)
-        out_ref[modes] = probe_ref[modes] - probe_rate * part_ref[...] / tile_total
+    first = half * (core if is_mine else 1 - core)
+    copies = []
+    for k in range(half):
+        staged[k] = probe_ref[first + k] - probe_rate * part_ref[k] / tile_total
+        copies.append(pltpu.make_async_copy(staged.at[k], out_ref.at[first + k], sems.at[k]))
+        copies[-1].start()
+    for copy in copies:
+        copy.wait()
+
+
+def put_half(tile_total, is_mine, probe, part, *buffer):
+    half = part.shape[0]
+    vmem, hbm = (pl.BlockSpec(memory_space=space) for space in (pltpu.VMEM, pltpu.HBM))
+    return pl.pallas_call(
+        functools.partial(probe_kernel, tile_total, is_mine),
+        out_shape=jax.ShapeDtypeStruct(probe.shape, probe.dtype),
+        in_specs=[vmem, vmem] + [hbm] * len(buffer),
+        out_specs=hbm,
+        scratch_shapes=[
+            pltpu.VMEM(part.shape, part.dtype),
+            pltpu.SemaphoreType.DMA((half,)),
+        ],
+        input_output_aliases={2: 0} if buffer else {},
+        cost_estimate=pl.CostEstimate(
+            flops=3 * part.size, bytes_accessed=12 * part.size, transcendentals=0
+        ),
+        compiler_params=pltpu.CompilerParams(vmem_limit_bytes=8 << 20),
+        name="put_mine" if is_mine else "put_other",
+    )(probe, part, *buffer)
 
 
 def in_vmem(kernel, shapes, *operands):
@@ -409,12 +436,11 @@
     mine = lax.all_to_all(mine, "row", 0, 0, tiled=True, axis_index_groups=members)
     mine = mine.reshape(half, 2, width, width)
     other = lax.ppermute(mine, "col", pair)
+    half_done = put_half(tile_total, True, probe_here, mine)
     object_field = in_vmem(
         object_kernel, [block], own, middle, near_strip, far_strip, weight
     )
-    probe = in_vmem(
-        functools.partial(probe_kernel, tile_total), [probe.shape], probe_here, mine, other
-    )
+    probe = put_half(tile_total, False, probe_here, other, half_done)
     return (object_field, probe)
 
 

time: 53.9 us -> 54.5 us (1.011)
  Pallas kernels: 6.61 us -> 7.24 us
    pallas_call x0 -> x2, Pallas kernels: none -> 1.47 us  [put_half(): pl.pallas_call(functools.partial(probe_kernel, tile_total, is_mine), out_...]
    pallas_call x4 -> x3, Pallas kernels: 2.32 us -> 1.47 us  [in_vmem(): pl.pallas_call(kernel, out_shape=out if len(out) > 1 else out[0], in_spec...]
  transfers between devices with their start and end apart: 11 -> 11, of which waited for: 6 -> 6; matrix products, arithmetic and copies ran while one was open for 0% -> 0% of each run, Pallas kernels for 6% -> 7%
where the time goes in v7:
time: 54.5 us; the launch traced here: 54.2 us
  waiting for transfers between devices  18.7 us (34%)
  starting transfers between devices  15.4 us (28%)
  blocking collectives  11.4 us (21%)
  Pallas kernels  7.24 us (13%)
  between operations  1.39 us (3%)
    all_to_all x1, blocking collectives, body(): lax.all_to_all(mine, 'row', 0, 0, tiled=True, axis_index_groups=members)  11.4 us
    all_to_all x1, waiting for transfers between devices, body(): lax.all_to_all(mine, 'row', 0, 0, tiled=True, axis_index_groups=members)  6.1 us
    all_to_all x1, starting transfers between devices, body(): lax.all_to_all(mine, 'row', 0, 0, tiled=True, axis_index_groups=members)  5.48 us
    ppermute x1, waiting for transfers between devices, body(): far_strip = lax.ppermute(far_strip, 'row', far)  4.24 us
    ppermute x1, waiting for transfers between devices, body(): far_block = lax.ppermute(object_field, 'row', far)  3.31 us
    ppermute x1, starting transfers between devices, body(): far_block = lax.ppermute(object_field, 'row', far)  3.28 us
    ppermute x1, waiting for transfers between devices, body(): near_block = lax.ppermute(object_field, 'row', near)  2.71 us
    ppermute x1, starting transfers between devices, body(): near_strip = lax.ppermute(near_strip, 'row', near)  2.23 us
  transfers between devices with their start and end apart: 11, of which 6 were waited for; matrix products, arithmetic and copies ran while one was open for 0% of the time, Pallas kernels for 7%

profile of v7, /device:TPU:16, one launch (start us, length us, event | category | flops | bytes accessed | tf_op | source)
XLA Modules:
  0.0 54.2 jit_solution(13115263554684282479)
XLA Ops:
  0.6 3.3 %collective-permute-start.3 = (f32[2,128,128]{2,1,0:T(8,128)}, f32[2,128,128]{2,1,0:T(8,128)S(1)}, u32[]{:S(2)}, u32[]{:S(2)}) collective-permute-start(f32[2,128,128]{2,1,0:T(8,128)} %refs_2_.1), channel_id=1, source_target_pairs={{2,4},{6,8},{10,12},{4,2},{8,6},{12,10},{3,5},{7,9},{11,13},{5,3},... | collective-permute-start | bytes 393224 | tf_op jit(solution)/shard_map/ppermute | solution.py:411
  3.9 1.7 %collective-permute-start.1 = (f32[2,128,128]{2,1,0:T(8,128)}, f32[2,128,128]{2,1,0:T(8,128)S(1)}, u32[]{:S(2)}, u32[]{:S(2)}) collective-permute-start(f32[2,128,128]{2,1,0:T(8,128)} %refs_2_.1), channel_id=1, source_target_pairs={{0,2},{2,0},{4,6},{6,4},{8,10},{10,8},{12,14},{14,12},{1,3},{3,1},... | collective-permute-start | bytes 393224 | tf_op jit(solution)/shard_map/ppermute | solution.py:410
  5.7 0.0 collective-permute-start
  5.7 3.3 %collective-permute-done.3.far_ref = f32[2,128,128]{2,1,0:T(8,128)S(1)} collective-permute-done((f32[2,128,128]{2,1,0:T(8,128)}, f32[2,128,128]{2,1,0:T(8,128)S(1)}, u32[]{:S(2)}, u32[]{:S(2)}) %collective-permute-start.3) | collective-permute-done | bytes 131104 | tf_op jit(solution)/shard_map/ppermute | solution.py:411
  9.0 0.0 collective-permute-start.4
  9.0 2.7 %collective-permute-done.1.near_ref = f32[2,128,128]{2,1,0:T(8,128)S(1)} collective-permute-done((f32[2,128,128]{2,1,0:T(8,128)}, f32[2,128,128]{2,1,0:T(8,128)S(1)}, u32[]{:S(2)}, u32[]{:S(2)}) %collective-permute-start.1) | collective-permute-done | bytes 131104 | tf_op jit(solution)/shard_map/ppermute | solution.py:410
  11.7 0.0 collective-permute-start.2
  12.3 1.5 %stage.1 = (f32[4,2,128,128]{3,2,1,0:T(8,128)S(1)}, f32[1,1,2,128,128]{4,3,2,1,0:T(8,128)S(1)}, f32[2,128,128]{2,1,0:T(8,128)S(1)}, bf16[4,256,256]{2,1,0:T(8,12...) custom-call(f32[4,2,128,128]{3,2,1,0:T(8,128)} %refs_0_.1, f32[1,1,2,128,128]{4,3,2,1,0:T(8,128)} %refs_1_.1, ...), custom_call_target="tpu_custom_call" | custom-call | flops 1048576 | bytes 2621472 | tf_op jit(solution)/shard_map/stage/pallas_call | solution.py:58
  13.9 1.9 %first.1 = (f32[2,2,128,128]{3,2,1,0:T(8,128)S(1)}, f32[2,2,128,128]{3,2,1,0:T(8,128)S(1)}, f32[2,2,2,128,128]{4,3,2,1,0:T(8,128)S(1)}, f32[2,2,128,128]{3,2,1,0:T(8,128)S(1)}) custom-call(s32[1,1,2,2]{3,2,1,0:T(2,128)S(1)} %get-tuple-element.18.offsets_ref, s32[1,1]{1,0:T(1,128)S(6)} %copy.10.counts_ref, f32[2,128,128]{2,1,0:T(8,128)S(1)} %get-tuple-element.17.own_ref, ...), custom_call_target="tpu_custom_call" | custom-call | flops 1207959552 | bytes 2621440 | tf_op jit(solution)/shard_map/first/pallas_call | solution.py:270
  15.7 0.6 %collective-permute-start.8 = (f32[2,2,128,128]{3,2,1,0:T(8,128)S(1)}, f32[2,2,128,128]{3,2,1,0:T(8,128)S(1)}, u32[]{:S(2)}, u32[]{:S(2)}) collective-permute-start(f32[2,2,128,128]{3,2,1,0:T(8,128)S(1)} %get-tuple-element.31), channel_id=1, source_target_pairs={{0,1},{1,0},{2,3},{3,2},{4,5},{5,4},{6,7},{7,6},{8,9},{9,8},{10,11... | collective-permute-start | bytes 786440 | tf_op jit(solution)/shard_map/ppermute | solution.py:422
  16.3 1.0 %second.1 = (f32[2,2,128,128]{3,2,1,0:T(8,128)S(1)}, f32[2,2,384,128]{3,2,1,0:T(8,128)S(1)}) custom-call(s32[1,1,2,2]{3,2,1,0:T(2,128)S(1)} %get-tuple-element.18.offsets_ref, f32[4,2,128,128]{3,2,1,0:T(8,128)S(1)} %get-tuple-element.19.probe_ref, bf16[4,256,256]{2,1,0:T(8,128)(2,1)S(1)} %get-tuple-element.20.tables_ref, ...), custom_call_target="tpu_custom_call" | custom-call | flops 402653184 | bytes 1966080 | tf_op jit(solution)/shard_map/second/pallas_call | solution.py:297
  17.3 0.2 collective-permute-done.8
  17.5 11.4 %all_to_all.10.parts_ref = f32[8,64,128]{2,1,0:T(8,128)S(1)} all-to-all(f32[8,64,128]{2,1,0:T(8,128)S(1)} %bitcast.6), channel_id=1, replica_groups={{10,8,2,0,14,12,6,4},{11,9,3,1,15,13,7,5},{26,24,18,16,30,28,22,20},{27..., dimensions={0} | all-to-all | bytes 524288 | tf_op jit(solution)/shard_map/all_to_all | solution.py:428
  28.9 0.7 %shard_map.79 = f32[8,64,128]{2,1,0:T(8,128)} custom-call(f32[8,64,128]{2,1,0:T(8,128)S(1)} %all_to_all.10.parts_ref), custom_call_target="tpu_custom_call" | custom-call | flops 131072 | bytes 524288 | tf_op jit(solution)/shard_map/pallas_call | solution.py:381
  29.7 5.5 %all-to-all-start.1 = ((f32[8,64,128]{2,1,0:T(8,128)}), f32[8,64,128]{2,1,0:T(8,128)S(1)}, u32[]{:S(2)}, u32[]{:S(2)}) async-start(f32[8,64,128]{2,1,0:T(8,128)} %shard_map.79), calls=%async_computation.1 | async-start | bytes 524288 | tf_op jit(solution)/shard_map/all_to_all | solution.py:436
  35.2 0.1 collective-permute-start.5
  35.3 6.1 %all-to-all-done.1 = f32[8,64,128]{2,1,0:T(8,128)S(1)} async-done(((f32[8,64,128]{2,1,0:T(8,128)}), f32[8,64,128]{2,1,0:T(8,128)S(1)}, u32[]{:S(2)}, u32[]{:S(2)}) %all-to-all-start.1) | async-done | bytes 262176 | tf_op jit(solution)/shard_map/all_to_all | solution.py:436
  41.4 2.2 %collective-permute-start.6 = (f32[2,128,128]{2,1,0:T(8,128)S(1)}, f32[2,128,128]{2,1,0:T(8,128)S(1)}, u32[]{:S(2)}, u32[]{:S(2)}) collective-permute-start(f32[2,128,128]{2,1,0:T(8,128)S(1)} %get-tuple-element.27), channel_id=1, source_target_pairs={{0,2},{2,0},{4,6},{6,4},{8,10},{10,8},{12,14},{14,12},{1,3},{3,1},... | collective-permute-start | bytes 393224 | tf_op jit(solution)/shard_map/ppermute | solution.py:434
  43.6 2.0 %collective-permute-start.7 = (f32[2,128,128]{2,1,0:T(8,128)S(1)}, f32[2,128,128]{2,1,0:T(8,128)S(1)}, u32[]{:S(2)}, u32[]{:S(2)}) collective-permute-start(f32[2,128,128]{2,1,0:T(8,128)S(1)} %get-tuple-element.28), channel_id=1, source_target_pairs={{2,4},{6,8},{10,12},{4,2},{8,6},{12,10},{3,5},{7,9},{11,13},{5,3},... | collective-permute-start | bytes 393224 | tf_op jit(solution)/shard_map/ppermute | solution.py:435
  45.7 2.1 %collective-permute-done.6.near_ref = f32[2,128,128]{2,1,0:T(8,128)S(1)} collective-permute-done((f32[2,128,128]{2,1,0:T(8,128)S(1)}, f32[2,128,128]{2,1,0:T(8,128)S(1)}, u32[]{:S(2)}, u32[]{:S(2)}) %collective-permute-start.6) | collective-permute-done | bytes 131104 | tf_op jit(solution)/shard_map/ppermute | solution.py:434
  47.8 4.2 %collective-permute-done.7.far_ref = f32[2,128,128]{2,1,0:T(8,128)S(1)} collective-permute-done((f32[2,128,128]{2,1,0:T(8,128)S(1)}, f32[2,128,128]{2,1,0:T(8,128)S(1)}, u32[]{:S(2)}, u32[]{:S(2)}) %collective-permute-start.7) | collective-permute-done | bytes 131104 | tf_op jit(solution)/shard_map/ppermute | solution.py:435
  52.0 0.7 %shard_map.78 = f32[2,128,128]{2,1,0:T(8,128)} custom-call(f32[2,128,128]{2,1,0:T(8,128)S(1)} %get-tuple-element.17.own_ref, f32[2,128,128]{2,1,0:T(8,128)S(1)} %get-tuple-element.26.middle_ref, f32[2,128,128]{2,1,0:T(8,128)S(1)} %collective-permute-done.6.near_ref, f32[2,128,128]{2,1,0:T(8,128)S(1)} %collective-permute-done.7.far_ref, ...), custom_call_target="tpu_custom_call" | custom-call | flops 164864 | bytes 659456 | tf_op jit(solution)/shard_map/pallas_call | solution.py:381
  52.7 0.7 %put_mine.1.refs_0_ = f32[4,2,128,128]{3,2,1,0:T(8,128)} custom-call(f32[4,2,128,128]{3,2,1,0:T(8,128)S(1)} %get-tuple-element.19.probe_ref, f32[2,2,128,128]{3,2,1,0:T(8,128)S(1)} %bitcast.5), custom_call_target="tpu_custom_call" | custom-call | flops 196608 | bytes 786432 | tf_op jit(solution)/shard_map/put_mine/pallas_call | solution.py:359
  53.5 0.7 %put_other.1 = f32[4,2,128,128]{3,2,1,0:T(8,128)} custom-call(f32[4,2,128,128]{3,2,1,0:T(8,128)S(1)} %get-tuple-element.19.probe_ref, f32[2,2,128,128]{3,2,1,0:T(8,128)S(1)} %collective-permute-done.9.part_ref, f32[4,2,128,128]{3,2,1,0:T(8,128)} %put_mine.1.refs_0_), custom_call_target="tpu_custom_call", output_to_operand_aliasing={{}: (2, {})} | custom-call | flops 196608 | bytes 786432 | tf_op jit(solution)/shard_map/put_other/pallas_call | solution.py:359
  (9 shorter events, 0.1 us)
Async XLA Ops:
  0.6 8.3 %collective-permute-start.3 = (f32[2,128,128]{2,1,0:T(8,128)}, f32[2,128,128]{2,1,0:T(8,128)S(1)}, u32[]{:S(2)}, u32[]{:S(2)}) collective-permute-start(f32[2,128,128]{2,1,0:T(8,128)} %refs_2_.1), channel_id=1, source_target_pairs={{2,4},{6,8},{10,12},{4,2},{8,6},{12,10},{3,5},{7,9},{11,13},{5,3},... | collective-permute-start | bytes 393224 | tf_op jit(solution)/shard_map/ppermute | solution.py:411
  3.9 7.8 %collective-permute-start.1 = (f32[2,128,128]{2,1,0:T(8,128)}, f32[2,128,128]{2,1,0:T(8,128)S(1)}, u32[]{:S(2)}, u32[]{:S(2)}) collective-permute-start(f32[2,128,128]{2,1,0:T(8,128)} %refs_2_.1), channel_id=1, source_target_pairs={{0,2},{2,0},{4,6},{6,4},{8,10},{10,8},{12,14},{14,12},{1,3},{3,1},... | collective-permute-start | bytes 393224 | tf_op jit(solution)/shard_map/ppermute | solution.py:410
  5.7 8.2 %collective-permute-start = (f32[2,128,128]{2,1,0:T(8,128)}, f32[2,128,128]{2,1,0:T(8,128)S(1)}, u32[]{:S(2)}, u32[]{:S(2)}) collective-permute-start(f32[2,128,128]{2,1,0:T(8,128)} %refs_2_.1), channel_id=1, source_target_pairs={{0,1},{1,0},{2,3},{3,2},{4,5},{5,4},{6,7},{7,6},{8,9},{9,8},{10,11... | collective-permute-start | bytes 393224 | tf_op jit(solution)/shard_map/ppermute | solution.py:412
  9.0 4.9 %collective-permute-start.4 = (f32[2,128,128]{2,1,0:T(8,128)S(1)}, f32[2,128,128]{2,1,0:T(8,128)S(1)}, u32[]{:S(2)}, u32[]{:S(2)}) collective-permute-start(f32[2,128,128]{2,1,0:T(8,128)S(1)} %collective-permute-done.3.far_ref), channel_id=1, source_target_pairs={{0,1},{1,0},{2,3},{3,2},{4,5},{5,4},{6,7},{7,6},{8,9},{9,8},{10,11... | collective-permute-start | bytes 393224 | tf_op jit(solution)/shard_map/ppermute | solution.py:414
  11.7 2.2 %collective-permute-start.2 = (f32[2,128,128]{2,1,0:T(8,128)S(1)}, f32[2,128,128]{2,1,0:T(8,128)S(1)}, u32[]{:S(2)}, u32[]{:S(2)}) collective-permute-start(f32[2,128,128]{2,1,0:T(8,128)S(1)} %collective-permute-done.1.near_ref), channel_id=1, source_target_pairs={{0,1},{1,0},{2,3},{3,2},{4,5},{5,4},{6,7},{7,6},{8,9},{9,8},{10,11... | collective-permute-start | bytes 393224 | tf_op jit(solution)/shard_map/ppermute | solution.py:413
  15.7 1.7 %collective-permute-start.8 = (f32[2,2,128,128]{3,2,1,0:T(8,128)S(1)}, f32[2,2,128,128]{3,2,1,0:T(8,128)S(1)}, u32[]{:S(2)}, u32[]{:S(2)}) collective-permute-start(f32[2,2,128,128]{3,2,1,0:T(8,128)S(1)} %get-tuple-element.31), channel_id=1, source_target_pairs={{0,1},{1,0},{2,3},{3,2},{4,5},{5,4},{6,7},{7,6},{8,9},{9,8},{10,11... | collective-permute-start | bytes 786440 | tf_op jit(solution)/shard_map/ppermute | solution.py:422
  29.7 11.7 %all-to-all-start.1 = ((f32[8,64,128]{2,1,0:T(8,128)}), f32[8,64,128]{2,1,0:T(8,128)S(1)}, u32[]{:S(2)}, u32[]{:S(2)}) async-start(f32[8,64,128]{2,1,0:T(8,128)} %shard_map.79), calls=%async_computation.1 | async-start | bytes 524288 | tf_op jit(solution)/shard_map/all_to_all | solution.py:436
  35.2 6.2 %collective-permute-start.5 = (f32[2,384,128]{2,1,0:T(8,128)S(1)}, f32[2,384,128]{2,1,0:T(8,128)S(1)}, u32[]{:S(2)}, u32[]{:S(2)}) collective-permute-start(f32[2,384,128]{2,1,0:T(8,128)S(1)} %slice_bitcast_fusion), channel_id=1, source_target_pairs={{0,1},{1,0},{2,3},{3,2},{4,5},{5,4},{6,7},{7,6},{8,9},{9,8},{10,11... | collective-permute-start | bytes 1179656 | tf_op jit(solution)/shard_map/ppermute | solution.py:424
  41.4 12.1 %collective-permute-start.9 = (f32[2,2,128,128]{3,2,1,0:T(8,128)S(1)}, f32[2,2,128,128]{3,2,1,0:T(8,128)S(1)}, u32[]{:S(2)}, u32[]{:S(2)}) collective-permute-start(f32[2,2,128,128]{3,2,1,0:T(8,128)S(1)} %bitcast.4), channel_id=1, source_target_pairs={{0,1},{1,0},{2,3},{3,2},{4,5},{5,4},{6,7},{7,6},{8,9},{9,8},{10,11... | collective-permute-start | bytes 786440 | tf_op jit(solution)/shard_map/ppermute | solution.py:438
  41.4 6.4 %collective-permute-start.6 = (f32[2,128,128]{2,1,0:T(8,128)S(1)}, f32[2,128,128]{2,1,0:T(8,128)S(1)}, u32[]{:S(2)}, u32[]{:S(2)}) collective-permute-start(f32[2,128,128]{2,1,0:T(8,128)S(1)} %get-tuple-element.27), channel_id=1, source_target_pairs={{0,2},{2,0},{4,6},{6,4},{8,10},{10,8},{12,14},{14,12},{1,3},{3,1},... | collective-permute-start | bytes 393224 | tf_op jit(solution)/shard_map/ppermute | solution.py:434
  43.6 8.4 %collective-permute-start.7 = (f32[2,128,128]{2,1,0:T(8,128)S(1)}, f32[2,128,128]{2,1,0:T(8,128)S(1)}, u32[]{:S(2)}, u32[]{:S(2)}) collective-permute-start(f32[2,128,128]{2,1,0:T(8,128)S(1)} %get-tuple-element.28), channel_id=1, source_target_pairs={{2,4},{6,8},{10,12},{4,2},{8,6},{12,10},{3,5},{7,9},{11,13},{5,3},... | collective-permute-start | bytes 393224 | tf_op jit(solution)/shard_map/ppermute | solution.py:435
